TPU v7x, 32 devices: a whole 2x2x4 slice. The times are simulated.
32 devices in a mesh: wide: 16 (over z, y, core), narrow: 2 (over x).
Axes of the slice: x: 2, y: 2, z: 4, core: 2. Of those that a mesh axis runs over, the one named last changes fastest.
Arguments:
- tokens_short: bfloat16 [4096, 2048], P(('wide', 'narrow')), may hold values from -6 to 6
- tokens_long: bfloat16 [16384, 2048], P(('wide', 'narrow')), may hold values from -6 to 6
- cot_short: bfloat16 [4096, 2048], P(('wide', 'narrow')), may hold values from -6 to 6
- cot_long: bfloat16 [16384, 2048], P(('wide', 'narrow')), may hold values from -6 to 6
- seq_lengths: int32 [2, 32], P(None, ('wide', 'narrow')), may hold values from 64 to 512, as said below
- norm_gain: bfloat16 [2048], P(('wide', 'narrow')), may hold values from 0.25 to 1.75
- in_w: bfloat16 [2048, 8448], P(('wide', 'narrow')), may hold values from -0.125 to 0.125
- dt_w: bfloat16 [2048, 64], P(('wide', 'narrow')), may hold values from -0.125 to 0.125
- conv_w: bfloat16 [4, 4352], P(None, ('wide', 'narrow')), may hold values from -3 to 3
- conv_b: bfloat16 [4352], P(('wide', 'narrow')), may hold values from -3 to 3
- dt_bias: bfloat16 [64], replicated, may hold values from -8 to -3.5
- a_log: bfloat16 [64], replicated, may hold values from 0 to 2.796875
- d_skip: bfloat16 [64], replicated, may hold values from 0.5 to 1.5
- gate_gain: bfloat16 [4096], P(('wide', 'narrow')), may hold values from 0.25 to 1.75
- out_w: bfloat16 [4096, 2048], P(('wide', 'narrow')), may hold values from -0.09375 to 0.09375
Outputs:
- out_short: bfloat16 [4096, 2048], P(('wide', 'narrow'))
- out_long: bfloat16 [16384, 2048], P(('wide', 'narrow'))
- grad_short: float32 [4096, 2048], P(('wide', 'narrow'))
- grad_long: float32 [16384, 2048], P(('wide', 'narrow'))
- grad_norm_gain: float32 [2048], P(('wide', 'narrow'))
- grad_in_w: float32 [2048, 8448], P(('wide', 'narrow'))
- grad_dt_w: float32 [2048, 64], P(('wide', 'narrow'))
- grad_conv_w: float32 [4, 4352], P(None, ('wide', 'narrow'))
- grad_conv_b: float32 [4352], P(('wide', 'narrow'))
- grad_dt_bias: float32 [64], replicated
- grad_a_log: float32 [64], replicated
- grad_d_skip: float32 [64], replicated
- grad_gate_gain: float32 [4096], P(('wide', 'narrow'))
- grad_out_w: float32 [4096, 2048], P(('wide', 'narrow'))
Inputs may be any that keep to these rules, and one draw needn't show every extreme that they name: `seq_lengths`: row 0 lies between 64 and 128, row 1 between 256 and 512; in each row some slot is full.
All inputs are finite; a program needn't handle non-finite values.
Results may differ from a plain program's by a relative error of at most 0.0085.
Values may be sent and summed in bfloat16 or wider, within the bound.
No kernel may reach another device: no remote copies, remote signals or barrier semaphores. Data moves between devices by JAX's collectives and lax.ppermute only.
A program may use at most 448 MiB of HBM per device.

v0:
```python
import jax
import jax.numpy as jnp
from jax import lax
from jax.sharding import PartitionSpec as P

DI = 4096
HEADS = 64
HEAD_DIM = 64
STATE = 128
SPAN = 256


EPS = 1e-05
HIGHEST = lax.Precision.HIGHEST


def silu_of(values):
    return values * jax.nn.sigmoid(values)


def silu_slope(values):
    logistic = jax.nn.sigmoid(values)
    return logistic * (1.0 + values * (1.0 - logistic))


def input_norm(tokens):
    residual = tokens.astype(jnp.float32)
    row_scale = lax.rsqrt(jnp.mean(residual * residual, axis=-1, keepdims=True) + EPS)
    return (residual, row_scale, residual * row_scale)


def causal_conv(values, kernel):
    kernel_len = kernel.shape[0]
    seq_len = values.shape[0]
    padded = jnp.concatenate(
        [jnp.zeros((kernel_len - 1, values.shape[1]), jnp.float32), values], axis=0
    )
    return sum((kernel[offset] * padded[offset : offset + seq_len] for offset in range(kernel_len)))


def conv_backward(values, d_conv, kernel):
    kernel_len = kernel.shape[0]
    seq_len = values.shape[0]
    padded = jnp.concatenate(
        [jnp.zeros((kernel_len - 1, values.shape[1]), jnp.float32), values], axis=0
    )
    g_kernel = jnp.stack(
        [
            jnp.sum(d_conv * padded[offset : offset + seq_len], axis=0)
            for offset in range(kernel_len)
        ]
    )
    d_padded = jnp.concatenate(
        [d_conv, jnp.zeros((kernel_len - 1, values.shape[1]), jnp.float32)], axis=0
    )
    d_values = sum(
        (
            kernel[offset] * d_padded[kernel_len - 1 - offset : kernel_len - 1 - offset + seq_len]
            for offset in range(kernel_len)
        )
    )
    return (g_kernel, d_values)


def to_heads(values, blocks, block_len):
    return values.reshape(blocks, block_len, HEADS, HEAD_DIM).transpose(0, 2, 1, 3)


def from_heads(values):
    return values.transpose(0, 2, 1, 3).reshape(-1, values.shape[1] * values.shape[3])


def span_parts(b_block, c_block, dt_block, neg_rate):
    block_len = dt_block.shape[-1]
    places = jnp.arange(block_len)
    upper_ones = (places[:, None] <= places[None, :]).astype(jnp.float32)
    causal = places[:, None] >= places[None, :]
    cumulative = jnp.dot(dt_block * neg_rate[:, None], upper_ones, precision=HIGHEST)
    spread = cumulative[:, :, None] - cumulative[:, None, :]
    decays = jnp.where(causal[None], jnp.exp(jnp.where(causal[None], spread, 0.0)), 0.0)
    scores = jnp.dot(c_block, b_block.T, precision=HIGHEST)
    weights = jnp.exp(cumulative[:, -1:] - cumulative) * dt_block
    return (upper_ones, cumulative, decays, scores, weights)


def span_forward(state_in, inputs, neg_rate):
    x_block, b_block, c_block, dt_block = inputs
    upper_ones, cumulative, decays, scores, weights = span_parts(
        b_block, c_block, dt_block, neg_rate
    )
    mixing = scores[None] * decays * dt_block[:, None, :]
    inside = jnp.einsum("hij,hjp->hip", mixing, x_block, precision=HIGHEST)
    carried = jnp.exp(cumulative)[:, :, None] * jnp.einsum(
        "in,hpn->hip", c_block, state_in, precision=HIGHEST
    )
    state_out = jnp.exp(cumulative[:, -1])[:, None, None] * state_in + jnp.einsum(
        "hjp,jn->hpn", weights[:, :, None] * x_block, b_block, precision=HIGHEST
    )
    return (state_out, inside + carried)


def span_backward(d_state, inputs, neg_rate):
    x_block, b_block, c_block, dt_block, dy_block, state_in = inputs
    upper_ones, cumulative, decays, scores, weights = span_parts(
        b_block, c_block, dt_block, neg_rate
    )
    block_len = dt_block.shape[-1]
    is_last = (jnp.arange(block_len) == block_len - 1).astype(jnp.float32)
    mixing = scores[None] * decays * dt_block[:, None, :]
    exp_cum = jnp.exp(cumulative)
    last_decay = exp_cum[:, -1]
    d_mixing = jnp.einsum("hip,hjp->hij", dy_block, x_block, precision=HIGHEST)
    d_x = jnp.einsum("hij,hip->hjp", mixing, dy_block, precision=HIGHEST)
    carried_in = jnp.einsum("in,hpn->hip", c_block, state_in, precision=HIGHEST)
    d_carried = dy_block * exp_cum[:, :, None]
    d_c = jnp.einsum("hip,hpn->in", d_carried, state_in, precision=HIGHEST)
    d_state_in = (
        jnp.einsum("hip,in->hpn", d_carried, c_block, precision=HIGHEST)
        + last_decay[:, None, None] * d_state
    )
    d_cum = jnp.sum(d_carried * carried_in, axis=-1)
    scaled = d_mixing * decays
    d_scores = jnp.einsum("hij,hj->ij", scaled, dt_block, precision=HIGHEST)
    through = scaled * scores[None]
    d_dt = jnp.sum(through, axis=1)
    k_term = through * dt_block[:, None, :]
    d_cum = d_cum + jnp.sum(k_term, axis=2) - jnp.sum(k_term, axis=1)
    d_c = d_c + jnp.dot(d_scores, b_block, precision=HIGHEST)
    d_b = jnp.dot(d_scores.T, c_block, precision=HIGHEST)
    x_state = jnp.einsum("hjp,hpn->hjn", x_block, d_state, precision=HIGHEST)
    d_weights = jnp.sum(x_state * b_block[None], axis=-1)
    d_b = d_b + jnp.einsum("hj,hjn->jn", weights, x_state, precision=HIGHEST)
    d_x = d_x + weights[:, :, None] * jnp.einsum("jn,hpn->hjp", b_block, d_state, precision=HIGHEST)
    d_dt = d_dt + d_weights * jnp.exp(cumulative[:, -1:] - cumulative)
    w_term = d_weights * weights
    last_term = jnp.sum(w_term, axis=1) + jnp.sum(d_state * state_in, axis=(1, 2)) * last_decay
    d_cum = d_cum - w_term + last_term[:, None] * is_last[None, :]
    d_rate = jnp.dot(d_cum, upper_ones.T, precision=HIGHEST)
    d_dt = d_dt + d_rate * neg_rate[:, None]
    d_neg = jnp.sum(d_rate * dt_block, axis=1)
    return (d_state_in, (d_x, d_b, d_c, d_dt, d_neg))


def ssd_inputs(conv_pre, dt_raw, dt_bias):
    activated = silu_of(conv_pre)
    x_seq = activated[:, :DI].astype(jnp.bfloat16).astype(jnp.float32)
    b_seq = activated[:, DI : DI + STATE].astype(jnp.bfloat16).astype(jnp.float32)
    c_seq = activated[:, DI + STATE :].astype(jnp.bfloat16).astype(jnp.float32)
    soft_in = dt_raw + dt_bias
    seq_len = conv_pre.shape[0]
    block_len = min(SPAN, seq_len)
    blocks = seq_len // block_len
    dt_blocks = jax.nn.softplus(soft_in).reshape(blocks, block_len, HEADS).transpose(0, 2, 1)
    block_inputs = (
        to_heads(x_seq, blocks, block_len),
        b_seq.reshape(blocks, block_len, STATE),
        c_seq.reshape(blocks, block_len, STATE),
        dt_blocks,
    )
    return (x_seq, soft_in, block_inputs)


def forward_pass(micro_group, shards, head_params):
    in_w, dt_w, norm_gain, conv_w, conv_b, gate_gain, out_w = shards
    dt_bias, a_log, d_skip = head_params
    normals = [input_norm(entry[0]) for entry in micro_group]
    kept = None
    pieces = (
        lax.all_gather(in_w, ("wide", "narrow"), axis=0, tiled=True),
        lax.all_gather(dt_w, ("wide", "narrow"), axis=0, tiled=True),
        lax.all_gather(norm_gain, ("wide", "narrow"), axis=0, tiled=True),
    )
    gain_part = pieces[2].astype(jnp.float32)
    updated = []
    for add_position in range(len(normals)):
        part_rows = normals[add_position][2]
        normal_part = (part_rows * gain_part).astype(jnp.bfloat16)
        updated.append(
            (
                jnp.dot(normal_part, pieces[0], preferred_element_type=jnp.float32),
                jnp.dot(normal_part, pieces[1], preferred_element_type=jnp.float32),
            )
        )
    projections = tuple(updated)
    conv_full, bias_full, gate_full, out_full = (
        lax.all_gather(conv_w, ("wide", "narrow"), axis=1, tiled=True),
        lax.all_gather(conv_b, ("wide", "narrow"), axis=0, tiled=True),
        lax.all_gather(gate_gain, ("wide", "narrow"), axis=0, tiled=True),
        lax.all_gather(out_w, ("wide", "narrow"), axis=0, tiled=True),
    )
    kernel = conv_full.astype(jnp.float32)
    neg_rate = -jnp.exp(a_log)
    skip_full = jnp.repeat(d_skip, HEAD_DIM)

    def forward_step(state_in, inputs):
        state_out, y_block = span_forward(state_in, inputs, neg_rate)
        return (state_out, (y_block, state_in))

    outputs = []
    saved = []
    for position in range(len(micro_group)):
        tokens, length = micro_group[position]
        residual, row_scale, unit_rows = normals[position]
        projected, dt_raw = projections[position]
        conv_pre = causal_conv(projected[:, DI:], kernel) + bias_full.astype(jnp.float32)
        x_seq, soft_in, block_inputs = ssd_inputs(conv_pre, dt_raw, dt_bias)
        final_state, (y_blocks, states) = lax.scan(
            forward_step, jnp.zeros((HEADS, HEAD_DIM, STATE), jnp.float32), block_inputs
        )
        y_total = from_heads(y_blocks) + skip_full * x_seq
        gate_z = projected[:, :DI]
        gated_y = y_total * silu_of(gate_z)
        gate_scale = lax.rsqrt(jnp.mean(gated_y * gated_y, axis=-1, keepdims=True) + EPS)
        normed = (gated_y * gate_scale * gate_full.astype(jnp.float32)).astype(jnp.bfloat16)
        branch = jnp.dot(normed, out_full, preferred_element_type=jnp.float32)
        live_rows = (jnp.arange(tokens.shape[0]) < length).astype(jnp.float32)[:, None]
        outputs.append((residual + live_rows * branch).astype(jnp.bfloat16))
        saved.append((projected, dt_raw, conv_pre, states, y_total, normed, live_rows))
    return (outputs, saved, kept)


def backward_pass(micro_group, cotangents, saved, shards, head_params):
    in_w, dt_w, norm_gain, conv_w, conv_b, gate_gain, out_w = shards
    dt_bias, a_log, d_skip = head_params
    in_full, dt_full, norm_full, conv_full, gate_full, out_full = (
        lax.all_gather(in_w, ("wide", "narrow"), axis=0, tiled=True),
        lax.all_gather(dt_w, ("wide", "narrow"), axis=0, tiled=True),
        lax.all_gather(norm_gain, ("wide", "narrow"), axis=0, tiled=True),
        lax.all_gather(conv_w, ("wide", "narrow"), axis=1, tiled=True),
        lax.all_gather(gate_gain, ("wide", "narrow"), axis=0, tiled=True),
        lax.all_gather(out_w, ("wide", "narrow"), axis=0, tiled=True),
    )
    neg_rate = -jnp.exp(a_log)
    skip_full = jnp.repeat(d_skip, HEAD_DIM)
    gate_f32 = gate_full.astype(jnp.float32)
    norm_f32 = norm_full.astype(jnp.float32)
    kernel = conv_full.astype(jnp.float32)

    def backward_step(carried, inputs):
        d_state, d_neg = carried
        d_state_in, block_grads = span_backward(d_state, inputs, neg_rate)
        return ((d_state_in, d_neg + block_grads[4]), block_grads[:4])

    d_inputs = []
    factors = []
    small = None
    heads_sum = None
    for position in range(len(micro_group)):
        tokens, length = micro_group[position]
        projected, dt_raw, conv_pre, states, y_total, normed, live_rows = saved[position]
        residual, row_scale, unit_rows = input_norm(tokens)
        seq_len = tokens.shape[0]
        d_out = cotangents[position].astype(jnp.float32)
        d_branch = (live_rows * d_out).astype(jnp.bfloat16)
        d_normed = jnp.einsum("tj,ij->ti", d_branch, out_full, preferred_element_type=jnp.float32)
        gate_z = projected[:, :DI]
        gate_silu = silu_of(gate_z)
        gated_y = y_total * gate_silu
        gate_scale = lax.rsqrt(jnp.mean(gated_y * gated_y, axis=-1, keepdims=True) + EPS)
        unit_gated = gated_y * gate_scale
        g_gate_gain = jnp.sum(d_normed * unit_gated, axis=0)
        d_unit = d_normed * gate_f32
        d_gated = gate_scale * (
            d_unit - unit_gated * jnp.mean(d_unit * unit_gated, axis=-1, keepdims=True)
        )
        d_y = d_gated * gate_silu
        d_gate_z = d_gated * y_total * silu_slope(gate_z)
        x_seq, soft_in, block_inputs = ssd_inputs(conv_pre, dt_raw, dt_bias)
        blocks = states.shape[0]
        block_len = seq_len // blocks
        dy_blocks = to_heads(d_y, blocks, block_len)
        zero_state = (
            jnp.zeros((HEADS, HEAD_DIM, STATE), jnp.float32),
            jnp.zeros((HEADS,), jnp.float32),
        )
        (first_grad, d_neg), (dx_blocks, db_blocks, dc_blocks, ddt_blocks) = lax.scan(
            backward_step, zero_state, block_inputs + (dy_blocks, states), reverse=True
        )
        g_d_skip = jnp.sum((d_y * x_seq).reshape(seq_len, HEADS, HEAD_DIM), axis=(0, 2))
        d_x_seq = from_heads(dx_blocks) + skip_full * d_y
        d_act = jnp.concatenate(
            [d_x_seq, db_blocks.reshape(seq_len, STATE), dc_blocks.reshape(seq_len, STATE)], axis=-1
        )
        d_conv = d_act * silu_slope(conv_pre)
        g_conv_b = jnp.sum(d_conv, axis=0)
        g_conv_w, d_conv_in = conv_backward(projected[:, DI:], d_conv, kernel)
        d_soft = ddt_blocks.transpose(0, 2, 1).reshape(seq_len, HEADS) * jax.nn.sigmoid(soft_in)
        g_dt_bias = jnp.sum(d_soft, axis=0)
        g_a_log = d_neg * neg_rate
        d_proj = jnp.concatenate([d_gate_z, d_conv_in], axis=-1).astype(jnp.bfloat16)
        d_step = d_soft.astype(jnp.bfloat16)
        normal_in = (unit_rows * norm_f32).astype(jnp.bfloat16)
        g_dt_w = jnp.einsum("ti,tj->ij", normal_in, d_step, preferred_element_type=jnp.float32)
        d_normal = jnp.einsum(
            "tj,ij->ti", d_proj, in_full, preferred_element_type=jnp.float32
        ) + jnp.einsum("tj,ij->ti", d_step, dt_full, preferred_element_type=jnp.float32)
        g_norm_gain = jnp.sum(d_normal * unit_rows, axis=0)
        d_unit_in = d_normal * norm_f32
        d_inputs.append(
            d_out
            + row_scale
            * (d_unit_in - unit_rows * jnp.mean(d_unit_in * unit_rows, axis=-1, keepdims=True))
        )
        factors.append((normal_in, d_proj, normed, d_branch))
        local_small = (g_dt_w, g_norm_gain, g_gate_gain, g_conv_w, g_conv_b)
        local_heads = (g_dt_bias, g_a_log, g_d_skip)
        small = local_small if small is None else jax.tree.map(jnp.add, small, local_small)
        heads_sum = (
            local_heads if heads_sum is None else jax.tree.map(jnp.add, heads_sum, local_heads)
        )
    return (d_inputs, factors, small, heads_sum)


def reduce_grads(factors, small_terms, heads_sum):
    in_total = jnp.zeros((factors[0][0].shape[1], factors[0][1].shape[1]), jnp.float32)
    for normal_in, d_proj, normed, d_branch in factors:
        in_total = in_total + jnp.einsum(
            "ti,tj->ij", normal_in, d_proj, preferred_element_type=jnp.float32
        )
    g_in_w = lax.psum_scatter(in_total, ("wide", "narrow"), scatter_dimension=0, tiled=True)
    out_total = jnp.zeros((factors[0][2].shape[1], factors[0][3].shape[1]), jnp.float32)
    for normal_in, d_proj, normed, d_branch in factors:
        out_total = out_total + jnp.einsum(
            "ti,tj->ij", normed, d_branch, preferred_element_type=jnp.float32
        )
    rest = (
        lax.psum_scatter(out_total, ("wide", "narrow"), scatter_dimension=0, tiled=True),
        lax.psum_scatter(small_terms[0], ("wide", "narrow"), scatter_dimension=0, tiled=True),
        lax.psum_scatter(small_terms[1], ("wide", "narrow"), scatter_dimension=0, tiled=True),
        lax.psum_scatter(small_terms[2], ("wide", "narrow"), scatter_dimension=0, tiled=True),
        lax.psum_scatter(small_terms[3], ("wide", "narrow"), scatter_dimension=1, tiled=True),
        lax.psum_scatter(small_terms[4], ("wide", "narrow"), scatter_dimension=0, tiled=True),
    )
    head_part = lax.psum((heads_sum[0], heads_sum[1], heads_sum[2]), ("wide", "narrow"))
    return (g_in_w, rest, head_part)


def per_device(
    tokens_short,
    tokens_long,
    cot_short,
    cot_long,
    seq_lengths,
    norm_gain,
    in_w,
    dt_w,
    conv_w,
    conv_b,
    dt_bias,
    a_log,
    d_skip,
    gate_gain,
    out_w,
):
    shards = (in_w, dt_w, norm_gain, conv_w, conv_b, gate_gain, out_w)
    head_params = (
        dt_bias.astype(jnp.float32),
        a_log.astype(jnp.float32),
        d_skip.astype(jnp.float32),
    )
    micro_group = [(tokens_short, seq_lengths[0, 0]), (tokens_long, seq_lengths[1, 0])]
    outputs, saved, kept = forward_pass(micro_group, shards, head_params)
    d_inputs, factors, small, heads_sum = backward_pass(
        micro_group, [cot_short, cot_long], saved, shards, head_params
    )
    g_in_w, rest, head_part = reduce_grads(factors, small, heads_sum)
    g_out_w, g_dt_w, g_norm_gain, g_gate_gain, g_conv_w, g_conv_b = rest
    g_dt_bias, g_a_log, g_d_skip = head_part
    return (
        outputs[0],
        outputs[1],
        d_inputs[0],
        d_inputs[1],
        g_norm_gain,
        g_in_w,
        g_dt_w,
        g_conv_w,
        g_conv_b,
        g_dt_bias,
        g_a_log,
        g_d_skip,
        g_gate_gain,
        g_out_w,
    )


def solution(mesh):
    placed = (
        P(("wide", "narrow"), None),
        P(("wide", "narrow"), None),
        P(("wide", "narrow"), None),
        P(("wide", "narrow"), None),
        P(None, ("wide", "narrow")),
        P(("wide", "narrow")),
        P(("wide", "narrow"), None),
        P(("wide", "narrow"), None),
        P(None, ("wide", "narrow")),
        P(("wide", "narrow")),
        P(),
        P(),
        P(),
        P(("wide", "narrow")),
        P(("wide", "narrow"), None),
    )
    return jax.shard_map(
        per_device,
        mesh=mesh,
        in_specs=placed,
        out_specs=(
            P(("wide", "narrow"), None),
            P(("wide", "narrow"), None),
            P(("wide", "narrow"), None),
            P(("wide", "narrow"), None),
            P(("wide", "narrow")),
            P(("wide", "narrow"), None),
            P(("wide", "narrow"), None),
            P(None, ("wide", "narrow")),
            P(("wide", "narrow")),
            P(),
            P(),
            P(),
            P(("wide", "narrow")),
            P(("wide", "narrow"), None),
        ),
        check_vma=False,
    )
```

profile of v0, /device:TPU:0, one launch (start us, length us, event | category | flops | bytes accessed | tf_op | source)
XLA Modules:
  0.0 2572.6 jit_solution(14217200676588883074)
XLA Ops:
  11.1 44.4 %all-reduce.11 = (bf16[2048]{0:T(1024)(128)(2,1)S(1)}, bf16[4352]{0:T(1024)(128)(2,1)S(1)}) all-reduce(bf16[2048]{0:T(1024)(128)(2,1)S(1)} %dynamic-update-slice, bf16[4352]{0:T(1024)(128)(2,1)S(1)} %dynamic-update-slice.1), channel_id=1, replica_groups=mesh['wide'=16,'narrow'=2] {'wide','narrow'}, use_global_device_ids=true, to_apply=%add.4 | all-reduce | flops 6400 | bytes 25600
  55.6 66.4 %all-gather.1 = bf16[32,1,128]{2,1,0:T(2,128)(2,1)S(1)} all-gather(bf16[1,1,128]{2,1,0:T(2,128)(2,1)} %bitcast.397), channel_id=1, replica_groups=mesh['wide'=16,'narrow'=2] {'wide','narrow'}, dimensions={0}, use_global_device_ids=true | all-gather | bytes 8448 | tf_op jit(solution)/shard_map/all_gather | solution.py:188
  122.8 66.4 %all-gather = bf16[32,136,4]{1,2,0:T(4,128)(2,1)S(1)} all-gather(bf16[1,136,4]{1,2,0:T(4,128)(2,1)} %bitcast.396), channel_id=1, replica_groups=mesh['wide'=16,'narrow'=2] {'wide','narrow'}, dimensions={0}, use_global_device_ids=true | all-gather | bytes 35904 | tf_op jit(solution)/shard_map/all_gather | solution.py:186
  190.0 71.5 %all_gather.31 = bf16[2048,64]{1,0:T(8,128)(2,1)S(1)} all-gather(bf16[64,64]{1,0:T(8,128)(2,1)} %param.26), channel_id=1, replica_groups=mesh['wide'=16,'narrow'=2] {'wide','narrow'}, dimensions={0}, use_global_device_ids=true | all-gather | bytes 270336 | tf_op jit(solution)/shard_map/all_gather | solution.py:170
  317.1 17.1 all-gather.7.cloned.1.call-done
  379.1 37.0 %fusion.258 = f32[512,8448]{1,0:T(8,128)} fusion(bf16[2048,8448]{1,0:T(8,128)(2,1)} %all-gather.5.cloned.1.call-done, bf16[512,2048]{1,0:T(8,128)(2,1)S(1)} %copy-done.8, f32[2048]{0:T(1024)S(1)} %convert_element_type.148, f32[512]{0:T(512)S(1)} %add_rsqrt_fusion.1), kind=kOutput, calls=%fused_computation.388 | convolution fusion | flops 17720934400 | bytes 54011904 | tf_op jit(solution)/shard_map/dot_general | solution.py:180
  423.6 18.5 multiply_convert_fusion
  521.6 64.8 %while.10 = (s32[]{:T(128)}, f32[64,64,128]{2,1,0:T(8,128)S(1)}, f32[2,64,256,64]{2,3,1,0:T(8,128)}, f32[2,64,64,128]{3,2,1,0:T(8,128)}, f32[2,64,256]{2,1,0:T(8...) while((s32[]{:T(128)}, f32[64,64,128]{2,1,0:T(8,128)S(1)}, ...), condition=%wide.region_4.5_spmd.clone, body=%wide.region_3.4_spmd.clone.sunk | while | flops 6620364800 | bytes 150935888 | solution.py:207
  523.1 22.5 fusion.352
  555.2 22.5 fusion.352
  628.6 17.1 multiply_reduce_fusion.12
  645.7 18.4 multiply_reduce_fusion.13
  690.1 220.1 %while.11 = (s32[]{:T(128)}, f32[64,64,128]{2,1,0:T(8,128)S(1)}, f32[64]{0:T(128)}, f32[2,64,256,64]{2,3,1,0:T(8,128)}, f32[2,256,128]{2,1,0:T(8,128)}, /*index=...) while((s32[]{:T(128)}, f32[64,64,128]{2,1,0:T(8,128)S(1)}, ...), condition=%wide.region_24.25_spmd.clone, body=%wide.region_15.24_spmd.clone.sunk | while | flops 14985576448 | bytes 191517456 | solution.py:276
  759.1 26.8 %multiply_reduce_fusion.39 = (f32[64,256]{1,0:T(8,128)S(1)}, f32[64,256]{1,0:T(8,128)S(1)}, f32[64,256]{1,0:T(8,128)S(1)}, f32[64,256,256]{2,1,0:T(8,128)}) fusion(f32[64,256]{1,0:T(8,128)S(1)} %get-tuple-element.886, f32[256,256]{1,0:T(8,128)S(1)} %copy-done.25, f32[64,256]{1,0:T(8,128)S(1)} %fusion.368, pred[256,256]{1,0:T(8,128)(4,1)S(1)} %copy-done.39, ...), kind=kOutput, calls=%fused_computation.58.clone.1 | convolution fusion | flops 3258925056 | bytes 25886724 | tf_op jit(solution)/shard_map/while/body/eval_jaxpr/hip,hjp->hij/dot_general | solution.py:112
  826.7 17.1 fusion.374
  865.2 27.0 %multiply_reduce_fusion.39 = (f32[64,256]{1,0:T(8,128)S(1)}, f32[64,256]{1,0:T(8,128)S(1)}, f32[64,256]{1,0:T(8,128)S(1)}, f32[64,256,256]{2,1,0:T(8,128)}) fusion(f32[64,256]{1,0:T(8,128)S(1)} %get-tuple-element.886, f32[256,256]{1,0:T(8,128)S(1)} %copy-done.25, f32[64,256]{1,0:T(8,128)S(1)} %fusion.368, pred[256,256]{1,0:T(8,128)(4,1)S(1)} %copy-done.39, ...), kind=kOutput, calls=%fused_computation.58.clone.1 | convolution fusion | flops 3258925056 | bytes 25886724 | tf_op jit(solution)/shard_map/while/body/eval_jaxpr/hip,hjp->hij/dot_general | solution.py:112
  953.9 23.8 fusion.261
  981.0 29.4 %convolution_add_fusion.3 = f32[4096,2048]{1,0:T(8,128)} fusion(f32[4096,2048]{1,0:T(8,128)} %fusion.205, bf16[512,2048]{1,0:T(8,128)(2,1)} %param.22, f32[512]{0:T(512)S(1)} %copy-done.109, f32[512,4096]{1,0:T(8,128)} %get-tuple-element.686, f32[4096]{0:T(1024)S(1)} %bitcast.383, f32[512]{0:T(512)S(1)} %copy-done.90), kind=kOutput, calls=%fused_computation.167 | convolution fusion | flops 8607760384 | bytes 77615104 | tf_op jit(solution)/shard_map/ti,tj->ij/dot_general | solution.py:323
  1031.8 25.2 fusion.181
  1056.9 49.5 %convolution_add_fusion.2 = f32[2048,8448]{1,0:T(8,128)} fusion(f32[2048,8448]{1,0:T(8,128)} %fusion.181, bf16[512,4352]{1,0:T(8,128)(2,1)} %add_convert_fusion, bf16[512,4096]{1,0:T(8,128)(2,1)} %get-tuple-element.704, bf16[512,2048]{1,0:T(8,128)(2,1)S(1)} %copy-done.9, f32[2048]{0:T(1024)S(1)} %copy-done.33, f32[512]{0:T(512)S(1)} %copy-done.50), kind=kOutput, calls=%fused_computation.166 | convolution fusion | flops 17755537408 | bytes 149170176 | tf_op jit(solution)/shard_map/ti,tj->ij/dot_general | solution.py:317
  1125.5 26.1 %fusion.141 = f32[512,2048]{1,0:T(8,128)} fusion(bf16[2048,8448]{1,0:T(8,128)(2,1)} %all-gather.5.cloned.1.call-done, bf16[512,4352]{1,0:T(8,128)(2,1)} %add_convert_fusion, bf16[512,4096]{1,0:T(8,128)(2,1)} %get-tuple-element.704), kind=kOutput, calls=%fused_computation.200 | convolution fusion | flops 17734041600 | bytes 47448064 | tf_op jit(solution)/shard_map/tj,ij->ti/dot_general | solution.py:294
  1157.8 39.8 %all-reduce.10 = (f32[2048]{0:T(1024)S(1)}, f32[4352]{0:T(1024)S(1)}, f32[64]{0:T(128)}, f32[64]{0:T(128)}, f32[64]{0:T(128)}, /*index=5*/f32[4096]{0:T(1024)S(1)}) all-reduce(f32[2048]{0:T(1024)S(1)} %add.467, f32[4352]{0:T(1024)S(1)} %add.471, f32[64]{0:T(128)S(1)} %add.472, ...), channel_id=2, replica_groups=mesh['wide'=16,'narrow'=2] {'wide','narrow'}, use_global_device_ids=true, to_apply=%region_28.29.clone | all-reduce | flops 10688 | bytes 85504
  1234.8 704.7 %reduce-scatter.9.cloned.1.call-done = f32[128,2048]{1,0:T(8,128)} async-done(((f32[4096,2048]{1,0:T(8,128)}), f32[128,2048]{1,0:T(8,128)}) %reduce-scatter.9.cloned.1.call-update) | async-done | bytes 1048592 | tf_op jit(solution)/shard_map/reduce_scatter | solution.py:327
  1939.5 626.0 %reduce-scatter.5.cloned.1.call-done = f32[64,8448]{1,0:T(8,128)} async-done(((f32[2048,8448]{1,0:T(8,128)}), f32[64,8448]{1,0:T(8,128)}) %reduce-scatter.5.cloned.1.call-update) | async-done | bytes 2162704 | tf_op jit(solution)/shard_map/reduce_scatter | solution.py:320
  (542 shorter events, 549.4 us)
Async XLA Ops:
  7.2 264.8 %all-gather.5.cloned.1.call-start = ((), (), s32[]{:S(2)}) async-start(), calls=%async_computation.3 | async-start | bytes 35684352 | tf_op jit(solution)/shard_map/all_gather | solution.py:169
  7.9 259.0 %copy-start.113 = (s32[2,1]{0,1:T(1,128)S(1)}, s32[2,1]{0,1:T(1,128)}, u32[]{:S(2)}) copy-start(s32[2,1]{0,1:T(1,128)} %param.23) | copy-start | bytes 28
  7.9 262.1 %copy-start.11 = (bf16[128,2048]{1,0:T(8,128)(2,1)S(1)}, bf16[128,2048]{1,0:T(8,128)(2,1)}, u32[]{:S(2)}) copy-start(bf16[128,2048]{1,0:T(8,128)(2,1)} %param.19) | copy-start | bytes 1572868
  7.9 326.3 %all-gather.7.cloned.1.call-start = ((), (), s32[]{:S(2)}) async-start(), calls=%async_computation.4 | async-start | bytes 17301504 | tf_op jit(solution)/shard_map/all_gather | solution.py:189
  8.7 261.6 %copy-start.114 = (bf16[64]{0:T(256)(128)(2,1)S(1)}, bf16[64]{0:T(256)(128)(2,1)}, u32[]{:S(2)}) copy-start(bf16[64]{0:T(256)(128)(2,1)} %param.30) | copy-start | bytes 388
  8.7 1222.0 %all-reduce.14.cloned.1.call-start = ((), (), s32[]{:S(2)}) async-start(), calls=%async_computation.8 | async-start | bytes 139264
  55.5 432.7 %copy-start.32 = (f32[2048]{0:T(1024)}, f32[2048]{0:T(1024)S(1)}, u32[]{:S(2)}) copy-start(f32[2048]{0:T(1024)S(1)} %convert_element_type.148) | copy-start | bytes 24580
  122.0 328.5 %copy-start.34 = (f32[32,1,128]{2,1,0:T(1,128)}, f32[32,1,128]{2,1,0:T(1,128)S(1)}, u32[]{:S(2)}) copy-start(f32[32,1,128]{2,1,0:T(1,128)S(1)} %convert_element_type.173) | copy-start | bytes 49156
  122.8 522.9 %copy-start.47 = (f32[4096]{0:T(1024)}, f32[4096]{0:T(1024)S(1)}, u32[]{:S(2)}) copy-start(f32[4096]{0:T(1024)S(1)} %mul.1105) | copy-start | bytes 49156
  263.8 115.3 %copy-start.49 = (f32[512]{0:T(512)}, f32[512]{0:T(512)S(1)}, u32[]{:S(2)}) copy-start(f32[512]{0:T(512)S(1)} %add_rsqrt_fusion.1) | copy-start | bytes 6148
  268.2 182.3 %copy-start.111 = (f32[128]{0:T(128)}, f32[128]{0:T(128)S(1)}, u32[]{:S(2)}) copy-start(f32[128]{0:T(128)S(1)} %compare_convert_fusion.2) | copy-start | bytes 1540
  270.3 217.9 %copy-start.93 = (f32[128]{0:T(128)}, f32[128]{0:T(128)S(1)}, u32[]{:S(2)}) copy-start(f32[128]{0:T(128)S(1)} %add_rsqrt_fusion.3) | copy-start | bytes 1540
  270.7 203.5 %copy-start.63 = (f32[128,64]{0,1:T(8,128)}, f32[128,64]{0,1:T(8,128)S(1)}, u32[]{:S(2)}) copy-start(f32[128,64]{0,1:T(8,128)S(1)} %convolution_add_fusion.10) | copy-start | bytes 98308
  271.3 152.3 %copy-start.55 = (f32[4352]{0:T(1024)}, f32[4352]{0:T(1024)S(1)}, u32[]{:S(2)}) copy-start(f32[4352]{0:T(1024)S(1)} %get-tuple-element.613) | copy-start | bytes 52228
  271.3 152.3 %copy-start.57 = (f32[4352]{0:T(1024)}, f32[4352]{0:T(1024)S(1)}, u32[]{:S(2)}) copy-start(f32[4352]{0:T(1024)S(1)} %get-tuple-element.614) | copy-start | bytes 52228
  271.3 152.3 %copy-start.59 = (f32[4352]{0:T(1024)}, f32[4352]{0:T(1024)S(1)}, u32[]{:S(2)}) copy-start(f32[4352]{0:T(1024)S(1)} %get-tuple-element.615) | copy-start | bytes 52228
  271.3 152.3 %copy-start.61 = (f32[4352]{0:T(1024)}, f32[4352]{0:T(1024)S(1)}, u32[]{:S(2)}) copy-start(f32[4352]{0:T(1024)S(1)} %get-tuple-element.616) | copy-start | bytes 52228
  317.1 133.4 %copy-start.100 = (f32[128]{0:T(128)}, f32[128]{0:T(128)S(1)}, u32[]{:S(2)}) copy-start(f32[128]{0:T(128)S(1)} %add_rsqrt_fusion.2) | copy-start | bytes 1540
  693.1 27.6 %copy-start.38 = (pred[256,256]{1,0:T(8,128)(4,1)}, pred[256,256]{1,0:T(8,128)(4,1)S(1)}, u32[]{:S(2)}) copy-start(pred[256,256]{1,0:T(8,128)(4,1)S(1)} %iota_compare_fusion.19) | copy-start | bytes 196612 | tf_op jit(solution)/shard_map/while
  978.6 256.2 %reduce-scatter.7.cloned.1.call-start = ((), (), s32[]{:S(2)}) async-start(), calls=%async_computation.6 | async-start | bytes 1081344 | tf_op jit(solution)/shard_map/reduce_scatter | solution.py:328
  978.8 31.5 %copy-start.66 = (bf16[512,64]{0,1:T(8,128)(2,1)}, bf16[512,64]{0,1:T(8,128)(2,1)S(1)}, u32[]{:S(2)}) copy-start(bf16[512,64]{0,1:T(8,128)(2,1)S(1)} %get-tuple-element.678) | copy-start | bytes 196612
  980.9 958.6 %reduce-scatter.9.cloned.1.call-start = ((), (), s32[]{:S(2)}) async-start(), calls=%async_computation.7 | async-start | bytes 34603008 | tf_op jit(solution)/shard_map/reduce_scatter | solution.py:327
  1010.4 1555.1 %reduce-scatter.5.cloned.1.call-start = ((), (), s32[]{:S(2)}) async-start(), calls=%async_computation.5 | async-start | bytes 71368704 | tf_op jit(solution)/shard_map/reduce_scatter | solution.py:320
  1151.7 47.8 %copy-start.27 = (bf16[128,2048]{1,0:T(8,128)(2,1)S(1)}, bf16[128,2048]{1,0:T(8,128)(2,1)}, u32[]{:S(2)}) copy-start(bf16[128,2048]{1,0:T(8,128)(2,1)} %param.21) | copy-start | bytes 1572868
  (138 other events, 1527.0 us)
Sparse Core Ops, SparseCore 0:
  10.9 206.4 all-gather.4
  220.4 113.8 all-gather.6
  978.8 116.0 all-reduce.13
  1097.5 137.2 reduce-scatter.6
  1237.7 701.8 reduce-scatter.8
  1947.5 617.9 reduce-scatter.4
where the time goes:
time: 2580 us; the launch traced here: 2570 us
  waiting for transfers between devices  1350 us (52%)
  matrix products  546 us (21%)
  blocking collectives  289 us (11%)
  other arithmetic  182 us (7%)
  local copies, waits for them, and re-layouts  177 us (7%)
    reduce_scatter x1, waiting for transfers between devices, reduce_grads(): lax.psum_scatter(out_total, ('wide', 'narrow'), scatter_dimension=0, tile...  705 us
    reduce_scatter x1, waiting for transfers between devices, reduce_grads(): lax.psum_scatter(in_total, ('wide', 'narrow'), scatter_dimension=0, tiled...  626 us
    unnamed x2, blocking collectives  84.2 us
    dot_general x2, matrix products, reduce_grads(): jnp.einsum('ti,tj->ij', normal_in, d_proj, preferred_element_type=jnp.flo...  74.7 us
    all_gather x1, blocking collectives, forward_pass(): lax.all_gather(dt_w, ('wide', 'narrow'), axis=0, tiled=True)  71.5 us
    reshape x6, local copies, waits for them, and re-layouts, from_heads(): values.transpose(0, 2, 1, 3).reshape(-1, values.shape[1] * values.shape[3])  68 us
    all_gather x1, blocking collectives, forward_pass(): lax.all_gather(gate_gain, ('wide', 'narrow'), axis=0, tiled=True)  66.4 us
    all_gather x1, blocking collectives, forward_pass(): lax.all_gather(conv_w, ('wide', 'narrow'), axis=1, tiled=True)  66.4 us
  transfers between devices with their start and end apart: 6, of which 4 were waited for; matrix products, arithmetic and copies ran while one was open for 11% of the time, Pallas kernels for 0%

commit v1 on v0

v1 whole, which is shorter than its diff:
```python
import functools

import jax
import jax.numpy as jnp
import numpy as np
from jax import lax
from jax.experimental import pallas as pl
from jax.experimental.pallas import tpu as pltpu
from jax.sharding import Mesh
from jax.sharding import PartitionSpec as P

D = 2048
DI = 4096
HEADS = 64
HEAD_DIM = 64
STATE = 128
KERNEL = 4
SPAN = 256
EPS = 1e-05
BF = jnp.bfloat16
F32 = jnp.float32

SLOTS = 4
AHEADS = 8
WIDTH = DI // SLOTS
LOCAL_HEADS = HEADS // SLOTS
XBC = WIDTH + 2 * STATE
XCOLS = XBC + 128
ALL = ("ra", "core", "rb", "x")
NEG = -1e30
TILE = 512

SWAP = [(0, 1), (1, 0)]
CYCLE = (0, 2, 4, 6, 7, 5, 3, 1)


def nt(a, b):
    return lax.dot_general(a, b, (((1,), (1,)), ((), ())), preferred_element_type=F32)


def nn(a, b):
    return lax.dot_general(a, b, (((1,), (0,)), ((), ())), preferred_element_type=F32)


def tn(a, b):
    return lax.dot_general(a, b, (((0,), (0,)), ((), ())), preferred_element_type=F32)


LOG2E = 1.4426950408889634
ROWS = 64


def sigmoid(v):
    return 0.5 * jnp.tanh(0.5 * v) + 0.5


def lane_index():
    return lax.broadcasted_iota(jnp.int32, (1, 128), 1)


def three_parts(values):
    values = jnp.where(lane_index() < LOCAL_HEADS, values, 0.0)
    high = values.astype(BF).astype(F32)
    rest = values - high
    mid = rest.astype(BF).astype(F32)
    low = rest - mid
    return (high + pltpu.roll(mid, LOCAL_HEADS, 1) + pltpu.roll(low, 2 * LOCAL_HEADS, 1)).astype(BF)


def add_parts(values):
    return values + pltpu.roll(values, 128 - LOCAL_HEADS, 1) + pltpu.roll(values, 128 - 2 * LOCAL_HEADS, 1)


def triangle(n, lower):
    i = lax.broadcasted_iota(jnp.int32, (n, n), 0)
    j = lax.broadcasted_iota(jnp.int32, (n, n), 1)
    return jnp.where(i >= j if lower else i <= j, 1.0, 0.0).astype(BF)


def running_sum(values, lower):
    return add_parts(nn(triangle(values.shape[0], lower), three_parts(values)))


def two_parts(values):
    values = jnp.where(lane_index() < LOCAL_HEADS, values, 0.0)
    high = values.astype(BF).astype(F32)
    return (high + pltpu.roll(values - high, LOCAL_HEADS, 1)).astype(BF)


def softplus(v):
    return jnp.maximum(v, 0.0) + jnp.log1p(jnp.exp(-jnp.abs(v)))


def conv_tile(p_ref, cw_ref, cb_ref, r0, seq, cols):
    starts = (r0 & (seq - 1)) == 0
    before = p_ref[pl.ds(pl.multiple_of(jnp.maximum(r0 - 8, 0), 8), 8), cols]
    before = jnp.where(starts, 0.0, before)
    here = p_ref[pl.ds(r0, ROWS), cols]
    both = jnp.concatenate([before, here], axis=0)
    back = [here] + [pltpu.roll(both, m, 0)[8:] for m in (1, 2, 3)]
    total = cb_ref[0:1, cols]
    for m in range(KERNEL):
        total = total + cw_ref[3 - m : 4 - m, cols] * back[m]
    return total, back


def fwd_kernel(
    steps_ref, p_ref, cw_ref, cb_ref, hp_ref, dsk_ref, seg_ref, bc_ref, *refs
):
    y_ref, act_ref, slope_ref, h_ref, dt_s, parts_s, grow_s, rt_s, g_s = refs[-9:]
    first = steps_ref[pl.program_id(0)] == 0
    seq = jnp.where(first, 128, 512)
    lane = lane_index()

    def conv_step(i, carry):
        r0 = pl.multiple_of(i * ROWS, ROWS)
        rows = pl.ds(r0, ROWS)
        for c in range(XBC // 128):
            cols = slice(c * 128, c * 128 + 128)
            conv, _ = conv_tile(p_ref, cw_ref, cb_ref, r0, seq, cols)
            gate = sigmoid(conv)
            act = conv * gate
            act_ref[rows, cols] = act.astype(BF)
            slope_ref[rows, cols] = (gate + act * (1.0 - gate)).astype(BF)
        dt_s[rows, :] = softplus(p_ref[rows, XBC:] + hp_ref[0:1])
        return carry

    lax.fori_loop(0, TILE // ROWS, conv_step, 0)
    rate = hp_ref[1:2]

    def block(off, q, read_state, make_state):
        rows = pl.ds(off, q)
        dt = dt_s[rows, :]
        cum2 = running_sum(dt * rate, True) * LOG2E
        parts_s[:q, :] = three_parts(cum2)
        turned = (cum2 - jnp.log2(dt)).T
        for h in range(LOCAL_HEADS):
            rt_s[h, :, :q] = turned[h : h + 1]
        b = act_ref[rows, WIDTH : WIDTH + STATE]
        c = act_ref[rows, WIDTH + STATE :]
        g_s[:q, :q] = nt(c, b)
        if read_state:
            grow_s[:q, :] = two_parts(jnp.exp2(cum2))
        if make_state:
            grow_s[:q, :] = two_parts(jnp.exp2(cum2[q - 1 : q] - cum2) * dt)
            b_turned = b.astype(F32).T.astype(BF)
        diagonal = lax.broadcasted_iota(jnp.int32, (128, 128), 0) >= lax.broadcasted_iota(
            jnp.int32, (128, 128), 1
        )

        def pair(p, carry):
            lanes = pl.ds(pl.multiple_of(p * 128, 128), 128)
            x2 = act_ref[rows, lanes]
            zero = jnp.zeros_like(x2)
            x_heads = [jnp.where(lane < HEAD_DIM, x2, zero), jnp.where(lane < HEAD_DIM, zero, x2)]
            cols = nn(parts_s[:q, :], bc_ref[:, pl.ds(pl.multiple_of(p * 256, 256), 256)])
            if read_state:
                carried = nn(grow_s[:q, :], seg_ref[:, lanes]) * nn(c, h_ref[0, :, lanes].astype(BF))
            for rt in range(q // 128):
                top = rt * 128
                mixes = []
                for j in range(2):
                    col = cols[top : top + 128, j * 128 : j * 128 + 128]
                    for ct in range(rt + 1):
                        lo = ct * 128
                        spread = col - rt_s[p * 2 + j, :, lo : lo + 128]
                        if ct == rt:
                            spread = jnp.where(diagonal, spread, NEG)
                        mixes.append((g_s[top : top + 128, lo : lo + 128] * jnp.exp2(spread)).astype(BF))
                x_both = jnp.concatenate([x[: top + 128] for x in x_heads], axis=0)
                out = nn(jnp.concatenate(mixes, axis=1), x_both)
                out = out + dsk_ref[0:1, lanes] * x2[top : top + 128].astype(F32)
                if read_state:
                    out = out + carried[top : top + 128]
                y_ref[pl.ds(off + top, 128), lanes] = out.astype(y_ref.dtype)
            if make_state:
                wide = nn(grow_s[:q, :], seg_ref[:, lanes])
                h_ref[0, :, lanes] = nn(b_turned, (wide * x2.astype(F32)).astype(BF))
            return carry

        lax.fori_loop(0, LOCAL_HEADS // 2, pair, 0)

    @pl.when(first)
    def _():
        def one(i, carry):
            block(pl.multiple_of(i * 128, 128), 128, False, False)
            return carry

        lax.fori_loop(0, TILE // 128, one, 0)

    @pl.when(jnp.logical_not(first))
    def _():
        block(0, SPAN, False, True)
        block(SPAN, SPAN, True, False)


def bwd_kernel(
    steps_ref, p_ref, act_ref, slope_ref, dy_ref, h_ref, cw_ref, hp_ref, dsk_ref, seg_ref, bc_ref, *refs
):
    dp_ref, acc_ref, hacc_ref = refs[-18:-15]
    dt_s, parts_s, grow_s, ct_s, gt_s, dgt_s, kc_s, kr_s, fold_s, dbc_s, ds_s, da_s, dst_s, after_s, sums_s = refs[-15:]
    first = steps_ref[pl.program_id(0)] == 0
    seq = jnp.where(first, 128, 512)
    lane = lane_index()
    head_row = lax.broadcasted_iota(jnp.int32, (LOCAL_HEADS, 1), 0)

    @pl.when(pl.program_id(0) == 0)
    def _():
        acc_ref[...] = jnp.zeros_like(acc_ref)
        hacc_ref[...] = jnp.zeros_like(hacc_ref)

    rate = hp_ref[1:2]
    dt_s[...] = softplus(p_ref[:, XBC:] + hp_ref[0:1])

    def block(off, q, state_in, state_out):
        rows = pl.ds(off, q)
        dt = dt_s[rows, :]
        cum2 = running_sum(dt * rate, True) * LOG2E
        parts_s[:q, :] = three_parts(cum2 - jnp.log2(dt))
        turned = cum2.T
        for h in range(LOCAL_HEADS):
            ct_s[h, :, :q] = turned[h : h + 1]
        b = act_ref[rows, WIDTH : WIDTH + STATE]
        c = act_ref[rows, WIDTH + STATE :]
        gt_s[:q, :q] = nt(b, c)
        dgt_s[:q, :q] = jnp.zeros((q, q), F32)
        kc_s[:q, :] = jnp.zeros((q, 128), F32)
        kr_s[:, :q] = jnp.zeros((LOCAL_HEADS, q), F32)
        if state_in or state_out:
            fold_s[:q, :] = jnp.zeros((q, 128), F32)
            dbc_s[:q, :] = jnp.zeros((q, 128), F32)
        if state_in:
            grow_s[:q, :] = two_parts(jnp.exp2(cum2))
            c_turned = c.astype(F32).T.astype(BF)
        if state_out:
            decay = jnp.exp2(cum2[q - 1 : q] - cum2)
            grow_s[:q, :] = two_parts(decay * dt)
        diagonal = lax.broadcasted_iota(jnp.int32, (128, 128), 1) >= lax.broadcasted_iota(
            jnp.int32, (128, 128), 0
        )
        tiles = q // 128

        def pair(p, carry):
            lanes = pl.ds(pl.multiple_of(p * 128, 128), 128)
            x2 = act_ref[rows, lanes]
            dy2 = dy_ref[rows, lanes]
            zero = jnp.zeros_like(dy2)
            dy_heads = [jnp.where(lane < HEAD_DIM, dy2, zero), jnp.where(lane < HEAD_DIM, zero, dy2)]
            cols = nn(parts_s[:q, :], bc_ref[:, pl.ds(pl.multiple_of(p * 256, 256), 256)])
            if state_in:
                hb = h_ref[0, :, lanes].astype(BF)
                dyc = dy2.astype(F32) * nn(grow_s[:q, :], seg_ref[:, lanes])
                dyb = dyc.astype(BF)
                fold_s[:q, :] += nt((dyc * nn(c, hb)).astype(BF), seg_ref[:, lanes])
                dbc_s[:q, :] += nt(dyb, hb)
                ds_s[:, lanes] = nn(c_turned, dyb).astype(BF)
            if state_out:
                sb = ds_s[:, lanes]
                wide = nn(grow_s[:q, :], seg_ref[:, lanes])
                bd = nn(b, sb)
                xf = x2.astype(F32)
                fold_s[:q, :] += nt((xf * bd).astype(BF), seg_ref[:, lanes])
                dbc_s[:q, :] += nt((wide * xf).astype(BF), sb)
                late = wide * bd
            picks = [jnp.where(lane == p * 2 + j, 1.0, 0.0).astype(BF) for j in range(2)]
            marks = [jnp.where(head_row == p * 2 + j, 1.0, 0.0).astype(BF) for j in range(2)]
            for jt in range(tiles):
                lo = jt * 128
                span = q - lo
                xj = x2[lo : lo + 128]
                mixes = []
                terms = []
                dgs = [None] * tiles
                for j in range(2):
                    col = cols[lo : lo + 128, j * 128 : j * 128 + 128]
                    for it in range(jt, tiles):
                        at = it * 128
                        spread = ct_s[p * 2 + j, :, at : at + 128] - col
                        if it == jt:
                            spread = jnp.where(diagonal, spread, NEG)
                        e = jnp.exp2(spread)
                        score = gt_s[lo : lo + 128, at : at + 128]
                        dme = nt(xj, dy_heads[j][at : at + 128]) * e
                        dgs[it] = dme if dgs[it] is None else dgs[it] + dme
                        terms.append((dme * score).astype(BF))
                        mixes.append((score * e).astype(BF))
                for it in range(jt, tiles):
                    dgt_s[lo : lo + 128, it * 128 : it * 128 + 128] += dgs[it]
                half = len(terms) // 2
                kc_s[lo : lo + 128, :] += nn(
                    jnp.concatenate(terms, axis=1),
                    jnp.concatenate([jnp.broadcast_to(v, (span, 128)) for v in picks], axis=0),
                )
                kr_s[:, lo:q] += nn(
                    jnp.concatenate([jnp.broadcast_to(v, (LOCAL_HEADS, 128)) for v in marks], axis=1),
                    jnp.concatenate(
                        [jnp.concatenate(terms[:half], axis=1), jnp.concatenate(terms[half:], axis=1)], axis=0
                    ),
                )
                dy_both = jnp.concatenate([d[lo:] for d in dy_heads], axis=0)
                out = nn(jnp.concatenate(mixes, axis=1), dy_both)
                dyj = dy2[lo : lo + 128].astype(F32)
                acc_ref[5:6, lanes] += jnp.sum(dyj * xj.astype(F32), axis=0, keepdims=True)
                out = out + dsk_ref[0:1, lanes] * dyj
                if state_out:
                    out = out + late[lo : lo + 128]
                da_s[pl.ds(off + lo, 128), lanes] = out
            return carry

        lax.fori_loop(0, LOCAL_HEADS // 2, pair, 0)

        dgt = dgt_s[:q, :q].astype(BF)
        db = nn(dgt, c)
        dc = tn(dgt, b)
        kcol = kc_s[:q, :]
        row_terms = jnp.concatenate([kr_s[:, :q], jnp.zeros((128 - LOCAL_HEADS, q), F32)], axis=0)
        d_cum = row_terms.T - kcol
        inverse = jnp.where(dt > 1e-30, 1.0 / jnp.maximum(dt, 1e-30), 0.0)
        d_dt = kcol * inverse
        if state_in:
            d_cum = d_cum + fold_s[:q, :]
            dc = dc + dbc_s[:q, :]
        if state_out:
            db = db + dbc_s[:q, :]
            d_weights = fold_s[:q, :]
            d_dt = d_dt + d_weights * decay
            w_term = d_weights * decay * dt
            last = lax.broadcasted_iota(jnp.int32, (q, 1), 0) == q - 1
            d_cum = d_cum - w_term + jnp.where(last, jnp.sum(w_term, axis=0, keepdims=True), 0.0)
        da_s[rows, WIDTH : WIDTH + STATE] = db
        da_s[rows, WIDTH + STATE :] = dc
        d_rate = running_sum(d_cum, False)
        dst_s[rows, :] = d_dt + d_rate * rate
        hacc_ref[1:2, :] += jnp.sum(d_rate * dt, axis=0, keepdims=True)

    @pl.when(first)
    def _():
        def one(i, carry):
            block(pl.multiple_of(i * 128, 128), 128, False, False)
            return carry

        lax.fori_loop(0, TILE // 128, one, 0)

    @pl.when(jnp.logical_not(first))
    def _():
        block(SPAN, SPAN, True, False)
        block(0, SPAN, False, True)

    d_soft = dst_s[...] * jax.nn.sigmoid(p_ref[:, XBC:] + hp_ref[0:1])
    d_soft = jnp.where(lane < LOCAL_HEADS, d_soft, 0.0)
    hacc_ref[0:1, :] += jnp.sum(d_soft, axis=0, keepdims=True)
    dp_ref[:, XBC:] = d_soft.astype(BF)
    sums_s[...] = jnp.zeros_like(sums_s)
    after_s[...] = jnp.zeros_like(after_s)

    def conv_step(i, carry):
        r0 = pl.multiple_of(TILE - ROWS - i * ROWS, ROWS)
        rows = pl.ds(r0, ROWS)
        ends = ((r0 + ROWS) & (seq - 1)) == 0
        fold = lambda v: jnp.sum(v.reshape(ROWS // 8, 8, 128), axis=0)
        for c in range(XBC // 128):
            cols = slice(c * 128, c * 128 + 128)
            here = p_ref[rows, cols]
            d_conv = da_s[rows, cols] * slope_ref[rows, cols].astype(F32)
            both = jnp.concatenate([d_conv, jnp.where(ends, 0.0, after_s[:, cols])], axis=0)
            after_s[:, cols] = d_conv[:8]
            total = cw_ref[3:4, cols] * d_conv
            sums_s[3, :, cols] += fold(d_conv * here)
            sums_s[4, :, cols] += fold(d_conv)
            for m in (1, 2, 3):
                ahead = pltpu.roll(both, ROWS + 8 - m, 0)[:ROWS]
                total = total + cw_ref[3 - m : 4 - m, cols] * ahead
                sums_s[3 - m, :, cols] += fold(ahead * here)
            dp_ref[rows, cols] = total.astype(BF)
        return carry

    lax.fori_loop(0, TILE // ROWS, conv_step, 0)
    for k in range(KERNEL + 1):
        acc_ref[k : k + 1, :] += jnp.sum(sums_s[k], axis=0, keepdims=True)


def stats_kernel(order_ref, y_ref, z_ref, dn_ref, gain_ref, st_ref, both_s):
    lane = lane_index()

    def step(i, carry):
        rows = pl.ds(pl.multiple_of(i * ROWS, ROWS), ROWS)
        p1 = jnp.zeros((ROWS, 128), F32)
        p2 = jnp.zeros((ROWS, 128), F32)
        for k in range(AHEADS):
            lanes = pl.ds(pl.multiple_of(order_ref[k] * 128, 128), 128)
            z = z_ref[rows, lanes].astype(F32)
            g = y_ref[rows, lanes].astype(F32) * (z * sigmoid(z))
            p1 = p1 + g * g
            p2 = p2 + g * (dn_ref[rows, k * 128 : k * 128 + 128].astype(F32) * gain_ref[0:1, lanes])
        both_s[rows, :] = jnp.where(
            lane == 0,
            jnp.sum(p1, axis=1, keepdims=True),
            jnp.where(lane == 1, jnp.sum(p2, axis=1, keepdims=True), 0.0),
        )
        return carry

    lax.fori_loop(0, y_ref.shape[0] // ROWS, step, 0)
    st_ref[...] = both_s[...].T[0:8]


def gate_kernel(order_ref, st_ref, y_ref, z_ref, dn_ref, gain_ref, n_ref, dy_ref, dz_ref, st_s):
    st_s[...] = jnp.concatenate([st_ref[...], jnp.zeros((120, y_ref.shape[0]), F32)], axis=0).T

    def step(i, carry):
        rows = pl.ds(pl.multiple_of(i * ROWS, ROWS), ROWS)
        st = st_s[rows, :]
        rg = lax.rsqrt(st[:, 0:1] * (1.0 / DI) + EPS)
        mean = rg * rg * st[:, 1:2] * (1.0 / DI)
        for k in range(AHEADS):
            lanes = pl.ds(pl.multiple_of(order_ref[k] * 128, 128), 128)
            fixed = slice(k * 128, k * 128 + 128)
            gain = gain_ref[0:1, lanes]
            z = z_ref[rows, lanes].astype(F32)
            y = y_ref[rows, lanes].astype(F32)
            sg = sigmoid(z)
            silu = z * sg
            ghat = y * silu * rg
            dg = rg * (dn_ref[rows, fixed].astype(F32) * gain) - ghat * mean
            n_ref[rows, fixed] = (ghat * gain).astype(BF)
            dy_ref[rows, lanes] = (dg * silu).astype(BF)
            dz_ref[rows, lanes] = (dg * y * (sg + silu * (1.0 - sg))).astype(BF)
        return carry

    lax.fori_loop(0, y_ref.shape[0] // ROWS, step, 0)


def norm_kernel(pieces, order_ref, *refs):
    gain_ref, u_ref = refs[pieces], refs[-1]
    at = 0
    for x_ref in refs[:pieces]:
        count = x_ref.shape[0] // ROWS

        def step(i, carry, x_ref=x_ref, at=at):
            rows = pl.ds(pl.multiple_of(i * ROWS, ROWS), ROWS)
            out = pl.ds(pl.multiple_of(at + i * ROWS, ROWS), ROWS)
            total = jnp.zeros((ROWS, 128), F32)
            for k in range(D // 128):
                v = x_ref[rows, k * 128 : k * 128 + 128].astype(F32)
                total = total + v * v
            scale = lax.rsqrt(jnp.sum(total, axis=1, keepdims=True) * (1.0 / D) + EPS)
            for k in range(AHEADS):
                lanes = pl.ds(pl.multiple_of(order_ref[k] * 256, 256), 256)
                u_ref[out, k * 256 : k * 256 + 256] = (
                    x_ref[rows, lanes].astype(F32) * scale * gain_ref[0:1, lanes]
                ).astype(BF)
            return carry

        lax.fori_loop(0, count, step, 0)
        at += x_ref.shape[0]


def whole(shape):
    return pl.BlockSpec(shape, lambda i, s: (0,) * len(shape))


def placed(cols):
    return pl.BlockSpec((TILE, cols), lambda i, s: (s[i], 0))


def params():
    return pltpu.CompilerParams(vmem_limit_bytes=56 * 1024 * 1024)


def onto(earlier, first_input):
    specs = [pl.BlockSpec(memory_space=pl.ANY)] * len(earlier)
    return list(earlier), specs, {first_input + i: i for i in range(len(earlier))}


STATES = pl.BlockSpec((1, STATE, WIDTH), lambda i, s: (s[i], 0, 0))


def ssd_forward(steps, proj, conv_w, conv_b, heads, skip, seg, spread, earlier=()):
    tokens = proj.shape[0]
    count = len(steps)
    more, more_specs, aliases = onto(earlier, 8)
    return pl.pallas_call(
        fwd_kernel,
        grid_spec=pltpu.PrefetchScalarGridSpec(
            num_scalar_prefetch=1,
            grid=(count,),
            in_specs=[
                placed(XCOLS), whole((8, XBC)), whole((8, XBC)), whole((8, 128)), whole((8, WIDTH)),
                whole((128, WIDTH)), whole((128, 128 * LOCAL_HEADS)), *more_specs,
            ],
            out_specs=[placed(WIDTH), placed(XBC), placed(XBC), STATES],
            scratch_shapes=[
                pltpu.VMEM((TILE, 128), F32),
                pltpu.VMEM((SPAN, 128), BF),
                pltpu.VMEM((SPAN, 128), BF),
                pltpu.VMEM((LOCAL_HEADS, 1, SPAN), F32),
                pltpu.VMEM((SPAN, SPAN), F32),
            ],
        ),
        out_shape=[
            jax.ShapeDtypeStruct((tokens, WIDTH), BF),
            jax.ShapeDtypeStruct((tokens, XBC), BF),
            jax.ShapeDtypeStruct((tokens, XBC), BF),
            jax.ShapeDtypeStruct((tokens // TILE, STATE, WIDTH), F32),
        ],
        input_output_aliases=aliases,
        compiler_params=params(),
        cost_estimate=pl.CostEstimate(
            flops=count * 4 * 10**9, bytes_accessed=count * 6 * 10**6, transcendentals=count * 2 * 10**6
        ),
        name="ssd_forward",
    )(jnp.asarray(steps, jnp.int32), proj, conv_w, conv_b, heads, skip, seg, spread, *more)


def ssd_backward(steps, proj, act, slope, dy, states, conv_w, conv_b, heads, skip, seg, spread, earlier=()):
    tokens = proj.shape[0]
    count = len(steps)
    more, more_specs, aliases = onto(earlier, 11)
    return pl.pallas_call(
        bwd_kernel,
        grid_spec=pltpu.PrefetchScalarGridSpec(
            num_scalar_prefetch=1,
            grid=(count,),
            in_specs=[
                placed(XCOLS), placed(XBC), placed(XBC), placed(WIDTH), STATES, whole((8, XBC)),
                whole((8, 128)), whole((8, WIDTH)), whole((128, WIDTH)), whole((128, 128 * LOCAL_HEADS)),
                *more_specs,
            ],
            out_specs=[placed(XCOLS), whole((8, XBC)), whole((8, 128))],
            scratch_shapes=[
                pltpu.VMEM((TILE, 128), F32),
                pltpu.VMEM((SPAN, 128), BF),
                pltpu.VMEM((SPAN, 128), BF),
                pltpu.VMEM((LOCAL_HEADS, 1, SPAN), F32),
                pltpu.VMEM((SPAN, SPAN), F32),
                pltpu.VMEM((SPAN, SPAN), F32),
                pltpu.VMEM((SPAN, 128), F32),
                pltpu.VMEM((LOCAL_HEADS, SPAN), F32),
                pltpu.VMEM((SPAN, 128), F32),
                pltpu.VMEM((SPAN, 128), F32),
                pltpu.VMEM((STATE, WIDTH), BF),
                pltpu.VMEM((TILE, XBC), F32),
                pltpu.VMEM((TILE, 128), F32),
                pltpu.VMEM((8, XBC), F32),
                pltpu.VMEM((KERNEL + 1, 8, XBC), F32),
            ],
        ),
        out_shape=[
            jax.ShapeDtypeStruct((tokens, XCOLS), BF),
            jax.ShapeDtypeStruct((8, XBC), F32),
            jax.ShapeDtypeStruct((8, 128), F32),
        ],
        input_output_aliases=aliases,
        compiler_params=params(),
        cost_estimate=pl.CostEstimate(
            flops=count * 10 * 10**9, bytes_accessed=count * 9 * 10**6, transcendentals=count * 4 * 10**6
        ),
        name="ssd_backward",
    )(jnp.asarray(steps, jnp.int32), proj, act, slope, dy, states, conv_w, heads, skip, seg, spread, *more)


def gate_stats(order, y, z, dn, gain):
    steps = y.shape[0] // TILE
    block = pl.BlockSpec((TILE, WIDTH), lambda i, o: (i, 0))
    return pl.pallas_call(
        stats_kernel,
        grid_spec=pltpu.PrefetchScalarGridSpec(
            num_scalar_prefetch=1,
            grid=(steps,),
            in_specs=[block, block, block, whole((8, WIDTH))],
            out_specs=pl.BlockSpec((8, TILE), lambda i, o: (0, i)),
            scratch_shapes=[pltpu.VMEM((TILE, 128), F32)],
        ),
        out_shape=jax.ShapeDtypeStruct((8, y.shape[0]), F32),
        compiler_params=params(),
        cost_estimate=pl.CostEstimate(flops=3 * 10**9, bytes_accessed=16 * 10**6, transcendentals=3 * 10**6),
        name="gate_stats",
    )(order, y, z, dn, gain)


def gate_backward(order, st, y, z, dn, gain):
    steps = y.shape[0] // TILE
    block = pl.BlockSpec((TILE, WIDTH), lambda i, o: (i, 0))
    return pl.pallas_call(
        gate_kernel,
        grid_spec=pltpu.PrefetchScalarGridSpec(
            num_scalar_prefetch=1,
            grid=(steps,),
            in_specs=[pl.BlockSpec((8, TILE), lambda i, o: (0, i)), block, block, block, whole((8, WIDTH))],
            out_specs=[block, block, block],
            scratch_shapes=[pltpu.VMEM((TILE, 128), F32)],
        ),
        out_shape=[jax.ShapeDtypeStruct(y.shape, BF)] * 3,
        compiler_params=params(),
        cost_estimate=pl.CostEstimate(flops=6 * 10**9, bytes_accessed=32 * 10**6, transcendentals=3 * 10**6),
        name="gate_backward",
    )(order, st, y, z, dn, gain)


def norm_tokens(order, values, gain, row, tokens, earlier=()):
    rows = sum(v.shape[0] for v in values)
    start = row // rows
    count = len(values)
    more, more_specs, aliases = onto(earlier, count + 2)
    return pl.pallas_call(
        functools.partial(norm_kernel, count),
        grid_spec=pltpu.PrefetchScalarGridSpec(
            num_scalar_prefetch=1,
            grid=(1,),
            in_specs=[*(whole(v.shape) for v in values), whole((8, D)), *more_specs],
            out_specs=[pl.BlockSpec((rows, D), lambda i, o: (start, 0))],
        ),
        out_shape=[jax.ShapeDtypeStruct((tokens, D), BF)],
        input_output_aliases=aliases,
        compiler_params=params(),
        cost_estimate=pl.CostEstimate(flops=rows * 10**6, bytes_accessed=rows * 8192, transcendentals=rows),
        name="norm_tokens",
    )(order, *values, gain, *more)[0]


def pack_kernel(at_ref, in_ref, dt_ref, xs_ref, xk_ref, zs_ref, zk_ref):
    rows = in_ref.shape[0]
    source = lax.broadcasted_iota(jnp.int32, (HEADS, 128), 0)
    lane = lax.broadcasted_iota(jnp.int32, (HEADS, 128), 1)
    for x_ref, z_ref, x in ((xs_ref, zs_ref, 1 - at_ref[0]), (xk_ref, zk_ref, at_ref[0])):
        for core in range(2):
            slot = 2 * core + x
            for k in range(AHEADS):
                cols = slice(k * 128, k * 128 + 128)
                at = (k * SLOTS + slot) * 128
                z_ref[core, :, cols] = in_ref[:, pl.ds(pl.multiple_of(at, 128), 128)]
                x_ref[core, :, cols] = in_ref[:, pl.ds(pl.multiple_of(DI + at, 128), 128)]
            x_ref[core, :, WIDTH:XBC] = in_ref[:, 2 * DI :]
            wanted = jnp.where(lane < LOCAL_HEADS, (lane // 2) * 8 + slot * 2 + lane % 2, -1)
            x_ref[core, :, XBC:] = nn(dt_ref[...], jnp.where(source == wanted, 1.0, 0.0).astype(BF)).astype(BF)


def pack_weights(xi, in_w, dt_w):
    rows = in_w.shape[0]
    shapes = [(2, rows, XCOLS)] * 2 + [(2, rows, WIDTH)] * 2
    return pl.pallas_call(
        pack_kernel,
        in_specs=[pl.BlockSpec(memory_space=pltpu.SMEM)] + [pl.BlockSpec(memory_space=pltpu.VMEM)] * 2,
        out_specs=[pl.BlockSpec(memory_space=pltpu.VMEM)] * 4,
        out_shape=[jax.ShapeDtypeStruct(shape, BF) for shape in shapes],
        cost_estimate=pl.CostEstimate(flops=10**8, bytes_accessed=3 * 10**6, transcendentals=0),
        name="pack_weights",
    )(xi[None].astype(jnp.int32), in_w, dt_w)


def pair_kernel(at_ref, keep_ref, got_ref, send_ref, stay_ref):
    rows = keep_ref.shape[1]
    mine = pl.ds(pl.multiple_of(at_ref[0] * rows, rows), rows)
    other = pl.ds(pl.multiple_of((1 - at_ref[0]) * rows, rows), rows)
    for out, core in ((send_ref, 1 - at_ref[1]), (stay_ref, at_ref[1])):
        out[mine, :] = keep_ref[core]
        out[other, :] = got_ref[core]


def pair_rows(xi, ci, keep, got):
    shape = (2 * keep.shape[1], keep.shape[2])
    return pl.pallas_call(
        pair_kernel,
        in_specs=[pl.BlockSpec(memory_space=pltpu.SMEM)] + [pl.BlockSpec(memory_space=pltpu.VMEM)] * 2,
        out_specs=[pl.BlockSpec(memory_space=pltpu.VMEM)] * 2,
        out_shape=[jax.ShapeDtypeStruct(shape, BF)] * 2,
        cost_estimate=pl.CostEstimate(flops=0, bytes_accessed=2 * 10**6, transcendentals=0),
        name="pair_rows",
    )(jnp.stack([xi, ci]).astype(jnp.int32), keep, got)


def place_kernel(at_ref, stay_ref, got_ref, out_ref):
    rows = stay_ref.shape[0]
    out_ref[pl.ds(pl.multiple_of(at_ref[0] * rows, rows), rows), :] = stay_ref[...]
    out_ref[pl.ds(pl.multiple_of((1 - at_ref[0]) * rows, rows), rows), :] = got_ref[...]


def place_rows(index, stay, got):
    return pl.pallas_call(
        place_kernel,
        in_specs=[pl.BlockSpec(memory_space=pltpu.SMEM)] + [pl.BlockSpec(memory_space=pltpu.VMEM)] * 2,
        out_specs=pl.BlockSpec(memory_space=pltpu.VMEM),
        out_shape=jax.ShapeDtypeStruct((2 * stay.shape[0], stay.shape[1]), BF),
        cost_estimate=pl.CostEstimate(flops=0, bytes_accessed=2 * 10**6, transcendentals=0),
        name="place_rows",
    )(index[None].astype(jnp.int32), stay, got)


def swap_x(v):
    return lax.ppermute(v, "x", SWAP)


def swap_core(v):
    return lax.ppermute(v, "core", SWAP)


def pick(v, index, axis=0):
    return lax.dynamic_index_in_dim(v, index, axis, keepdims=False)


def joined(index, mine, other, axis):
    return jnp.where(
        index == 0,
        jnp.concatenate([mine, other], axis=axis),
        jnp.concatenate([other, mine], axis=axis),
    )


def from_slots(v):
    slots, rows, cols = v.shape
    return (
        v.reshape(slots, rows, AHEADS, cols // AHEADS)
        .transpose(1, 2, 0, 3)
        .reshape(rows, slots * cols)
    )


class Return:
    def __init__(self, block):
        self.xi, self.ci = lax.axis_index("x"), lax.axis_index("core")
        self.rows = block.shape[0] // 4
        self.halves = block.astype(BF).reshape(2, 2 * self.rows, -1)
        self.flying = swap_core(pick(self.halves, 1 - self.ci))

    def turn(self, chain):
        got = chain.take(self.flying)
        pair = joined(self.ci, pick(self.halves, self.ci)[None], got[None], 0)
        self.pair = pair.reshape(2, 2, self.rows, -1)
        self.flying = swap_x(pick(self.pair, 1 - self.xi, 1))

    def land(self, chain):
        got = chain.take(self.flying)
        own = joined(self.xi, pick(self.pair, self.xi, 1)[:, None], got[:, None], 1)
        return own.reshape(4, self.rows, -1).astype(F32)


class Chain:
    def __init__(self):
        self.last = ()

    def tie(self, value):
        return lax.optimization_barrier((value, self.last))[0]

    def mark(self, value):
        self.last = value
        return value

    def take(self, value):
        return self.mark(self.tie(value))


class Ring:
    def __init__(self):
        self.size = len(CYCLE)
        place = [CYCLE.index(i) for i in range(self.size)]
        position = jnp.asarray(place, jnp.int32)[lax.axis_index("ra")]
        cycle = jnp.asarray(CYCLE, jnp.int32)
        steps = jnp.arange(self.size, dtype=jnp.int32)
        self.order = cycle[(position + steps) % self.size]
        self.inverse = (jnp.asarray(place, jnp.int32) - position) % self.size

    def pairs(self, d):
        return [(CYCLE[i], CYCLE[(i + d) % self.size]) for i in range(self.size)]

    def right(self, v):
        return lax.ppermute(v, "ra", self.pairs(1))

    def left(self, v):
        return lax.ppermute(v, "ra", self.pairs(-1))


class Gather:
    def __init__(self, ring, block):
        self.ring = ring
        self.rights, self.lefts = [block], [block]

    def start(self):
        r, l = self.rights[-1], self.lefts[-1]
        if len(self.rights) == 4:
            half = r.shape[0] // 2
            r, l = r[:half], l[half:]
        self.flying = self.ring.right(r), self.ring.left(l)

    def land(self, chain):
        r, l = chain.take(self.flying)
        self.rights.append(r)
        self.lefts.append(l)

    def blocks(self):
        r, l = self.rights, self.lefts
        return [r[0], l[1], l[2], l[3], jnp.concatenate([r[4], l[4]], axis=0), r[3], r[2], r[1]]


class Scatter:
    def __init__(self, ring, block):
        self.ring, self.block, self.count = ring, block, 0

    def start(self):
        block, ring, k = self.block, self.ring, self.count
        self.count += 1
        if k == 0:
            far = block(4)
            half = far.shape[0] // 2
            sends = far[:half], far[half:]
        elif k == 1:
            up, down = self.next
            half = up.shape[0] // 2
            r, l = self.right.astype(F32), self.left.astype(F32)
            sends = (
                jnp.concatenate([up[:half] + r, up[half:]], axis=0),
                jnp.concatenate([down[:half], down[half:] + l], axis=0),
            )
        else:
            sends = self.next[0] + self.right.astype(F32), self.next[1] + self.left.astype(F32)
        self.flying = ring.right(sends[0].astype(BF)), ring.left(sends[1].astype(BF))
        self.next = (block(3 - k), block(5 + k)) if k < 3 else (block(0),)

    def land(self, chain):
        self.right, self.left = chain.take(self.flying)

    def total(self):
        return self.next[0] + self.right.astype(F32) + self.left.astype(F32)


def flat_index(sizes):
    index = 0
    for name, size in zip(ALL, sizes):
        index = index * size + lax.axis_index(name)
    return index


class SmallSum:
    def __init__(self, v, sizes):
        self.value = v
        self.count = int(np.prod(sizes))
        self.bits = [2, 4, 8, 16, 1]

    def start(self):
        bit = self.bits.pop(0)
        self.flying = lax.ppermute(self.value, ALL, [(i, i ^ bit) for i in range(self.count)])

    def land(self, chain):
        self.value = self.value + chain.take(self.flying)


def permute_blocks(v, order, width):
    return jnp.concatenate(
        [
            lax.dynamic_slice(v, (0, order[k] * width), (v.shape[0], width))
            for k in range(v.shape[1] // width)
        ],
        axis=1,
    )


def reordered(v, order, short, long):
    parts = [v[:, k * short : (k + 1) * short] for k in order]
    base = 4 * short
    parts += [v[:, base + k * long : base + (k + 1) * long] for k in order]
    return jnp.concatenate(parts, axis=1)


def pad_rows(v, rows=8):
    return jnp.concatenate([v, jnp.zeros((rows - v.shape[0], v.shape[1]), v.dtype)], axis=0)


def pad_cols(v, cols):
    return jnp.concatenate([v, jnp.zeros(v.shape[:-1] + (cols - v.shape[-1],), v.dtype)], axis=-1)


def gather_small(v, sizes, chain):
    count = int(np.prod(sizes))
    if count != 32:
        return lax.all_gather(v[None], ALL, axis=0, tiled=True)
    me = flat_index(sizes)
    v = v[None]
    bit = 1
    while bit < count:
        got = chain.take(lax.ppermute(v, ALL, [(i, i ^ bit) for i in range(count)]))
        v = joined((me // bit) % 2, v, got, 0)
        bit *= 2
    return v


def per_device(
    sizes, tokens_short, tokens_long, cot_short, cot_long, seq_lengths,
    norm_gain, in_w, dt_w, conv_w, conv_b, dt_bias, a_log, d_skip, gate_gain, out_w,
):
    ringed = sizes == (8, 2, 1, 2)
    short, long = tokens_short.shape[0], tokens_long.shape[0]
    base = 4 * short
    tokens = base + 4 * long
    xi, ci = lax.axis_index("x"), lax.axis_index("core")
    slot = ci * 2 + xi
    feature = D // AHEADS
    mine_cols = lambda v: pick(v.reshape(v.shape[0], AHEADS, SLOTS, -1), slot, 2).reshape(v.shape[0], -1)
    chain = Chain()

    if ringed:
        ring = Ring()
        order, inverse = ring.order, ring.inverse
        from_ring = lambda v: permute_blocks(v, inverse, feature)
    else:
        order = jnp.arange(AHEADS, dtype=jnp.int32)
        from_ring = lambda v: v

    width = conv_w.shape[1]
    pieces = [conv_w.reshape(-1), conv_b, norm_gain, gate_gain]
    ends = np.cumsum([0] + [p.shape[0] for p in pieces])
    small = jnp.concatenate(pieces)
    half = long // 2

    part = long // 4
    long_parts = [tokens_long[k * part : (k + 1) * part] for k in range(4)]
    if ringed:
        x_send, x_keep, z_send, z_keep = chain.mark(pack_weights(xi, in_w, dt_w))
        x_got = swap_x(x_send)
        c_s, c_l = swap_core(chain.tie(tokens_short)), swap_core(chain.tie(tokens_long))
        send, stay = chain.mark(pair_rows(xi, ci, x_keep, chain.take(x_got)))
        got = swap_core(send)
        t_s = swap_x(chain.tie(tokens_short))
        gather_x = Gather(ring, chain.mark(place_rows(ci, stay, chain.take(got))))
        gather_x.start()
        pieces_l = [swap_x(chain.tie(long_parts[0]))]
    else:
        c_s, c_l = swap_core(tokens_short), swap_core(tokens_long)
        t_s = swap_x(tokens_short)
        pieces_l = [swap_x(v) for v in long_parts]

    small = chain.mark(gather_small(small, sizes, chain))
    norm_full = chain.mark(pad_rows(small[:, ends[2] : ends[3]].reshape(1, -1).astype(F32)))

    xh = ()

    def norm(values, row):
        nonlocal xh
        xh = (chain.mark(norm_tokens(order, values, norm_full, row, tokens, xh)),)

    t_s = chain.take(t_s)
    cx_s = swap_core(t_s)
    if ringed:
        pieces_l.append(swap_x(chain.tie(long_parts[1])))
        gather_x.land(chain)
        gather_x.start()
    norm([chain.tie(tokens_short)], 0)
    norm([chain.take(c_s)], 2 * short)
    norm([chain.tie(tokens_long)], base)
    if ringed:
        pieces_l[0] = chain.take(pieces_l[0])
        pieces_l.append(swap_x(chain.tie(long_parts[2])))
        gather_x.land(chain)
        gather_x.start()
    norm([chain.take(c_l)], base + 2 * long)
    norm([t_s], short)
    if ringed:
        pieces_l[1] = chain.take(pieces_l[1])
        pieces_l.append(swap_x(chain.tie(long_parts[3])))
        gather_x.land(chain)
        gather_x.start()
    pieces_c = [swap_core(pieces_l[0]), swap_core(pieces_l[1])]
    norm([chain.take(cx_s)], 3 * short)
    norm(pieces_l[:2], base + long)
    if ringed:
        gather_o = Gather(ring, chain.tie(out_w))
        gather_o.start()
        pieces_l[2] = chain.take(pieces_l[2])
        z_got = swap_x(chain.tie(z_send))
        gather_x.land(chain)
    pieces_c = chain.take(pieces_c)
    norm(pieces_c, base + 3 * long)

    small, dt_bias, a_log, d_skip, cot_s, cot_l = chain.mark(
        chain.tie((small, dt_bias, a_log, d_skip, cot_short, cot_long))
    )
    live_s = (jnp.arange(short) < seq_lengths[0, 0]).astype(F32)[:, None]
    live_l = (jnp.arange(long) < seq_lengths[1, 0]).astype(F32)[:, None]
    dv_s, dv_l = (live_s * cot_s).astype(BF), (live_l * cot_l).astype(BF)
    taps = small[:, : ends[2]].reshape(-1, KERNEL + 1, width)
    taps = taps.transpose(1, 0, 2).reshape(KERNEL + 1, -1).astype(F32)
    taps = jnp.concatenate([mine_cols(taps[:, :DI]), taps[:, DI:]], axis=1)
    conv_taps, conv_bias = pad_rows(taps[:KERNEL]), pad_rows(taps[KERNEL:])
    gate_mine = pad_rows(mine_cols(small[:, ends[3] :].reshape(1, -1).astype(F32)))
    neg_rate = -jnp.exp(a_log.astype(F32))
    heads = pad_rows(pad_cols(mine_cols(jnp.stack([dt_bias.astype(F32), neg_rate])), 128))
    skip = pad_rows(jnp.repeat(mine_cols(d_skip.astype(F32)[None]), HEAD_DIM, axis=1))
    head_rows = np.arange(128)[:, None]
    seg = jnp.asarray(
        (head_rows < 2 * LOCAL_HEADS) & (head_rows % LOCAL_HEADS == np.arange(WIDTH)[None, :] // HEAD_DIM), BF
    )
    spread = jnp.asarray(
        (head_rows < 3 * LOCAL_HEADS)
        & (head_rows % LOCAL_HEADS == np.arange(128 * LOCAL_HEADS)[None, :] // 128),
        BF,
    )
    seq_params = (conv_taps, conv_bias, heads, skip, seg, spread)

    pieces_l[3] = chain.take(pieces_l[3])
    pieces_c = [swap_core(pieces_l[2]), swap_core(pieces_l[3])]
    if ringed:
        w_x = chain.mark(jnp.concatenate(gather_x.blocks(), axis=0))
        gather_o.land(chain)
        gather_o.start()
    norm(pieces_l[2:], base + long + 2 * part)
    norm(chain.take(pieces_c), base + 3 * long + 2 * part)
    xh = xh[0]
    if ringed:
        send, stay = chain.mark(pair_rows(xi, ci, z_keep, chain.take(z_got)))
        dvx_s, dvx_a, dvx_b = swap_x(chain.tie(dv_s)), swap_x(chain.tie(dv_l[:half])), swap_x(chain.tie(dv_l[half:]))
        dvc_s, dvc_l = swap_core(chain.tie(dv_s)), swap_core(chain.tie(dv_l))
        got = chain.take(swap_core(send))
        gather_z = Gather(ring, chain.mark(place_rows(ci, stay, got)))
        gather_z.start()
        proj = chain.mark(nn(chain.tie(xh), w_x))
        for gather in (gather_o, gather_z):
            gather.land(chain)
            gather.start()
        dvx_s = chain.take(dvx_s)
        kept = chain.mark(ssd_forward((0, 1, 2), chain.tie(proj), *seq_params))
        for gather in (gather_o, gather_z):
            gather.land(chain)
            gather.start()
        dvx_a, dvx_b = chain.take(dvx_a), chain.take(dvx_b)
        dvcx_s, dvcx_a, dvcx_b = swap_core(dvx_s), swap_core(dvx_a), swap_core(dvx_b)
        y, act, slope, states = chain.mark(ssd_forward((3, 4), chain.tie(proj), *seq_params, earlier=kept))
        gather_o.land(chain)
        gather_z.land(chain)
        gather_z.start()
        w_o = chain.mark(jnp.concatenate(gather_o.blocks(), axis=0))
        dvcx_s, dvcx_a, dvcx_b, dvc_s, dvc_l = chain.take((dvcx_s, dvcx_a, dvcx_b, dvc_s, dvc_l))
        dv = chain.mark(
            jnp.concatenate([dv_s, dvx_s, dvc_s, dvcx_s, dv_l, dvx_a, dvx_b, dvc_l, dvcx_a, dvcx_b], axis=0)
        )
        dn = chain.mark(nt(dv, w_o).astype(BF))
        gather_z.land(chain)
        w_z = chain.mark(jnp.concatenate(gather_z.blocks(), axis=0))
        z = chain.mark(nn(chain.tie(xh), w_z).astype(BF))
    else:
        full = lax.all_gather(in_w, ALL, axis=0, tiled=True)
        full_dt = lax.all_gather(dt_w, ALL, axis=0, tiled=True)
        full_out = lax.all_gather(out_w, ALL, axis=0, tiled=True)
        w_z = mine_cols(full[:, :DI])
        w_x = jnp.concatenate(
            [mine_cols(full[:, DI : 2 * DI]), full[:, 2 * DI :], pad_cols(mine_cols(full_dt), 128)], axis=-1
        )
        w_o = pick(full_out.reshape(AHEADS, SLOTS, 128, D), slot, 1).reshape(WIDTH, D)
        dvx_s, dvx_l = swap_x(dv_s), swap_x(dv_l)
        dv = jnp.concatenate(
            [dv_s, dvx_s, swap_core(dv_s), swap_core(dvx_s), dv_l, dvx_l, swap_core(dv_l), swap_core(dvx_l)], axis=0
        )
        proj = nn(xh, w_x)
        y, act, slope, states = ssd_forward((0, 1, 2, 3, 4), proj, *seq_params)
        dn = nt(dv, w_o).astype(BF)
        z = nn(xh, w_z).astype(BF)

    st = chain.mark(gate_stats(order, y, chain.tie(z), dn, gate_mine))
    st = st + reordered(swap_core(st), (2, 3, 0, 1), short, long)
    st = st + reordered(swap_x(st), (1, 0, 3, 2), short, long)
    n, dy, dz = chain.mark(gate_backward(order, st, y, z, dn, gate_mine))

    far_s, far_l = slice(2 * short, base), slice(base + 2 * long, tokens)
    mid_s, mid_l = slice(short, 2 * short), slice(base + long, base + 2 * long)
    own_s, own_l = slice(0, short), slice(base, base + long)

    def send_far(product):
        values = chain.mark((product(far_s).astype(BF), product(far_l).astype(BF)))
        return swap_core(values[0]), swap_core(values[1])

    def send_mid(product, far):
        values = chain.mark(
            (
                (product(mid_s) + far[0][short:].astype(F32)).astype(BF),
                (product(mid_l) + far[1][long:].astype(F32)).astype(BF),
            )
        )
        return swap_x(values[0]), swap_x(values[1])

    def own_product(product):
        return chain.mark((product(own_s), product(own_l)))

    def with_own(own, far, mid):
        return (
            own[0] + far[0][:short].astype(F32) + mid[0].astype(F32),
            own[1] + far[1][:long].astype(F32) + mid[1].astype(F32),
        )

    def finish(product, far, mid):
        return with_own(own_product(product), far, mid)

    here = (jnp.arange(SLOTS) == slot).astype(F32)
    spread_cols = lambda v: (v.reshape(v.shape[0], AHEADS, 1, -1) * here[:, None]).reshape(v.shape[0], -1)

    def small_terms(acc, hacc):
        conv_part = jnp.concatenate([spread_cols(acc[:5, :WIDTH]), acc[:5, WIDTH:]], axis=1)
        skip_part = jnp.sum(acc[5, :WIDTH].reshape(LOCAL_HEADS, HEAD_DIM), axis=1)
        head_part = spread_cols(jnp.stack([hacc[0, :LOCAL_HEADS], hacc[1, :LOCAL_HEADS], skip_part]))
        return jnp.concatenate([conv_part.reshape(-1), head_part.reshape(-1)])

    def backward_call(steps, earlier):
        return chain.mark(
            ssd_backward(steps, chain.tie(proj), act, slope, dy, states, *seq_params, earlier=earlier)
        )

    def branch_product(part):
        return nn(chain.tie(n)[part], w_o)

    def unit_product(dx):
        return lambda part: nt(chain.tie(dx)[part], w_x) + nt(dz[part], w_z)

    g_out = chain.mark(tn(n, dv))
    if ringed:
        blocks_o = g_out.reshape(AHEADS, -1, D)
        scatter_o = Scatter(ring, lambda k: blocks_o[k])
        scatter_o.start()
        g_z = chain.mark(tn(chain.tie(xh), dz))
        blocks_z = g_z.reshape(AHEADS, -1, WIDTH)
        scatter_z = Scatter(ring, lambda k: blocks_z[k])
        scatter_z.start()
        scatter_o.land(chain)
        scatter_o.start()
        far_v = send_far(branch_product)
        scatter_z.land(chain)
        scatter_z.start()
        far_v = chain.take(far_v)
        mid_v = send_mid(branch_product, far_v)
        for scatter in (scatter_o, scatter_z):
            scatter.land(chain)
            scatter.start()
        dx, acc, hacc = backward_call((0, 3), ())
        for scatter in (scatter_o, scatter_z):
            scatter.land(chain)
            scatter.start()
        dx, acc2, hacc2 = backward_call((4,), (dx,))
        acc, hacc = acc + acc2, hacc + hacc2
        far_u = send_far(unit_product(dx))
        for scatter in (scatter_o, scatter_z):
            scatter.land(chain)
        own_out = chain.mark(scatter_o.total())
        back_z = Return(chain.mark(scatter_z.total()))
        mid_v = chain.take(mid_v)
        v_s, v_l = finish(branch_product, far_v, mid_v)
        back_z.turn(chain)
        dx, acc2, hacc2 = backward_call((2,), (chain.tie(dx),))
        acc, hacc = acc + acc2, hacc + hacc2
        far_u = chain.take(far_u)
        own_z = chain.mark(back_z.land(chain))
        mid_u = send_mid(unit_product(dx), far_u)
        dx, acc2, hacc2 = backward_call((1,), (chain.tie(dx),))
        acc, hacc = acc + acc2, hacc + hacc2
        scatter_x = Scatter(
            ring, lambda k: chain.mark(tn(xh[:, k * feature : (k + 1) * feature], chain.tie(dx)))
        )
        scatter_x.start()
        tally = SmallSum(small_terms(acc, hacc), sizes)
        tally.start()
        scatter_x.land(chain)
        scatter_x.start()
        tally.land(chain)
        tally.start()
        du_own = own_product(unit_product(dx))
        scatter_x.land(chain)
        scatter_x.start()
        tally.land(chain)
        tally.start()
        scatter_x.land(chain)
        scatter_x.start()
        tally.land(chain)
        tally.start()
        scatter_x.land(chain)
        back_x = Return(chain.mark(scatter_x.total()))
        tally.land(chain)
        tally.start()
        mid_u = chain.take(mid_u)
        du_s, du_l = chain.mark(with_own(du_own, far_u, mid_u))
        back_x.turn(chain)
        tally.land(chain)
        total = tally.value
    else:
        g_z = tn(xh, dz)
        far_v = send_far(branch_product)
        mid_v = send_mid(branch_product, far_v)
        v_s, v_l = finish(branch_product, far_v, mid_v)
        dx, acc, hacc = backward_call((0, 3, 4, 2, 1), ())
        far_u = send_far(unit_product(dx))
        mid_u = send_mid(unit_product(dx), far_u)
        du_s, du_l = finish(unit_product(dx), far_u, mid_u)
        g_x = tn(xh, dx)
        total = lax.psum(small_terms(acc, hacc), ALL)

    out_short = (tokens_short.astype(F32) + live_s * v_s).astype(BF)
    out_long = (tokens_long.astype(F32) + live_l * v_l).astype(BF)

    def token_grad(token, cot, d_u):
        residual = token.astype(F32)
        row_scale = lax.rsqrt(jnp.mean(residual * residual, axis=-1, keepdims=True) + EPS)
        unit = residual * row_scale
        d_norm = from_ring(d_u) * norm_full[0:1]
        return cot.astype(F32) + row_scale * (d_norm - unit * jnp.mean(d_norm * unit, axis=-1, keepdims=True))

    grad_short = token_grad(tokens_short, cot_short, du_s)
    grad_long = token_grad(tokens_long, cot_long, du_l)

    if ringed:
        own_x = back_x.land(chain)
        grad_in_w = jnp.concatenate(
            [
                from_slots(own_z),
                from_slots(own_x[:, :, :WIDTH]),
                jnp.sum(own_x[:, :, WIDTH:XBC], axis=0),
            ],
            axis=1,
        )
        grad_dt_w = from_slots(own_x[:, :, XBC : XBC + LOCAL_HEADS])
    else:
        here = (jnp.arange(SLOTS) == slot).astype(F32)
        widen = lambda v: (v.reshape(D, AHEADS, 1, -1) * here[:, None]).reshape(D, -1)
        reduce = lambda v: lax.psum_scatter(v, ALL, scatter_dimension=0, tiled=True)
        grad_in_w = reduce(
            jnp.concatenate([widen(g_z), widen(g_x[:, :WIDTH]), g_x[:, WIDTH:XBC]], axis=1)
        )
        grad_dt_w = reduce(widen(g_x[:, XBC : XBC + LOCAL_HEADS]))
        own_out = reduce((g_out.reshape(AHEADS, 1, 128, D) * here[:, None, None]).reshape(DI, D))

    grad_norm_gain = (
        jnp.sum(in_w.astype(F32) * grad_in_w, axis=1) + jnp.sum(dt_w.astype(F32) * grad_dt_w, axis=1)
    ) / norm_gain.astype(F32)
    grad_gate_gain = jnp.sum(out_w.astype(F32) * own_out, axis=1) / gate_gain.astype(F32)

    conv_total = total[: 5 * (DI + 2 * STATE)].reshape(5, -1)
    head_total = total[5 * (DI + 2 * STATE) :].reshape(3, HEADS)
    own_conv = lax.dynamic_slice(conv_total, (0, flat_index(sizes) * width), (5, width))
    return (
        out_short,
        out_long,
        grad_short,
        grad_long,
        grad_norm_gain,
        grad_in_w,
        grad_dt_w,
        own_conv[:KERNEL],
        own_conv[KERNEL],
        head_total[0],
        head_total[1] * neg_rate,
        head_total[2],
        grad_gate_gain,
        own_out,
    )


def solution(mesh):
    wide, narrow = mesh.shape["wide"], mesh.shape["narrow"]
    sizes = (wide // 2, 2, narrow // 2, 2)
    split = Mesh(mesh.devices.reshape(sizes), ALL)
    rows, vector, columns = P(ALL, None), P(ALL), P(None, ALL)
    return jax.shard_map(
        functools.partial(per_device, sizes),
        mesh=split,
        in_specs=(
            rows, rows, rows, rows, columns, vector, rows, rows, columns, vector, P(), P(), P(), vector, rows,
        ),
        out_specs=(
            rows, rows, rows, rows, vector, rows, rows, columns, vector, P(), P(), P(), vector, rows,
        ),
        check_vma=False,
    )
```

time: 2580 us -> 807 us (0.31)
  waiting for transfers between devices: 1350 us -> 109 us
  matrix products: 546 us -> 205 us
  blocking collectives: 289 us -> 0 us
  Pallas kernels: 0 us -> 250 us
  other arithmetic: 182 us -> 53.4 us
  local copies, waits for them, and re-layouts: 177 us -> 86.3 us
  starting transfers between devices: 0.65 us -> 85.2 us
    reduce_scatter x3 -> x0, waiting for transfers between devices: 1330 us -> none  [the longest x1 705 us: reduce_grads(): lax.psum_scatter(out_total, ('wide', 'narrow'), scatter_dimension=0, tile...]
    dot_general x64 -> x31, matrix products: 546 us -> 205 us  [the longest x13 77 us: nt(): lax.dot_general(a, b, (((1,), (1,)), ((), ())), preferred_element_type=F32)]
    pallas_call x0 -> x23, Pallas kernels: none -> 250 us  [the longest x4 106 us: ssd_backward(): pl.pallas_call(bwd_kernel, grid_spec=pltpu.PrefetchScalarGridSpec(num_sca...]
    all_gather x3 -> x0, blocking collectives: 204 us -> none  [the longest x1 71.5 us: forward_pass(): lax.all_gather(dt_w, ('wide', 'narrow'), axis=0, tiled=True)]
    ppermute x0 -> x96, waiting for transfers between devices: none -> 109 us  [the longest x24 31.6 us: right(): return lax.ppermute(v, 'ra', self.pairs(1))]
    reshape x10, local copies, waits for them, and re-layouts: 90.1 us -> 3.58 us  [the longest x4 2.56 us: from_slots(): return v.reshape(slots, rows, AHEADS, cols // AHEADS).transpose(1, 2, 0,...]
    ppermute x0 -> x96, starting transfers between devices: none -> 85.2 us  [the longest x24 33 us: left(): return lax.ppermute(v, 'ra', self.pairs(-1))]
    unnamed x2 -> x0, blocking collectives: 84.2 us -> none
  transfers between devices with their start and end apart: 6 -> 96, of which waited for: 4 -> 29; matrix products, arithmetic and copies ran while one was open for 11% -> 31% of each run, Pallas kernels for 0% -> 27%
where the time goes in v1:
time: 807 us; the launch traced here: 797 us
  Pallas kernels  250 us (31%)
  matrix products  205 us (25%)
  waiting for transfers between devices  109 us (14%)
  local copies, waits for them, and re-layouts  86.3 us (11%)
  starting transfers between devices  85.2 us (11%)
  other arithmetic  53.4 us (7%)
  between operations  8.09 us (1%)
    pallas_call x4, Pallas kernels, ssd_backward(): pl.pallas_call(bwd_kernel, grid_spec=pltpu.PrefetchScalarGridSpec(num_sca...  106 us
    dot_general x13, matrix products, nt(): lax.dot_general(a, b, (((1,), (1,)), ((), ())), preferred_element_type=F32)  77 us
    pallas_call x2, Pallas kernels, ssd_forward(): pl.pallas_call(fwd_kernel, grid_spec=pltpu.PrefetchScalarGridSpec(num_sca...  65.8 us
    dot_general x10, matrix products, tn(): lax.dot_general(a, b, (((0,), (0,)), ((), ())), preferred_element_type=F32)  64.4 us
    dot_general x8, matrix products, nn(): lax.dot_general(a, b, (((1,), (0,)), ((), ())), preferred_element_type=F32)  63.8 us
    unnamed x271, local copies, waits for them, and re-layouts  53.3 us
    pallas_call x10, Pallas kernels, norm_tokens(): pl.pallas_call(functools.partial(norm_kernel, count), grid_spec=pltpu.Pre...  35.5 us
    ppermute x24, starting transfers between devices, left(): return lax.ppermute(v, 'ra', self.pairs(-1))  33 us
  transfers between devices with their start and end apart: 96, of which 29 were waited for; matrix products, arithmetic and copies ran while one was open for 31% of the time, Pallas kernels for 27%

profile of v1, /device:TPU:0, one launch (start us, length us, event | category | flops | bytes accessed | tf_op | source)
XLA Modules:
  0.0 796.8 jit_solution(16095208366554026099)
XLA Ops:
  34.6 15.8 %collective-permute-done.11 = bf16[16,872]{1,0:T(8,128)(2,1)S(1)} collective-permute-done((bf16[16,872]{1,0:T(8,128)(2,1)S(1)}, bf16[16,872]{1,0:T(8,128)(2,1)S(1)}, u32[]{:S(2)}, u32[]{:S(2)}) %collective-permute-start.11) | collective-permute-done | bytes 27936 | tf_op jit(solution)/shard_map/ppermute | solution.py:878
  53.3 7.9 collective-permute-done.6.refs_0_
  156.6 22.1 %fusion.104.p_ref = f32[2560,1408]{1,0:T(8,128)} fusion(bf16[2560,2048]{1,0:T(8,128)(2,1)} %norm_tokens.19, bf16[2048,1408]{1,0:T(8,128)(2,1)} %constant_dynamic-update-slice_fusion), kind=kOutput, calls=%fused_computation.287 | convolution fusion | flops 14763950080 | bytes 30670848 | tf_op jit(solution)/shard_map/dot_general | solution.py:42
  185.4 39.8 %ssd_forward.2 = (bf16[2560,1024]{1,0:T(8,128)(2,1)}, bf16[2560,1280]{1,0:T(8,128)(2,1)}, bf16[2560,1280]{1,0:T(8,128)(2,1)}, f32[5,128,1024]{2,1,0:T(8,128)}) custom-call(s32[3]{0:T(128)} %call_exported.0.steps_ref, f32[2560,1408]{1,0:T(8,128)} %fusion.104.p_ref, f32[8,1280]{1,0:T(8,128)} %concatenate.170.cw_ref, f32[8,1280]{1,0:T(8,128)} %select_maximum_fusion.cb_ref, ...), custom_call_target="tpu_custom_call" | custom-call | flops 12000000000 | bytes 18000000 | tf_op jit(solution)/shard_map/ssd_forward/pallas_call | solution.py:481
  239.9 26.1 %ssd_forward.3 = (bf16[2560,1024]{1,0:T(8,128)(2,1)}, bf16[2560,1280]{1,0:T(8,128)(2,1)}, bf16[2560,1280]{1,0:T(8,128)(2,1)}, f32[5,128,1024]{2,1,0:T(8,128)}) custom-call(s32[2]{0:T(128)} %constant.217.clone.steps_ref, f32[2560,1408]{1,0:T(8,128)} %fusion.104.p_ref, ...), custom_call_target="tpu_custom_call", output_to_operand_aliasing={{0}: (8, {}), {1}: (9, {}), {2}: (10, {}), {3}: (11, {})} | custom-call | flops 8000000000 | bytes 12000000 | tf_op jit(solution)/shard_map/ssd_forward/pallas_call | solution.py:481
  270.1 10.1 %collective-permute-done.42 = bf16[256,1024]{1,0:T(8,128)(2,1)S(1)} collective-permute-done((bf16[256,1024]{1,0:T(8,128)(2,1)}, bf16[256,1024]{1,0:T(8,128)(2,1)S(1)}, u32[]{:S(2)}, u32[]{:S(2)}) %collective-permute-start.42) | collective-permute-done | bytes 524320 | tf_op jit(solution)/shard_map/ppermute | solution.py:765
  304.3 15.4 %convolution_convert_fusion.1.dn_ref = bf16[2560,1024]{1,0:T(8,128)(2,1)} fusion(bf16[2560,2048]{1,0:T(8,128)(2,1)} %constant_dynamic-update-slice_fusion.18, bf16[1024,2048]{1,0:T(8,128)(2,1)S(1)} %constant_dynamic-update-slice_fusion.9), kind=kOutput, calls=%fused_computation.6 | convolution fusion | flops 10740039680 | bytes 19922944 | tf_op jit(solution)/shard_map/dot_general | solution.py:38
  325.7 14.9 %convolution_convert_fusion.z_ref = bf16[2560,1024]{1,0:T(8,128)(2,1)} fusion(bf16[2560,2048]{1,0:T(8,128)(2,1)S(1)} %bitcast.117, bf16[2048,1024]{1,0:T(8,128)(2,1)} %constant_dynamic-update-slice_fusion.28), kind=kOutput, calls=%fused_computation.5 | convolution fusion | flops 10740039680 | bytes 19922944 | tf_op jit(solution)/shard_map/dot_general | solution.py:42
  340.6 13.3 %gate_stats.1 = f32[8,2560]{1,0:T(8,128)} custom-call(s32[8]{0:T(128)} %gather_fusion, bf16[2560,1024]{1,0:T(8,128)(2,1)} %get-tuple-element.262.y_ref, bf16[2560,1024]{1,0:T(8,128)(2,1)} %convolution_convert_fusion.z_ref, bf16[2560,1024]{1,0:T(8,128)(2,1)} %convolution_convert_fusion.1.dn_ref, f32[8,1024]{1,0:T(8,128)} %concatenate.178.gain_ref), custom_call_target="tpu_custom_call" | custom-call | flops 3000000000 | bytes 16000000 | tf_op jit(solution)/shard_map/gate_stats/pallas_call | solution.py:564
  361.6 18.1 %gate_backward.1 = (bf16[2560,1024]{1,0:T(8,128)(2,1)}, bf16[2560,1024]{1,0:T(8,128)(2,1)}, bf16[2560,1024]{1,0:T(8,128)(2,1)}) custom-call(s32[8]{0:T(128)} %gather_fusion, f32[8,2560]{1,0:T(8,128)} %add.377.st_ref, bf16[2560,1024]{1,0:T(8,128)(2,1)} %get-tuple-element.262.y_ref, bf16[2560,1024]{1,0:T(8,128)(2,1)} %convolution_convert_fusion.z_ref, ...), custom_call_target="tpu_custom_call" | custom-call | flops 6000000000 | bytes 32000000 | tf_op jit(solution)/shard_map/gate_backward/pallas_call | solution.py:583
  379.8 17.2 %fusion.103 = (bf16[1024,2048]{1,0:T(8,128)(2,1)}, f32[1024,2048]{1,0:T(8,128)S(1)}) fusion(bf16[2560,1024]{1,0:T(8,128)(2,1)} %get-tuple-element.315, bf16[2560,2048]{1,0:T(8,128)(2,1)} %constant_dynamic-update-slice_fusion.18), kind=kOutput, calls=%fused_computation.286 | convolution fusion | flops 10739515392 | bytes 28311552 | tf_op jit(solution)/shard_map/dot_general | solution.py:46
  401.1 15.7 %fusion.102 = (bf16[2048,1024]{1,0:T(8,128)(2,1)}, f32[2048,1024]{1,0:T(8,128)}) fusion(bf16[2560,2048]{1,0:T(8,128)(2,1)S(1)} %bitcast.119, bf16[2560,1024]{1,0:T(8,128)(2,1)} %get-tuple-element.282), kind=kOutput, calls=%fused_computation.285 | convolution fusion | flops 10739515392 | bytes 28311552 | tf_op jit(solution)/shard_map/dot_general | solution.py:46
  426.5 7.7 convolution_convert_fusion.2
  446.4 6.8 fusion.13
  473.2 8.2 %collective-permute-done.64 = bf16[256,1024]{1,0:T(8,128)(2,1)S(1)} collective-permute-done((bf16[256,1024]{1,0:T(8,128)(2,1)S(1)}, bf16[256,1024]{1,0:T(8,128)(2,1)S(1)}, u32[]{:S(2)}, u32[]{:S(2)}) %collective-permute-start.64) | collective-permute-done | bytes 524320 | tf_op jit(solution)/shard_map/ppermute | solution.py:768
  490.3 40.9 %ssd_backward.4 = (bf16[2560,1408]{1,0:T(8,128)(2,1)}, f32[8,1280]{1,0:T(8,128)}, f32[8,128]{1,0:T(8,128)}) custom-call(s32[2]{0:T(128)} %iota_multiply_fusion.steps_ref, f32[2560,1408]{1,0:T(8,128)} %fusion.104.p_ref, bf16[2560,1280]{1,0:T(8,128)(2,1)} %get-tuple-element.263.act_ref, bf16[2560,1280]{1,0:T(8,128)(2,1)} %get-tuple-element.264.slope_ref, ...), custom_call_target="tpu_custom_call" | custom-call | flops 20000000000 | bytes 18000000 | tf_op jit(solution)/shard_map/ssd_backward/pallas_call | solution.py:518
  532.2 21.9 %ssd_backward.5 = (bf16[2560,1408]{1,0:T(8,128)(2,1)}, f32[8,1280]{1,0:T(8,128)}, f32[8,128]{1,0:T(8,128)}) custom-call(s32[1]{0:T(128)} %constant.219.clone.steps_ref, f32[2560,1408]{1,0:T(8,128)} %fusion.104.p_ref, bf16[2560,1280]{1,0:T(8,128)(2,1)} %get-tuple-element.263.act_ref, ...), custom_call_target="tpu_custom_call", output_to_operand_aliasing={{0}: (11, {})} | custom-call | flops 10000000000 | bytes 9000000 | tf_op jit(solution)/shard_map/ssd_backward/pallas_call | solution.py:518
  554.2 11.4 %add_convert_fusion = bf16[1024,2048]{1,0:T(8,128)(2,1)} fusion(f32[1024,2048]{1,0:T(8,128)} %fusion.13, bf16[2048,1408]{1,0:T(8,128)(2,1)S(1)} %bitcast.123, bf16[2560,1408]{1,0:T(8,128)(2,1)} %get-tuple-element.318.refs_0_), kind=kOutput, calls=%fused_computation.1 | convolution fusion | flops 5909774336 | bytes 21233664 | tf_op jit(solution)/shard_map/dot_general | solution.py:38
  609.1 21.8 %ssd_backward.6 = (bf16[2560,1408]{1,0:T(8,128)(2,1)}, f32[8,1280]{1,0:T(8,128)}, f32[8,128]{1,0:T(8,128)}) custom-call(s32[1]{0:T(128)} %constant.220.clone.steps_ref, f32[2560,1408]{1,0:T(8,128)} %fusion.104.p_ref, bf16[2560,1280]{1,0:T(8,128)(2,1)} %get-tuple-element.263.act_ref, ...), custom_call_target="tpu_custom_call", output_to_operand_aliasing={{0}: (11, {})} | custom-call | flops 10000000000 | bytes 9000000 | tf_op jit(solution)/shard_map/ssd_backward/pallas_call | solution.py:518
  630.9 7.3 add_convert_fusion.1
  642.0 21.8 %ssd_backward.7 = (bf16[2560,1408]{1,0:T(8,128)(2,1)}, f32[8,1280]{1,0:T(8,128)}, f32[8,128]{1,0:T(8,128)}) custom-call(s32[1]{0:T(128)} %constant.221.clone.steps_ref, f32[2560,1408]{1,0:T(8,128)} %fusion.104.p_ref, bf16[2560,1280]{1,0:T(8,128)(2,1)} %get-tuple-element.263.act_ref, ...), custom_call_target="tpu_custom_call", output_to_operand_aliasing={{0}: (11, {})} | custom-call | flops 10000000000 | bytes 9000000 | tf_op jit(solution)/shard_map/ssd_backward/pallas_call | solution.py:518
  704.3 6.6 convolution_add_fusion
  725.9 9.1 %collective-permute-done.88 = bf16[256,1408]{1,0:T(8,128)(2,1)S(1)} collective-permute-done((bf16[256,1408]{1,0:T(8,128)(2,1)S(1)}, bf16[256,1408]{1,0:T(8,128)(2,1)S(1)}, u32[]{:S(2)}, u32[]{:S(2)}) %collective-permute-start.88) | collective-permute-done | bytes 720928 | tf_op jit(solution)/shard_map/ppermute | solution.py:768
  748.0 6.8 collective-permute-done.86
  (667 shorter events, 401.8 us)
Async XLA Ops:
  7.9 69.2 %collective-permute-start.3 = (bf16[128,2048]{1,0:T(8,128)(2,1)}, bf16[128,2048]{1,0:T(8,128)(2,1)}, u32[]{:S(2)}, u32[]{:S(2)}) collective-permute-start(bf16[128,2048]{1,0:T(8,128)(2,1)} %refs_0_), channel_id=1, source_target_pairs={{0,2},{2,0},{1,3},{3,1},{4,6},{6,4},{5,7},{7,5},{8,10},{10,8},{9,1... | collective-permute-start | bytes 1572872 | tf_op jit(solution)/shard_map/ppermute | solution.py:693
  7.9 81.8 %collective-permute-start.14 = (bf16[512,2048]{1,0:T(8,128)(2,1)}, bf16[512,2048]{1,0:T(8,128)(2,1)}, u32[]{:S(2)}, u32[]{:S(2)}) collective-permute-start(bf16[512,2048]{1,0:T(8,128)(2,1)} %refs_0_.1), channel_id=1, source_target_pairs={{0,2},{2,0},{1,3},{3,1},{4,6},{6,4},{5,7},{7,5},{8,10},{10,8},{9,1... | collective-permute-start | bytes 6291464 | tf_op jit(solution)/shard_map/ppermute | solution.py:693
  150.7 34.1 %collective-permute-start.41 = (bf16[128,2048]{1,0:T(8,128)(2,1)S(1)}, bf16[128,2048]{1,0:T(8,128)(2,1)}, u32[]{:S(2)}, u32[]{:S(2)}) collective-permute-start(bf16[128,2048]{1,0:T(8,128)(2,1)S(1)} %copy-done.47), channel_id=1, source_target_pairs={{0,1},{1,0},{2,3},{3,2},{4,5},{5,4},{6,7},{7,6},{8,9},{9,8},{10,11... | collective-permute-start | bytes 1572872 | tf_op jit(solution)/shard_map/ppermute | solution.py:689
  178.7 60.7 %collective-permute-start.30 = (bf16[256,2048]{1,0:T(8,128)(2,1)}, bf16[256,2048]{1,0:T(8,128)(2,1)}, u32[]{:S(2)}, u32[]{:S(2)}) collective-permute-start(bf16[256,2048]{1,0:T(8,128)(2,1)} %get-tuple-element.240), channel_id=1, source_target_pairs={{0,1},{1,0},{2,3},{3,2},{4,5},{5,4},{6,7},{7,6},{8,9},{9,8},{10,11... | collective-permute-start | bytes 3145736 | tf_op jit(solution)/shard_map/ppermute | solution.py:689
  179.6 59.8 %collective-permute-start.29 = (bf16[256,2048]{1,0:T(8,128)(2,1)}, bf16[256,2048]{1,0:T(8,128)(2,1)}, u32[]{:S(2)}, u32[]{:S(2)}) collective-permute-start(bf16[256,2048]{1,0:T(8,128)(2,1)} %get-tuple-element.239), channel_id=1, source_target_pairs={{0,1},{1,0},{2,3},{3,2},{4,5},{5,4},{6,7},{7,6},{8,9},{9,8},{10,11... | collective-permute-start | bytes 3145736 | tf_op jit(solution)/shard_map/ppermute | solution.py:689
  182.6 46.4 %collective-permute-start.40 = (bf16[128,2048]{1,0:T(8,128)(2,1)}, bf16[128,2048]{1,0:T(8,128)(2,1)S(1)}, u32[]{:S(2)}, u32[]{:S(2)}) collective-permute-start(bf16[128,2048]{1,0:T(8,128)(2,1)} %collective-permute-done.36), channel_id=1, source_target_pairs={{0,4},{8,0},{16,8},{24,16},{28,24},{20,28},{12,20},{4,12},{1,5},{9... | collective-permute-start | bytes 1572872 | tf_op jit(solution)/shard_map/ppermute | solution.py:768
  183.5 41.6 %collective-permute-start.39 = (bf16[128,2048]{1,0:T(8,128)(2,1)}, bf16[128,2048]{1,0:T(8,128)(2,1)S(1)}, u32[]{:S(2)}, u32[]{:S(2)}) collective-permute-start(bf16[128,2048]{1,0:T(8,128)(2,1)} %collective-permute-done.35), channel_id=1, source_target_pairs={{0,8},{8,16},{16,24},{24,28},{28,20},{20,12},{12,4},{4,0},{1,9},{9... | collective-permute-start | bytes 1572872 | tf_op jit(solution)/shard_map/ppermute | solution.py:765
  184.7 47.0 %collective-permute-start.37 = (bf16[256,1024]{1,0:T(8,128)(2,1)}, bf16[256,1024]{1,0:T(8,128)(2,1)}, u32[]{:S(2)}, u32[]{:S(2)}) collective-permute-start(bf16[256,1024]{1,0:T(8,128)(2,1)} %collective-permute-done.31), channel_id=1, source_target_pairs={{0,8},{8,16},{16,24},{24,28},{28,20},{20,12},{12,4},{4,0},{1,9},{9... | collective-permute-start | bytes 1572872 | tf_op jit(solution)/shard_map/ppermute | solution.py:765
  229.0 59.1 %collective-permute-start.52 = (bf16[512,2048]{1,0:T(8,128)(2,1)}, bf16[512,2048]{1,0:T(8,128)(2,1)}, u32[]{:S(2)}, u32[]{:S(2)}) collective-permute-start(bf16[512,2048]{1,0:T(8,128)(2,1)} %copy-done.15), channel_id=1, source_target_pairs={{0,2},{2,0},{1,3},{3,1},{4,6},{6,4},{5,7},{7,5},{8,10},{10,8},{9,1... | collective-permute-start | bytes 6291464 | tf_op jit(solution)/shard_map/ppermute | solution.py:693
  231.7 34.3 %collective-permute-start.44 = (bf16[64,2048]{1,0:T(8,128)(2,1)}, bf16[64,2048]{1,0:T(8,128)(2,1)}, u32[]{:S(2)}, u32[]{:S(2)}) collective-permute-start(bf16[64,2048]{1,0:T(8,128)(2,1)} %slice.441), channel_id=1, source_target_pairs={{0,8},{8,16},{16,24},{24,28},{28,20},{20,12},{12,4},{4,0},{1,9},{9... | collective-permute-start | bytes 786440 | tf_op jit(solution)/shard_map/ppermute | solution.py:765
  239.4 48.7 %collective-permute-start.50 = (bf16[256,2048]{1,0:T(8,128)(2,1)}, bf16[256,2048]{1,0:T(8,128)(2,1)}, u32[]{:S(2)}, u32[]{:S(2)}) collective-permute-start(bf16[256,2048]{1,0:T(8,128)(2,1)} %collective-permute-done.29), channel_id=1, source_target_pairs={{0,2},{2,0},{1,3},{3,1},{4,6},{6,4},{5,7},{7,5},{8,10},{10,8},{9,1... | collective-permute-start | bytes 3145736 | tf_op jit(solution)/shard_map/ppermute | solution.py:693
  239.4 48.7 %collective-permute-start.49 = (bf16[256,2048]{1,0:T(8,128)(2,1)}, bf16[256,2048]{1,0:T(8,128)(2,1)}, u32[]{:S(2)}, u32[]{:S(2)}) collective-permute-start(bf16[256,2048]{1,0:T(8,128)(2,1)} %collective-permute-done.30), channel_id=1, source_target_pairs={{0,2},{2,0},{1,3},{3,1},{4,6},{6,4},{5,7},{7,5},{8,10},{10,8},{9,1... | collective-permute-start | bytes 3145736 | tf_op jit(solution)/shard_map/ppermute | solution.py:693
  285.7 33.9 %collective-permute-start.46 = (bf16[128,1024]{1,0:T(8,128)(2,1)S(1)}, bf16[128,1024]{1,0:T(8,128)(2,1)S(1)}, u32[]{:S(2)}, u32[]{:S(2)}) collective-permute-start(bf16[128,1024]{1,0:T(8,128)(2,1)S(1)} %slice.443), channel_id=1, source_target_pairs={{0,8},{8,16},{16,24},{24,28},{28,20},{20,12},{12,4},{4,0},{1,9},{9... | collective-permute-start | bytes 786440 | tf_op jit(solution)/shard_map/ppermute | solution.py:765
  286.6 33.0 %collective-permute-start.47 = (bf16[128,1024]{1,0:T(8,128)(2,1)S(1)}, bf16[128,1024]{1,0:T(8,128)(2,1)S(1)}, u32[]{:S(2)}, u32[]{:S(2)}) collective-permute-start(bf16[128,1024]{1,0:T(8,128)(2,1)S(1)} %slice.444), channel_id=1, source_target_pairs={{0,4},{8,0},{16,8},{24,16},{28,24},{20,28},{12,20},{4,12},{1,5},{9... | collective-permute-start | bytes 786440 | tf_op jit(solution)/shard_map/ppermute | solution.py:768
  485.4 113.2 %collective-permute-start.62 = (bf16[512,2048]{1,0:T(8,128)(2,1)}, bf16[512,2048]{1,0:T(8,128)(2,1)}, u32[]{:S(2)}, u32[]{:S(2)}) collective-permute-start(bf16[512,2048]{1,0:T(8,128)(2,1)} %add_convert_fusion.2), channel_id=1, source_target_pairs={{0,1},{1,0},{2,3},{3,2},{4,5},{5,4},{6,7},{7,6},{8,9},{9,8},{10,11... | collective-permute-start | bytes 6291464 | tf_op jit(solution)/shard_map/ppermute | solution.py:689
  486.3 45.0 %collective-permute-start.69 = (bf16[128,2048]{1,0:T(8,128)(2,1)}, bf16[128,2048]{1,0:T(8,128)(2,1)S(1)}, u32[]{:S(2)}, u32[]{:S(2)}) collective-permute-start(bf16[128,2048]{1,0:T(8,128)(2,1)} %get-tuple-element.409), channel_id=1, source_target_pairs={{0,8},{8,16},{16,24},{24,28},{28,20},{20,12},{12,4},{4,0},{1,9},{9... | collective-permute-start | bytes 1572872 | tf_op jit(solution)/shard_map/ppermute | solution.py:765
  487.1 44.1 %collective-permute-start.70 = (bf16[128,2048]{1,0:T(8,128)(2,1)}, bf16[128,2048]{1,0:T(8,128)(2,1)S(1)}, u32[]{:S(2)}, u32[]{:S(2)}) collective-permute-start(bf16[128,2048]{1,0:T(8,128)(2,1)} %get-tuple-element.408), channel_id=1, source_target_pairs={{0,4},{8,0},{16,8},{24,16},{28,24},{20,28},{12,20},{4,12},{1,5},{9... | collective-permute-start | bytes 1572872 | tf_op jit(solution)/shard_map/ppermute | solution.py:768
  488.3 43.9 %collective-permute-start.67 = (bf16[256,1024]{1,0:T(8,128)(2,1)}, bf16[256,1024]{1,0:T(8,128)(2,1)S(1)}, u32[]{:S(2)}, u32[]{:S(2)}) collective-permute-start(bf16[256,1024]{1,0:T(8,128)(2,1)} %get-tuple-element.411), channel_id=1, source_target_pairs={{0,8},{8,16},{16,24},{24,28},{28,20},{20,12},{12,4},{4,0},{1,9},{9... | collective-permute-start | bytes 1572872 | tf_op jit(solution)/shard_map/ppermute | solution.py:765
  489.2 43.1 %collective-permute-start.68 = (bf16[256,1024]{1,0:T(8,128)(2,1)}, bf16[256,1024]{1,0:T(8,128)(2,1)S(1)}, u32[]{:S(2)}, u32[]{:S(2)}) collective-permute-start(bf16[256,1024]{1,0:T(8,128)(2,1)} %get-tuple-element.410), channel_id=1, source_target_pairs={{0,4},{8,0},{16,8},{24,16},{28,24},{20,28},{12,20},{4,12},{1,5},{9... | collective-permute-start | bytes 1572872 | tf_op jit(solution)/shard_map/ppermute | solution.py:768
  565.6 65.3 %collective-permute-start.77 = (bf16[1024,2048]{1,0:T(8,128)(2,1)}, bf16[1024,2048]{1,0:T(8,128)(2,1)}, u32[]{:S(2)}, u32[]{:S(2)}) collective-permute-start(bf16[1024,2048]{1,0:T(8,128)(2,1)} %add_convert_fusion), channel_id=1, source_target_pairs={{0,2},{2,0},{1,3},{3,1},{4,6},{6,4},{5,7},{7,5},{8,10},{10,8},{9,1... | collective-permute-start | bytes 12582920 | tf_op jit(solution)/shard_map/ppermute | solution.py:693
  595.3 35.6 %collective-permute-start.76 = (bf16[256,2048]{1,0:T(8,128)(2,1)}, bf16[256,2048]{1,0:T(8,128)(2,1)S(1)}, u32[]{:S(2)}, u32[]{:S(2)}) collective-permute-start(bf16[256,2048]{1,0:T(8,128)(2,1)} %fusion.9), channel_id=1, source_target_pairs={{0,2},{2,0},{1,3},{3,1},{4,6},{6,4},{5,7},{7,5},{8,10},{10,8},{9,1... | collective-permute-start | bytes 3145736 | tf_op jit(solution)/shard_map/ppermute | solution.py:693
  607.9 68.8 %collective-permute-start.92 = (bf16[2,64,1024]{2,1,0:T(8,128)(2,1)}, bf16[2,64,1024]{2,1,0:T(8,128)(2,1)}, u32[]{:S(2)}, u32[]{:S(2)}) collective-permute-start(bf16[2,64,1024]{2,1,0:T(8,128)(2,1)} %get-tuple-element.439), channel_id=1, source_target_pairs={{0,1},{1,0},{2,3},{3,2},{4,5},{5,4},{6,7},{7,6},{8,9},{9,8},{10,11... | collective-permute-start | bytes 786440 | tf_op jit(solution)/shard_map/ppermute | solution.py:689
  674.6 85.8 %collective-permute-start.82 = (bf16[512,2048]{1,0:T(8,128)(2,1)}, bf16[512,2048]{1,0:T(8,128)(2,1)}, u32[]{:S(2)}, u32[]{:S(2)}) collective-permute-start(bf16[512,2048]{1,0:T(8,128)(2,1)} %add_convert_fusion.1), channel_id=1, source_target_pairs={{0,1},{1,0},{2,3},{3,2},{4,5},{5,4},{6,7},{7,6},{8,9},{9,8},{10,11... | collective-permute-start | bytes 6291464 | tf_op jit(solution)/shard_map/ppermute | solution.py:689
  675.6 84.9 %collective-permute-start.81 = (bf16[128,2048]{1,0:T(8,128)(2,1)}, bf16[128,2048]{1,0:T(8,128)(2,1)}, u32[]{:S(2)}, u32[]{:S(2)}) collective-permute-start(bf16[128,2048]{1,0:T(8,128)(2,1)} %fusion.11), channel_id=1, source_target_pairs={{0,1},{1,0},{2,3},{3,2},{4,5},{5,4},{6,7},{7,6},{8,9},{9,8},{10,11... | collective-permute-start | bytes 1572872 | tf_op jit(solution)/shard_map/ppermute | solution.py:689
  (177 other events, 2537.2 us)

commit v2 on v1

--- a/solution.py
+++ b/solution.py
@@ -28,7 +28,8 @@
 XCOLS = XBC + 128
 ALL = ("ra", "core", "rb", "x")
 NEG = -1e30
-TILE = 512
+TILE = 640
+HEAD = 128
 
 SWAP = [(0, 1), (1, 0)]
 CYCLE = (0, 2, 4, 6, 7, 5, 3, 1)
@@ -91,8 +92,8 @@
     return jnp.maximum(v, 0.0) + jnp.log1p(jnp.exp(-jnp.abs(v)))
 
 
-def conv_tile(p_ref, cw_ref, cb_ref, r0, seq, cols):
-    starts = (r0 & (seq - 1)) == 0
+def conv_tile(p_ref, cw_ref, cb_ref, r0, cols):
+    starts = (r0 == 0) | (r0 == HEAD)
     before = p_ref[pl.ds(pl.multiple_of(jnp.maximum(r0 - 8, 0), 8), 8), cols]
     before = jnp.where(starts, 0.0, before)
     here = p_ref[pl.ds(r0, ROWS), cols]
@@ -108,8 +109,6 @@
     steps_ref, p_ref, cw_ref, cb_ref, hp_ref, dsk_ref, seg_ref, bc_ref, *refs
 ):
     y_ref, act_ref, slope_ref, h_ref, dt_s, parts_s, grow_s, rt_s, g_s = refs[-9:]
-    first = steps_ref[pl.program_id(0)] == 0
-    seq = jnp.where(first, 128, 512)
     lane = lane_index()
 
     def conv_step(i, carry):
@@ -117,7 +116,7 @@
         rows = pl.ds(r0, ROWS)
         for c in range(XBC // 128):
             cols = slice(c * 128, c * 128 + 128)
-            conv, _ = conv_tile(p_ref, cw_ref, cb_ref, r0, seq, cols)
+            conv, _ = conv_tile(p_ref, cw_ref, cb_ref, r0, cols)
             gate = sigmoid(conv)
             act = conv * gate
             act_ref[rows, cols] = act.astype(BF)
@@ -178,29 +177,18 @@
                 h_ref[0, :, lanes] = nn(b_turned, (wide * x2.astype(F32)).astype(BF))
             return carry
 
-        lax.fori_loop(0, LOCAL_HEADS // 2, pair, 0)
-
-    @pl.when(first)
-    def _():
-        def one(i, carry):
-            block(pl.multiple_of(i * 128, 128), 128, False, False)
-            return carry
-
-        lax.fori_loop(0, TILE // 128, one, 0)
-
-    @pl.when(jnp.logical_not(first))
-    def _():
-        block(0, SPAN, False, True)
-        block(SPAN, SPAN, True, False)
+        lax.fori_loop(0, LOCAL_HEADS // 2, pair, 0, unroll=True)
+
+    block(0, HEAD, False, False)
+    block(HEAD, SPAN, False, True)
+    block(HEAD + SPAN, SPAN, True, False)
 
 
 def bwd_kernel(
-    steps_ref, p_ref, act_ref, slope_ref, dy_ref, h_ref, cw_ref, hp_ref, dsk_ref, seg_ref, bc_ref, *refs
+    steps_ref, p_ref, act_ref, slope_ref, dy_ref, dz_ref, h_ref, cw_ref, hp_ref, dsk_ref, seg_ref, bc_ref, *refs
 ):
     dp_ref, acc_ref, hacc_ref = refs[-18:-15]
     dt_s, parts_s, grow_s, ct_s, gt_s, dgt_s, kc_s, kr_s, fold_s, dbc_s, ds_s, da_s, dst_s, after_s, sums_s = refs[-15:]
-    first = steps_ref[pl.program_id(0)] == 0
-    seq = jnp.where(first, 128, 512)
     lane = lane_index()
     head_row = lax.broadcasted_iota(jnp.int32, (LOCAL_HEADS, 1), 0)
 
@@ -307,7 +295,7 @@
                 da_s[pl.ds(off + lo, 128), lanes] = out
             return carry
 
-        lax.fori_loop(0, LOCAL_HEADS // 2, pair, 0)
+        lax.fori_loop(0, LOCAL_HEADS // 2, pair, 0, unroll=True)
 
         dgt = dgt_s[:q, :q].astype(BF)
         db = nn(dgt, c)
@@ -333,30 +321,22 @@
         dst_s[rows, :] = d_dt + d_rate * rate
         hacc_ref[1:2, :] += jnp.sum(d_rate * dt, axis=0, keepdims=True)
 
-    @pl.when(first)
-    def _():
-        def one(i, carry):
-            block(pl.multiple_of(i * 128, 128), 128, False, False)
-            return carry
-
-        lax.fori_loop(0, TILE // 128, one, 0)
-
-    @pl.when(jnp.logical_not(first))
-    def _():
-        block(SPAN, SPAN, True, False)
-        block(0, SPAN, False, True)
+    block(0, HEAD, False, False)
+    block(HEAD + SPAN, SPAN, True, False)
+    block(HEAD, SPAN, False, True)
 
     d_soft = dst_s[...] * jax.nn.sigmoid(p_ref[:, XBC:] + hp_ref[0:1])
     d_soft = jnp.where(lane < LOCAL_HEADS, d_soft, 0.0)
     hacc_ref[0:1, :] += jnp.sum(d_soft, axis=0, keepdims=True)
-    dp_ref[:, XBC:] = d_soft.astype(BF)
+    dp_ref[:, XBC:XCOLS] = d_soft.astype(BF)
+    dp_ref[:, XCOLS:] = dz_ref[...]
     sums_s[...] = jnp.zeros_like(sums_s)
     after_s[...] = jnp.zeros_like(after_s)
 
     def conv_step(i, carry):
         r0 = pl.multiple_of(TILE - ROWS - i * ROWS, ROWS)
         rows = pl.ds(r0, ROWS)
-        ends = ((r0 + ROWS) & (seq - 1)) == 0
+        ends = (r0 + ROWS == HEAD) | (r0 + ROWS == TILE)
         fold = lambda v: jnp.sum(v.reshape(ROWS // 8, 8, 128), axis=0)
         for c in range(XBC // 128):
             cols = slice(c * 128, c * 128 + 128)
@@ -508,24 +488,24 @@
             flops=count * 4 * 10**9, bytes_accessed=count * 6 * 10**6, transcendentals=count * 2 * 10**6
         ),
         name="ssd_forward",
-    )(jnp.asarray(steps, jnp.int32), proj, conv_w, conv_b, heads, skip, seg, spread, *more)
-
-
-def ssd_backward(steps, proj, act, slope, dy, states, conv_w, conv_b, heads, skip, seg, spread, earlier=()):
+    )(jnp.stack(steps).astype(jnp.int32), proj, conv_w, conv_b, heads, skip, seg, spread, *more)
+
+
+def ssd_backward(steps, proj, act, slope, dy, dz, states, conv_w, conv_b, heads, skip, seg, spread, earlier=()):
     tokens = proj.shape[0]
     count = len(steps)
-    more, more_specs, aliases = onto(earlier, 11)
+    more, more_specs, aliases = onto(earlier, 12)
     return pl.pallas_call(
         bwd_kernel,
         grid_spec=pltpu.PrefetchScalarGridSpec(
             num_scalar_prefetch=1,
             grid=(count,),
             in_specs=[
-                placed(XCOLS), placed(XBC), placed(XBC), placed(WIDTH), STATES, whole((8, XBC)),
+                placed(XCOLS), placed(XBC), placed(XBC), placed(WIDTH), placed(WIDTH), STATES, whole((8, XBC)),
                 whole((8, 128)), whole((8, WIDTH)), whole((128, WIDTH)), whole((128, 128 * LOCAL_HEADS)),
                 *more_specs,
             ],
-            out_specs=[placed(XCOLS), whole((8, XBC)), whole((8, 128))],
+            out_specs=[placed(XCOLS + WIDTH), whole((8, XBC)), whole((8, 128))],
             scratch_shapes=[
                 pltpu.VMEM((TILE, 128), F32),
                 pltpu.VMEM((SPAN, 128), BF),
@@ -545,7 +525,7 @@
             ],
         ),
         out_shape=[
-            jax.ShapeDtypeStruct((tokens, XCOLS), BF),
+            jax.ShapeDtypeStruct((tokens, XCOLS + WIDTH), BF),
             jax.ShapeDtypeStruct((8, XBC), F32),
             jax.ShapeDtypeStruct((8, 128), F32),
         ],
@@ -555,7 +535,7 @@
             flops=count * 10 * 10**9, bytes_accessed=count * 9 * 10**6, transcendentals=count * 4 * 10**6
         ),
         name="ssd_backward",
-    )(jnp.asarray(steps, jnp.int32), proj, act, slope, dy, states, conv_w, heads, skip, seg, spread, *more)
+    )(jnp.stack(steps).astype(jnp.int32), proj, act, slope, dy, dz, states, conv_w, heads, skip, seg, spread, *more)
 
 
 def gate_stats(order, y, z, dn, gain):
@@ -596,55 +576,58 @@
     )(order, st, y, z, dn, gain)
 
 
-def norm_tokens(order, values, gain, row, tokens, earlier=()):
+def norm_tokens(order, values, gain):
     rows = sum(v.shape[0] for v in values)
-    start = row // rows
-    count = len(values)
-    more, more_specs, aliases = onto(earlier, count + 2)
     return pl.pallas_call(
-        functools.partial(norm_kernel, count),
+        functools.partial(norm_kernel, len(values)),
         grid_spec=pltpu.PrefetchScalarGridSpec(
             num_scalar_prefetch=1,
             grid=(1,),
-            in_specs=[*(whole(v.shape) for v in values), whole((8, D)), *more_specs],
-            out_specs=[pl.BlockSpec((rows, D), lambda i, o: (start, 0))],
+            in_specs=[*(whole(v.shape) for v in values), whole((8, D))],
+            out_specs=[whole((rows, D))],
         ),
-        out_shape=[jax.ShapeDtypeStruct((tokens, D), BF)],
-        input_output_aliases=aliases,
+        out_shape=[jax.ShapeDtypeStruct((rows, D), BF)],
         compiler_params=params(),
         cost_estimate=pl.CostEstimate(flops=rows * 10**6, bytes_accessed=rows * 8192, transcendentals=rows),
         name="norm_tokens",
-    )(order, *values, gain, *more)[0]
-
-
-def pack_kernel(at_ref, in_ref, dt_ref, xs_ref, xk_ref, zs_ref, zk_ref):
+    )(order, *values, gain)[0]
+
+
+def pack_kernel(at_ref, in_ref, dt_ref, small_ref, send_ref, keep_ref):
     rows = in_ref.shape[0]
+    send_ref[:, rows:, :] = jnp.zeros((2, 8, XCOLS + WIDTH), BF)
+    send_ref[0, rows:, :] = small_ref[...]
     source = lax.broadcasted_iota(jnp.int32, (HEADS, 128), 0)
     lane = lax.broadcasted_iota(jnp.int32, (HEADS, 128), 1)
-    for x_ref, z_ref, x in ((xs_ref, zs_ref, 1 - at_ref[0]), (xk_ref, zk_ref, at_ref[0])):
+    for out_ref, x in ((send_ref, 1 - at_ref[0]), (keep_ref, at_ref[0])):
         for core in range(2):
             slot = 2 * core + x
             for k in range(AHEADS):
-                cols = slice(k * 128, k * 128 + 128)
                 at = (k * SLOTS + slot) * 128
-                z_ref[core, :, cols] = in_ref[:, pl.ds(pl.multiple_of(at, 128), 128)]
-                x_ref[core, :, cols] = in_ref[:, pl.ds(pl.multiple_of(DI + at, 128), 128)]
-            x_ref[core, :, WIDTH:XBC] = in_ref[:, 2 * DI :]
+                out_ref[core, :rows, XCOLS + k * 128 : XCOLS + k * 128 + 128] = in_ref[
+                    :, pl.ds(pl.multiple_of(at, 128), 128)
+                ]
+                out_ref[core, :rows, k * 128 : k * 128 + 128] = in_ref[
+                    :, pl.ds(pl.multiple_of(DI + at, 128), 128)
+                ]
+            out_ref[core, :rows, WIDTH:XBC] = in_ref[:, 2 * DI :]
             wanted = jnp.where(lane < LOCAL_HEADS, (lane // 2) * 8 + slot * 2 + lane % 2, -1)
-            x_ref[core, :, XBC:] = nn(dt_ref[...], jnp.where(source == wanted, 1.0, 0.0).astype(BF)).astype(BF)
-
-
-def pack_weights(xi, in_w, dt_w):
+            out_ref[core, :rows, XBC:XCOLS] = nn(
+                dt_ref[...], jnp.where(source == wanted, 1.0, 0.0).astype(BF)
+            ).astype(BF)
+
+
+def pack_weights(xi, in_w, dt_w, small):
     rows = in_w.shape[0]
-    shapes = [(2, rows, XCOLS)] * 2 + [(2, rows, WIDTH)] * 2
+    small = pad_rows(pad_cols(small[None], XCOLS + WIDTH))
     return pl.pallas_call(
         pack_kernel,
-        in_specs=[pl.BlockSpec(memory_space=pltpu.SMEM)] + [pl.BlockSpec(memory_space=pltpu.VMEM)] * 2,
-        out_specs=[pl.BlockSpec(memory_space=pltpu.VMEM)] * 4,
-        out_shape=[jax.ShapeDtypeStruct(shape, BF) for shape in shapes],
+        in_specs=[pl.BlockSpec(memory_space=pltpu.SMEM)] + [pl.BlockSpec(memory_space=pltpu.VMEM)] * 3,
+        out_specs=[pl.BlockSpec(memory_space=pltpu.VMEM)] * 2,
+        out_shape=[jax.ShapeDtypeStruct((2, r, XCOLS + WIDTH), BF) for r in (rows + 8, rows)],
         cost_estimate=pl.CostEstimate(flops=10**8, bytes_accessed=3 * 10**6, transcendentals=0),
         name="pack_weights",
-    )(xi[None].astype(jnp.int32), in_w, dt_w)
+    )(xi[None].astype(jnp.int32), in_w, dt_w, small)
 
 
 def pair_kernel(at_ref, keep_ref, got_ref, send_ref, stay_ref):
@@ -653,7 +636,7 @@
     other = pl.ds(pl.multiple_of((1 - at_ref[0]) * rows, rows), rows)
     for out, core in ((send_ref, 1 - at_ref[1]), (stay_ref, at_ref[1])):
         out[mine, :] = keep_ref[core]
-        out[other, :] = got_ref[core]
+        out[other, :] = got_ref[core, :rows]
 
 
 def pair_rows(xi, ci, keep, got):
@@ -668,21 +651,76 @@
     )(jnp.stack([xi, ci]).astype(jnp.int32), keep, got)
 
 
-def place_kernel(at_ref, stay_ref, got_ref, out_ref):
+def place_kernel(at_ref, stay_ref, got_ref, x_ref, z_ref):
     rows = stay_ref.shape[0]
-    out_ref[pl.ds(pl.multiple_of(at_ref[0] * rows, rows), rows), :] = stay_ref[...]
-    out_ref[pl.ds(pl.multiple_of((1 - at_ref[0]) * rows, rows), rows), :] = got_ref[...]
+    for index, ref in ((at_ref[0], stay_ref), (1 - at_ref[0], got_ref)):
+        at = pl.ds(pl.multiple_of(index * rows, rows), rows)
+        x_ref[at, :] = ref[:, :XCOLS]
+        z_ref[at, :] = ref[:, XCOLS:]
 
 
 def place_rows(index, stay, got):
+    rows = 2 * stay.shape[0]
     return pl.pallas_call(
         place_kernel,
         in_specs=[pl.BlockSpec(memory_space=pltpu.SMEM)] + [pl.BlockSpec(memory_space=pltpu.VMEM)] * 2,
-        out_specs=pl.BlockSpec(memory_space=pltpu.VMEM),
-        out_shape=jax.ShapeDtypeStruct((2 * stay.shape[0], stay.shape[1]), BF),
+        out_specs=[pl.BlockSpec(memory_space=pltpu.VMEM)] * 2,
+        out_shape=[jax.ShapeDtypeStruct((rows, XCOLS), BF), jax.ShapeDtypeStruct((rows, WIDTH), BF)],
         cost_estimate=pl.CostEstimate(flops=0, bytes_accessed=2 * 10**6, transcendentals=0),
         name="place_rows",
     )(index[None].astype(jnp.int32), stay, got)
+
+
+def assemble_kernel(at_ref, pz_ref, gz_ref, px_ref, gx_ref, in_ref, dt_ref, out_ref, dt_out_ref, sum_ref):
+    rows = in_ref.shape[0]
+    total = jnp.zeros((rows, 128), F32)
+    shared = [jnp.zeros((rows, 128), F32), jnp.zeros((rows, 128), F32)]
+    dt_total = jnp.zeros((rows, HEADS), F32)
+    lane = lax.broadcasted_iota(jnp.int32, (128, HEADS), 0)
+    place = lax.broadcasted_iota(jnp.int32, (128, HEADS), 1)
+    for core in range(2):
+        for mine in (True, False):
+            x = at_ref[0] if mine else 1 - at_ref[0]
+            slot = 2 * core + x
+            z_of = (lambda cols: pz_ref[core, x, :, cols]) if mine else (lambda cols: gz_ref[core, :, cols])
+            x_of = (lambda cols: px_ref[core, x, :, cols]) if mine else (lambda cols: gx_ref[core, :, cols])
+            for k in range(AHEADS):
+                cols = slice(k * 128, k * 128 + 128)
+                at = (k * SLOTS + slot) * 128
+                for value, start in ((z_of(cols), at), (x_of(cols), DI + at)):
+                    lanes = pl.ds(pl.multiple_of(start, 128), 128)
+                    value = value.astype(F32)
+                    out_ref[:, lanes] = value
+                    total = total + value * in_ref[:, lanes].astype(F32)
+            for k in range(2):
+                shared[k] = shared[k] + x_of(slice(WIDTH + k * 128, WIDTH + k * 128 + 128)).astype(F32)
+            wanted = jnp.where(lane < LOCAL_HEADS, (lane // 2) * 8 + slot * 2 + lane % 2, -1)
+            dt_total = dt_total + nn(x_of(slice(XBC, XCOLS)), jnp.where(place == wanted, 1.0, 0.0).astype(BF))
+    for k in range(2):
+        cols = slice(2 * DI + k * 128, 2 * DI + k * 128 + 128)
+        out_ref[:, cols] = shared[k]
+        total = total + shared[k] * in_ref[:, cols].astype(F32)
+    dt_out_ref[...] = dt_total
+    rows_sum = jnp.sum(total, axis=1, keepdims=True) + jnp.sum(
+        dt_total * dt_ref[...].astype(F32), axis=1, keepdims=True
+    )
+    sum_ref[...] = jnp.broadcast_to(rows_sum, (rows, 128))
+
+
+def assemble_rows(xi, z_pair, z_got, x_pair, x_got, in_w, dt_w):
+    rows = in_w.shape[0]
+    return pl.pallas_call(
+        assemble_kernel,
+        in_specs=[pl.BlockSpec(memory_space=pltpu.SMEM)] + [pl.BlockSpec(memory_space=pltpu.VMEM)] * 6,
+        out_specs=[pl.BlockSpec(memory_space=pltpu.VMEM)] * 3,
+        out_shape=[
+            jax.ShapeDtypeStruct(in_w.shape, F32),
+            jax.ShapeDtypeStruct(dt_w.shape, F32),
+            jax.ShapeDtypeStruct((rows, 128), F32),
+        ],
+        cost_estimate=pl.CostEstimate(flops=10**7, bytes_accessed=5 * 10**6, transcendentals=0),
+        name="assemble_rows",
+    )(xi[None].astype(jnp.int32), z_pair, z_got, x_pair, x_got, in_w, dt_w)
 
 
 def swap_x(v):
@@ -728,9 +766,7 @@
         self.flying = swap_x(pick(self.pair, 1 - self.xi, 1))
 
     def land(self, chain):
-        got = chain.take(self.flying)
-        own = joined(self.xi, pick(self.pair, self.xi, 1)[:, None], got[:, None], 1)
-        return own.reshape(4, self.rows, -1).astype(F32)
+        self.got = chain.take(self.flying)
 
 
 class Chain:
@@ -852,33 +888,12 @@
     )
 
 
-def reordered(v, order, short, long):
-    parts = [v[:, k * short : (k + 1) * short] for k in order]
-    base = 4 * short
-    parts += [v[:, base + k * long : base + (k + 1) * long] for k in order]
-    return jnp.concatenate(parts, axis=1)
-
-
 def pad_rows(v, rows=8):
     return jnp.concatenate([v, jnp.zeros((rows - v.shape[0], v.shape[1]), v.dtype)], axis=0)
 
 
 def pad_cols(v, cols):
     return jnp.concatenate([v, jnp.zeros(v.shape[:-1] + (cols - v.shape[-1],), v.dtype)], axis=-1)
-
-
-def gather_small(v, sizes, chain):
-    count = int(np.prod(sizes))
-    if count != 32:
-        return lax.all_gather(v[None], ALL, axis=0, tiled=True)
-    me = flat_index(sizes)
-    v = v[None]
-    bit = 1
-    while bit < count:
-        got = chain.take(lax.ppermute(v, ALL, [(i, i ^ bit) for i in range(count)]))
-        v = joined((me // bit) % 2, v, got, 0)
-        bit *= 2
-    return v
 
 
 def per_device(
@@ -887,8 +902,6 @@
 ):
     ringed = sizes == (8, 2, 1, 2)
     short, long = tokens_short.shape[0], tokens_long.shape[0]
-    base = 4 * short
-    tokens = base + 4 * long
     xi, ci = lax.axis_index("x"), lax.axis_index("core")
     slot = ci * 2 + xi
     feature = D // AHEADS
@@ -907,73 +920,49 @@
     pieces = [conv_w.reshape(-1), conv_b, norm_gain, gate_gain]
     ends = np.cumsum([0] + [p.shape[0] for p in pieces])
     small = jnp.concatenate(pieces)
-    half = long // 2
-
-    part = long // 4
-    long_parts = [tokens_long[k * part : (k + 1) * part] for k in range(4)]
+    group = ("core", "x")
+    everyone = lambda v: lax.all_gather(v, group, axis=0, tiled=True)
+
+    def stage(v, bit):
+        count = int(np.prod(sizes))
+        return lax.ppermute(v, ALL, [(i, i ^ bit) for i in range(count)])
+
+    def widen(v, got, bit):
+        return joined((flat_index(sizes) // bit) % 2, v, got, 0)
+
     if ringed:
-        x_send, x_keep, z_send, z_keep = chain.mark(pack_weights(xi, in_w, dt_w))
-        x_got = swap_x(x_send)
-        c_s, c_l = swap_core(chain.tie(tokens_short)), swap_core(chain.tie(tokens_long))
-        send, stay = chain.mark(pair_rows(xi, ci, x_keep, chain.take(x_got)))
+        rows, n = in_w.shape[0], small.shape[0]
+        x_send, x_keep = chain.mark(pack_weights(xi, in_w, dt_w, small))
+        x_got = chain.take(swap_x(x_send))
+        small = widen(small[None], x_got[0, rows : rows + 1, :n], 1)
+        passing = stage(small, 2)
+        send, stay = chain.mark(pair_rows(xi, ci, x_keep, x_got))
         got = swap_core(send)
-        t_s = swap_x(chain.tie(tokens_short))
-        gather_x = Gather(ring, chain.mark(place_rows(ci, stay, chain.take(got))))
+        small = widen(small, chain.take(passing), 2)
+        passing = stage(small, 4)
+        got = chain.take(got)
+        small = widen(small, chain.take(passing), 4)
+        passing = stage(small, 8)
+        x_block, z_block = chain.mark(place_rows(ci, stay, got))
+        small = widen(small, chain.take(passing), 8)
+        small = widen(small, chain.take(stage(small, 16)), 16)
+        gather_x = Gather(ring, chain.tie(x_block))
         gather_x.start()
-        pieces_l = [swap_x(chain.tie(long_parts[0]))]
     else:
-        c_s, c_l = swap_core(tokens_short), swap_core(tokens_long)
-        t_s = swap_x(tokens_short)
-        pieces_l = [swap_x(v) for v in long_parts]
-
-    small = chain.mark(gather_small(small, sizes, chain))
-    norm_full = chain.mark(pad_rows(small[:, ends[2] : ends[3]].reshape(1, -1).astype(F32)))
-
-    xh = ()
-
-    def norm(values, row):
-        nonlocal xh
-        xh = (chain.mark(norm_tokens(order, values, norm_full, row, tokens, xh)),)
-
-    t_s = chain.take(t_s)
-    cx_s = swap_core(t_s)
+        small = lax.all_gather(small[None], ALL, axis=0, tiled=True)
+    norm_full = pad_rows(small[:, ends[2] : ends[3]].reshape(1, -1).astype(F32))
+    u_own = chain.mark(norm_tokens(order, [chain.tie(tokens_short), tokens_long], norm_full))
+    xh = everyone(u_own)
     if ringed:
-        pieces_l.append(swap_x(chain.tie(long_parts[1])))
         gather_x.land(chain)
         gather_x.start()
-    norm([chain.tie(tokens_short)], 0)
-    norm([chain.take(c_s)], 2 * short)
-    norm([chain.tie(tokens_long)], base)
-    if ringed:
-        pieces_l[0] = chain.take(pieces_l[0])
-        pieces_l.append(swap_x(chain.tie(long_parts[2])))
-        gather_x.land(chain)
-        gather_x.start()
-    norm([chain.take(c_l)], base + 2 * long)
-    norm([t_s], short)
-    if ringed:
-        pieces_l[1] = chain.take(pieces_l[1])
-        pieces_l.append(swap_x(chain.tie(long_parts[3])))
-        gather_x.land(chain)
-        gather_x.start()
-    pieces_c = [swap_core(pieces_l[0]), swap_core(pieces_l[1])]
-    norm([chain.take(cx_s)], 3 * short)
-    norm(pieces_l[:2], base + long)
-    if ringed:
-        gather_o = Gather(ring, chain.tie(out_w))
-        gather_o.start()
-        pieces_l[2] = chain.take(pieces_l[2])
-        z_got = swap_x(chain.tie(z_send))
-        gather_x.land(chain)
-    pieces_c = chain.take(pieces_c)
-    norm(pieces_c, base + 3 * long)
 
     small, dt_bias, a_log, d_skip, cot_s, cot_l = chain.mark(
         chain.tie((small, dt_bias, a_log, d_skip, cot_short, cot_long))
     )
     live_s = (jnp.arange(short) < seq_lengths[0, 0]).astype(F32)[:, None]
     live_l = (jnp.arange(long) < seq_lengths[1, 0]).astype(F32)[:, None]
-    dv_s, dv_l = (live_s * cot_s).astype(BF), (live_l * cot_l).astype(BF)
+    dv_own = chain.mark(jnp.concatenate([(live_s * cot_s).astype(BF), (live_l * cot_l).astype(BF)], axis=0))
     taps = small[:, : ends[2]].reshape(-1, KERNEL + 1, width)
     taps = taps.transpose(1, 0, 2).reshape(KERNEL + 1, -1).astype(F32)
     taps = jnp.concatenate([mine_cols(taps[:, :DI]), taps[:, DI:]], axis=1)
@@ -992,47 +981,44 @@
         BF,
     )
     seq_params = (conv_taps, conv_bias, heads, skip, seg, spread)
-
-    pieces_l[3] = chain.take(pieces_l[3])
-    pieces_c = [swap_core(pieces_l[2]), swap_core(pieces_l[3])]
+    slots = [jnp.int32(k) for k in range(SLOTS)]
+
     if ringed:
+        gather_x.land(chain)
+        gather_x.start()
+        gather_x.land(chain)
+        gather_x.start()
+        gather_x.land(chain)
+        o_block, z_block = chain.tie((out_w, z_block))
+        gather_o, gather_z = Gather(ring, o_block), Gather(ring, z_block)
+        both = gather_o, gather_z
+        gather_o.start()
+        gather_z.start()
         w_x = chain.mark(jnp.concatenate(gather_x.blocks(), axis=0))
-        gather_o.land(chain)
-        gather_o.start()
-    norm(pieces_l[2:], base + long + 2 * part)
-    norm(chain.take(pieces_c), base + 3 * long + 2 * part)
-    xh = xh[0]
-    if ringed:
-        send, stay = chain.mark(pair_rows(xi, ci, z_keep, chain.take(z_got)))
-        dvx_s, dvx_a, dvx_b = swap_x(chain.tie(dv_s)), swap_x(chain.tie(dv_l[:half])), swap_x(chain.tie(dv_l[half:]))
-        dvc_s, dvc_l = swap_core(chain.tie(dv_s)), swap_core(chain.tie(dv_l))
-        got = chain.take(swap_core(send))
-        gather_z = Gather(ring, chain.mark(place_rows(ci, stay, got)))
-        gather_z.start()
-        proj = chain.mark(nn(chain.tie(xh), w_x))
-        for gather in (gather_o, gather_z):
+        xh = chain.take(xh)
+        dv = everyone(chain.tie(dv_own))
+        for gather in both:
             gather.land(chain)
             gather.start()
-        dvx_s = chain.take(dvx_s)
-        kept = chain.mark(ssd_forward((0, 1, 2), chain.tie(proj), *seq_params))
-        for gather in (gather_o, gather_z):
+        proj = chain.mark(nn(chain.tie(xh), w_x))
+        for gather in both:
             gather.land(chain)
             gather.start()
-        dvx_a, dvx_b = chain.take(dvx_a), chain.take(dvx_b)
-        dvcx_s, dvcx_a, dvcx_b = swap_core(dvx_s), swap_core(dvx_a), swap_core(dvx_b)
-        y, act, slope, states = chain.mark(ssd_forward((3, 4), chain.tie(proj), *seq_params, earlier=kept))
-        gather_o.land(chain)
-        gather_z.land(chain)
-        gather_z.start()
-        w_o = chain.mark(jnp.concatenate(gather_o.blocks(), axis=0))
-        dvcx_s, dvcx_a, dvcx_b, dvc_s, dvc_l = chain.take((dvcx_s, dvcx_a, dvcx_b, dvc_s, dvc_l))
-        dv = chain.mark(
-            jnp.concatenate([dv_s, dvx_s, dvc_s, dvcx_s, dv_l, dvx_a, dvx_b, dvc_l, dvcx_a, dvcx_b], axis=0)
-        )
+        kept = chain.mark(ssd_forward(slots[:2], chain.tie(proj), *seq_params))
+        for gather in both:
+            gather.land(chain)
+            gather.start()
+        y, act, slope, states = chain.mark(ssd_forward(slots[2:], chain.tie(proj), *seq_params, earlier=kept))
+        for gather in both:
+            gather.land(chain)
+        w_all = chain.mark(jnp.concatenate([w_x, jnp.concatenate(gather_z.blocks(), axis=0)], axis=1))
+        z = chain.mark(nn(chain.tie(xh), w_all[:, XCOLS:]).astype(BF))
+        w_o = jnp.zeros((WIDTH, D), BF)
+        for k, block in enumerate(gather_o.blocks()):
+            w_o = lax.dynamic_update_slice(w_o, chain.tie(block), (order[k] * (WIDTH // AHEADS), 0))
+        w_o = chain.mark(w_o)
+        dv = chain.take(dv)
         dn = chain.mark(nt(dv, w_o).astype(BF))
-        gather_z.land(chain)
-        w_z = chain.mark(jnp.concatenate(gather_z.blocks(), axis=0))
-        z = chain.mark(nn(chain.tie(xh), w_z).astype(BF))
     else:
         full = lax.all_gather(in_w, ALL, axis=0, tiled=True)
         full_dt = lax.all_gather(dt_w, ALL, axis=0, tiled=True)
@@ -1042,48 +1028,25 @@
             [mine_cols(full[:, DI : 2 * DI]), full[:, 2 * DI :], pad_cols(mine_cols(full_dt), 128)], axis=-1
         )
         w_o = pick(full_out.reshape(AHEADS, SLOTS, 128, D), slot, 1).reshape(WIDTH, D)
-        dvx_s, dvx_l = swap_x(dv_s), swap_x(dv_l)
-        dv = jnp.concatenate(
-            [dv_s, dvx_s, swap_core(dv_s), swap_core(dvx_s), dv_l, dvx_l, swap_core(dv_l), swap_core(dvx_l)], axis=0
-        )
+        dv = everyone(dv_own)
         proj = nn(xh, w_x)
-        y, act, slope, states = ssd_forward((0, 1, 2, 3, 4), proj, *seq_params)
+        y, act, slope, states = ssd_forward(slots, proj, *seq_params)
         dn = nt(dv, w_o).astype(BF)
         z = nn(xh, w_z).astype(BF)
-
-    st = chain.mark(gate_stats(order, y, chain.tie(z), dn, gate_mine))
-    st = st + reordered(swap_core(st), (2, 3, 0, 1), short, long)
-    st = st + reordered(swap_x(st), (1, 0, 3, 2), short, long)
-    n, dy, dz = chain.mark(gate_backward(order, st, y, z, dn, gate_mine))
-
-    far_s, far_l = slice(2 * short, base), slice(base + 2 * long, tokens)
-    mid_s, mid_l = slice(short, 2 * short), slice(base + long, base + 2 * long)
-    own_s, own_l = slice(0, short), slice(base, base + long)
-
-    def send_far(product):
-        values = chain.mark((product(far_s).astype(BF), product(far_l).astype(BF)))
-        return swap_core(values[0]), swap_core(values[1])
-
-    def send_mid(product, far):
-        values = chain.mark(
-            (
-                (product(mid_s) + far[0][short:].astype(F32)).astype(BF),
-                (product(mid_l) + far[1][long:].astype(F32)).astype(BF),
-            )
-        )
-        return swap_x(values[0]), swap_x(values[1])
-
-    def own_product(product):
-        return chain.mark((product(own_s), product(own_l)))
-
-    def with_own(own, far, mid):
-        return (
-            own[0] + far[0][:short].astype(F32) + mid[0].astype(F32),
-            own[1] + far[1][:long].astype(F32) + mid[1].astype(F32),
-        )
-
-    def finish(product, far, mid):
-        return with_own(own_product(product), far, mid)
+        w_all = jnp.concatenate([w_x, w_z], axis=1)
+
+    straight = jnp.arange(AHEADS, dtype=jnp.int32)
+    st = chain.mark(gate_stats(straight, y, chain.tie(z), dn, gate_mine))
+    st = st + swap_core(st)
+    st = st + swap_x(st)
+    n, dy, dz = chain.mark(gate_backward(straight, st, y, z, dn, gate_mine))
+
+    own = short + long
+    rows_of = lambda v, start, count: lax.dynamic_slice(v, (start * own, 0), (count * own, v.shape[1]))
+
+    def unit_product(dx, start, count):
+        dx = chain.tie(dx)
+        return nt(rows_of(dx, start, count), w_all)
 
     here = (jnp.arange(SLOTS) == slot).astype(F32)
     spread_cols = lambda v: (v.reshape(v.shape[0], AHEADS, 1, -1) * here[:, None]).reshape(v.shape[0], -1)
@@ -1096,94 +1059,77 @@
 
     def backward_call(steps, earlier):
         return chain.mark(
-            ssd_backward(steps, chain.tie(proj), act, slope, dy, states, *seq_params, earlier=earlier)
+            ssd_backward(steps, chain.tie(proj), act, slope, dy, dz, states, *seq_params, earlier=earlier)
         )
 
-    def branch_product(part):
-        return nn(chain.tie(n)[part], w_o)
-
-    def unit_product(dx):
-        return lambda part: nt(chain.tie(dx)[part], w_x) + nt(dz[part], w_z)
-
-    g_out = chain.mark(tn(n, dv))
+    far, mid = 2 * (1 - ci), 2 * ci + 1 - xi
+    g_out = chain.mark(tn(n, dv).astype(BF))
+    reduced = lambda v, axes: lax.psum_scatter(v, axes, scatter_dimension=0, tiled=True)
     if ringed:
-        blocks_o = g_out.reshape(AHEADS, -1, D)
-        scatter_o = Scatter(ring, lambda k: blocks_o[k])
-        scatter_o.start()
+        own_out = reduced(g_out, "ra").astype(F32)
         g_z = chain.mark(tn(chain.tie(xh), dz))
         blocks_z = g_z.reshape(AHEADS, -1, WIDTH)
         scatter_z = Scatter(ring, lambda k: blocks_z[k])
         scatter_z.start()
-        scatter_o.land(chain)
-        scatter_o.start()
-        far_v = send_far(branch_product)
+    else:
+        g_z = tn(xh, dz)
+    branch = chain.mark(nn(chain.tie(n), w_o).astype(BF))
+    branch = reduced(branch, group)
+    if ringed:
         scatter_z.land(chain)
         scatter_z.start()
-        far_v = chain.take(far_v)
-        mid_v = send_mid(branch_product, far_v)
-        for scatter in (scatter_o, scatter_z):
-            scatter.land(chain)
-            scatter.start()
-        dx, acc, hacc = backward_call((0, 3), ())
-        for scatter in (scatter_o, scatter_z):
-            scatter.land(chain)
-            scatter.start()
-        dx, acc2, hacc2 = backward_call((4,), (dx,))
-        acc, hacc = acc + acc2, hacc + hacc2
-        far_u = send_far(unit_product(dx))
-        for scatter in (scatter_o, scatter_z):
-            scatter.land(chain)
-        own_out = chain.mark(scatter_o.total())
-        back_z = Return(chain.mark(scatter_z.total()))
-        mid_v = chain.take(mid_v)
-        v_s, v_l = finish(branch_product, far_v, mid_v)
-        back_z.turn(chain)
-        dx, acc2, hacc2 = backward_call((2,), (chain.tie(dx),))
+        dx, acc, hacc = backward_call([far, far + 1], ())
+        scatter_z.land(chain)
+        scatter_z.start()
+        far_u = swap_core(chain.mark(unit_product(dx, far, 2).astype(BF)))
+        scatter_z.land(chain)
+        scatter_z.start()
+        dx, acc2, hacc2 = backward_call([mid], (chain.tie(dx),))
         acc, hacc = acc + acc2, hacc + hacc2
         far_u = chain.take(far_u)
-        own_z = chain.mark(back_z.land(chain))
-        mid_u = send_mid(unit_product(dx), far_u)
-        dx, acc2, hacc2 = backward_call((1,), (chain.tie(dx),))
+        mid_u = chain.mark(
+            (unit_product(dx, mid, 1) + rows_of(far_u, 1 - xi, 1).astype(F32)).astype(BF)
+        )
+        mid_u = swap_x(mid_u)
+        scatter_z.land(chain)
+        back_z = Return(chain.mark(scatter_z.total()))
+        dx, acc2, hacc2 = backward_call([slot], (chain.tie(dx),))
         acc, hacc = acc + acc2, hacc + hacc2
         scatter_x = Scatter(
-            ring, lambda k: chain.mark(tn(xh[:, k * feature : (k + 1) * feature], chain.tie(dx)))
+            ring, lambda k: chain.mark(tn(xh[:, k * feature : (k + 1) * feature], chain.tie(dx)[:, :XCOLS]))
         )
         scatter_x.start()
-        tally = SmallSum(small_terms(acc, hacc), sizes)
+        scatter_x.land(chain)
+        scatter_x.start()
+        back_z.turn(chain)
+        tally = SmallSum(small_terms(*chain.tie((acc, hacc))), sizes)
         tally.start()
         scatter_x.land(chain)
         scatter_x.start()
         tally.land(chain)
         tally.start()
-        du_own = own_product(unit_product(dx))
+        du_own = chain.mark(unit_product(dx, slot, 1) + rows_of(far_u, xi, 1).astype(F32))
         scatter_x.land(chain)
         scatter_x.start()
         tally.land(chain)
         tally.start()
-        scatter_x.land(chain)
-        scatter_x.start()
-        tally.land(chain)
-        tally.start()
+        back_z.land(chain)
+        mid_u = chain.take(mid_u)
+        du = du_own + mid_u.astype(F32)
         scatter_x.land(chain)
         back_x = Return(chain.mark(scatter_x.total()))
         tally.land(chain)
         tally.start()
-        mid_u = chain.take(mid_u)
-        du_s, du_l = chain.mark(with_own(du_own, far_u, mid_u))
         back_x.turn(chain)
         tally.land(chain)
-        total = tally.value
+        tally.start()
     else:
-        g_z = tn(xh, dz)
-        far_v = send_far(branch_product)
-        mid_v = send_mid(branch_product, far_v)
-        v_s, v_l = finish(branch_product, far_v, mid_v)
-        dx, acc, hacc = backward_call((0, 3, 4, 2, 1), ())
-        far_u = send_far(unit_product(dx))
-        mid_u = send_mid(unit_product(dx), far_u)
-        du_s, du_l = finish(unit_product(dx), far_u, mid_u)
-        g_x = tn(xh, dx)
+        dx, acc, hacc = backward_call(slots, ())
+        du = reduced(nt(dx, w_all), group)
+        g_x = tn(xh, dx[:, :XCOLS])
         total = lax.psum(small_terms(acc, hacc), ALL)
+    v_s, v_l = branch[:short].astype(F32), branch[short:].astype(F32)
+    du_s, du_l = du[:short], du[short:]
 
     out_short = (tokens_short.astype(F32) + live_s * v_s).astype(BF)
     out_long = (tokens_long.astype(F32) + live_l * v_l).astype(BF)
@@ -1195,33 +1141,33 @@
         d_norm = from_ring(d_u) * norm_full[0:1]
         return cot.astype(F32) + row_scale * (d_norm - unit * jnp.mean(d_norm * unit, axis=-1, keepdims=True))
 
-    grad_short = token_grad(tokens_short, cot_short, du_s)
-    grad_long = token_grad(tokens_long, cot_long, du_l)
+    grad_short, grad_long = chain.mark(
+        (token_grad(tokens_short, cot_short, du_s), token_grad(tokens_long, cot_long, du_l))
+    )
 
     if ringed:
-        own_x = back_x.land(chain)
-        grad_in_w = jnp.concatenate(
-            [
-                from_slots(own_z),
-                from_slots(own_x[:, :, :WIDTH]),
-                jnp.sum(own_x[:, :, WIDTH:XBC], axis=0),
-            ],
-            axis=1,
+        back_x.land(chain)
+        grad_in_w, grad_dt_w, norm_sum = chain.mark(
+            assemble_rows(xi, back_z.pair, back_z.got, back_x.pair, back_x.got, in_w, dt_w)
         )
-        grad_dt_w = from_slots(own_x[:, :, XBC : XBC + LOCAL_HEADS])
+        norm_sum = norm_sum[:, 0]
+        tally.land(chain)
+        total = tally.value
     else:
         here = (jnp.arange(SLOTS) == slot).astype(F32)
-        widen = lambda v: (v.reshape(D, AHEADS, 1, -1) * here[:, None]).reshape(D, -1)
+        wider = lambda v: (v.reshape(D, AHEADS, 1, -1) * here[:, None]).reshape(D, -1)
         reduce = lambda v: lax.psum_scatter(v, ALL, scatter_dimension=0, tiled=True)
         grad_in_w = reduce(
-            jnp.concatenate([widen(g_z), widen(g_x[:, :WIDTH]), g_x[:, WIDTH:XBC]], axis=1)
+            jnp.concatenate([wider(g_z), wider(g_x[:, :WIDTH]), g_x[:, WIDTH:XBC]], axis=1)
         )
-        grad_dt_w = reduce(widen(g_x[:, XBC : XBC + LOCAL_HEADS]))
-        own_out = reduce((g_out.reshape(AHEADS, 1, 128, D) * here[:, None, None]).reshape(DI, D))
-
-    grad_norm_gain = (
-        jnp.sum(in_w.astype(F32) * grad_in_w, axis=1) + jnp.sum(dt_w.astype(F32) * grad_dt_w, axis=1)
-    ) / norm_gain.astype(F32)
+        grad_dt_w = reduce(wider(g_x[:, XBC : XBC + LOCAL_HEADS]))
+        own_out = reduce(
+            (g_out.astype(F32).reshape(AHEADS, 1, 128, D) * here[:, None, None]).reshape(DI, D)
+        )
+
+        norm_sum = jnp.sum(in_w.astype(F32) * grad_in_w, axis=1) + jnp.sum(dt_w.astype(F32) * grad_dt_w, axis=1)
+
+    grad_norm_gain = norm_sum / norm_gain.astype(F32)
     grad_gate_gain = jnp.sum(out_w.astype(F32) * own_out, axis=1) / gate_gain.astype(F32)
 
     conv_total = total[: 5 * (DI + 2 * STATE)].reshape(5, -1)

time: 807 us -> 686 us (0.85)
  Pallas kernels: 250 us -> 176 us
  local copies, waits for them, and re-layouts: 86.3 us -> 49 us
  starting transfers between devices: 85.2 us -> 61 us
  between operations: 8.09 us -> 25.5 us
  waiting for transfers between devices: 109 us -> 125 us
  matrix products: 205 us -> 191 us
    ppermute x24 -> x20, waiting for transfers between devices: 30.9 us -> 79 us  [left(): return lax.ppermute(v, 'ra', self.pairs(-1))]
    unnamed x271 -> x128, local copies, waits for them, and re-layouts: 53.3 us -> 19.5 us
    pallas_call x10 -> x2, Pallas kernels: 35.5 us -> 8.98 us  [the longest x1 5.47 us: norm_tokens(): pl.pallas_call(functools.partial(norm_kernel, len(values)), grid_spec=plt...]
    pallas_call x2, Pallas kernels: 65.8 us -> 40.9 us  [ssd_forward(): pl.pallas_call(fwd_kernel, grid_spec=pltpu.PrefetchScalarGridSpec(num_sca...]
    pallas_call x4 -> x3, Pallas kernels: 106 us -> 86.9 us  [ssd_backward(): pl.pallas_call(bwd_kernel, grid_spec=pltpu.PrefetchScalarGridSpec(num_sca...]
    dot_general x13 -> x4, matrix products: 77 us -> 60.8 us  [nt(): lax.dot_general(a, b, (((1,), (1,)), ((), ())), preferred_element_type=F32)]
    ppermute x5 -> x4, waiting for transfers between devices: 17.5 us -> 2.77 us  [stage(): return lax.ppermute(v, ALL, [(i, i ^ bit) for i in range(count)])]
    ppermute x24 -> x20, waiting for transfers between devices: 31.6 us -> 16.9 us  [right(): return lax.ppermute(v, 'ra', self.pairs(1))]
  transfers between devices with their start and end apart: 96 -> 63, of which waited for: 29 -> 29; matrix products, arithmetic and copies ran while one was open for 31% -> 36% of each run, Pallas kernels for 27% -> 20%
where the time goes in v2:
time: 686 us; the launch traced here: 679 us
  matrix products  191 us (28%)
  Pallas kernels  176 us (26%)
  waiting for transfers between devices  125 us (18%)
  starting transfers between devices  61 us (9%)
  other arithmetic  50.2 us (7%)
  local copies, waits for them, and re-layouts  49 us (7%)
  between operations  25.5 us (4%)
    pallas_call x3, Pallas kernels, ssd_backward(): pl.pallas_call(bwd_kernel, grid_spec=pltpu.PrefetchScalarGridSpec(num_sca...  86.9 us
    ppermute x20, waiting for transfers between devices, left(): return lax.ppermute(v, 'ra', self.pairs(-1))  79 us
    dot_general x10, matrix products, tn(): lax.dot_general(a, b, (((0,), (0,)), ((), ())), preferred_element_type=F32)  75.3 us
    dot_general x4, matrix products, nt(): lax.dot_general(a, b, (((1,), (1,)), ((), ())), preferred_element_type=F32)  60.8 us
    dot_general x3, matrix products, nn(): lax.dot_general(a, b, (((1,), (0,)), ((), ())), preferred_element_type=F32)  55.3 us
    pallas_call x2, Pallas kernels, ssd_forward(): pl.pallas_call(fwd_kernel, grid_spec=pltpu.PrefetchScalarGridSpec(num_sca...  40.9 us
    ppermute x20, starting transfers between devices, left(): return lax.ppermute(v, 'ra', self.pairs(-1))  29.8 us
    unnamed x128, local copies, waits for them, and re-layouts  19.5 us
  transfers between devices with their start and end apart: 63, of which 29 were waited for; matrix products, arithmetic and copies ran while one was open for 36% of the time, Pallas kernels for 20%

profile of v2, /device:TPU:0, one launch (start us, length us, event | category | flops | bytes accessed | tf_op | source)
XLA Modules:
  0.0 678.5 jit_solution(18125853875051998532)
XLA Ops:
  15.4 15.3 %collective-permute-done.got_ref = bf16[2,72,2432]{2,1,0:T(8,128)(2,1)S(1)} collective-permute-done((bf16[2,72,2432]{2,1,0:T(8,128)(2,1)}, bf16[2,72,2432]{2,1,0:T(8,128)(2,1)S(1)}, u32[]{:S(2)}, u32[]{:S(2)}) %collective-permute-start) | collective-permute-done | bytes 700448 | tf_op jit(solution)/shard_map/ppermute | solution.py:727
  61.0 11.9 %collective-permute-done.7 = bf16[256,1408]{1,0:T(8,128)(2,1)} collective-permute-done((bf16[256,1408]{1,0:T(8,128)(2,1)S(1)}, bf16[256,1408]{1,0:T(8,128)(2,1)}, u32[]{:S(2)}, u32[]{:S(2)}) %collective-permute-start.7) | collective-permute-done | bytes 720928 | tf_op jit(solution)/shard_map/ppermute | solution.py:804
  78.4 10.5 %collective-permute-done.9 = bf16[256,1408]{1,0:T(8,128)(2,1)} collective-permute-done((bf16[256,1408]{1,0:T(8,128)(2,1)}, bf16[256,1408]{1,0:T(8,128)(2,1)}, u32[]{:S(2)}, u32[]{:S(2)}) %collective-permute-start.9) | collective-permute-done | bytes 720928 | tf_op jit(solution)/shard_map/ppermute | solution.py:804
  95.8 9.9 %collective-permute-done.11 = bf16[256,1408]{1,0:T(8,128)(2,1)S(1)} collective-permute-done((bf16[256,1408]{1,0:T(8,128)(2,1)}, bf16[256,1408]{1,0:T(8,128)(2,1)S(1)}, u32[]{:S(2)}, u32[]{:S(2)}) %collective-permute-start.11) | collective-permute-done | bytes 720928 | tf_op jit(solution)/shard_map/ppermute | solution.py:804
  142.2 20.0 %collective-permute-done.17 = bf16[128,2048]{1,0:T(8,128)(2,1)S(1)} collective-permute-done((bf16[128,2048]{1,0:T(8,128)(2,1)S(1)}, bf16[128,2048]{1,0:T(8,128)(2,1)S(1)}, u32[]{:S(2)}, u32[]{:S(2)}) %collective-permute-start.17) | collective-permute-done | bytes 524320 | tf_op jit(solution)/shard_map/ppermute | solution.py:804
  167.4 22.2 %fusion.77.p_ref = f32[2560,1408]{1,0:T(8,128)} fusion(bf16[2560,2048]{1,0:T(8,128)(2,1)} %all-gather.3.cloned.1.call-done, bf16[2048,1408]{1,0:T(8,128)(2,1)} %constant_dynamic-update-slice_fusion), kind=kOutput, calls=%fused_computation.218 | convolution fusion | flops 14763950080 | bytes 30670848 | tf_op jit(solution)/shard_map/dot_general | solution.py:43
  196.5 20.5 %ssd_forward.2 = (bf16[2560,1024]{1,0:T(8,128)(2,1)}, bf16[2560,1280]{1,0:T(8,128)(2,1)}, bf16[2560,1280]{1,0:T(8,128)(2,1)}, f32[4,128,1024]{2,1,0:T(8,128)}) custom-call(s32[2]{0:T(128)} %iota.32.steps_ref, f32[2560,1408]{1,0:T(8,128)} %fusion.77.p_ref, f32[8,1280]{1,0:T(8,128)} %concatenate.152.cw_ref, f32[8,1280]{1,0:T(8,128)} %select_maximum_fusion.cb_ref, ...), custom_call_target="tpu_custom_call" | custom-call | flops 8000000000 | bytes 12000000 | tf_op jit(solution)/shard_map/ssd_forward/pallas_call | solution.py:461
  221.4 20.4 %ssd_forward.3 = (bf16[2560,1024]{1,0:T(8,128)(2,1)}, bf16[2560,1280]{1,0:T(8,128)(2,1)}, bf16[2560,1280]{1,0:T(8,128)(2,1)}, f32[4,128,1024]{2,1,0:T(8,128)}) custom-call(s32[2]{0:T(128)} %constant.195.clone.1.steps_ref, f32[2560,1408]{1,0:T(8,128)} %fusion.77.p_ref, ...), custom_call_target="tpu_custom_call", output_to_operand_aliasing={{0}: (8, {}), {1}: (9, {}), {2}: (10, {}), {3}: (11, {})} | custom-call | flops 8000000000 | bytes 12000000 | tf_op jit(solution)/shard_map/ssd_forward/pallas_call | solution.py:461
  246.6 16.5 %convolution_convert_fusion.3.z_ref = bf16[2560,1024]{1,0:T(8,128)(2,1)} fusion(bf16[2560,2048]{1,0:T(8,128)(2,1)} %all-gather.3.cloned.1.call-done, bf16[2048,1024]{1,0:T(8,128)(2,1)} %constant_dynamic-update-slice_fusion.9), kind=kOutput, calls=%fused_computation.25 | convolution fusion | flops 10740039680 | bytes 19922944 | tf_op jit(solution)/shard_map/dot_general | solution.py:43
  272.4 16.9 %convolution_convert_fusion.2.dn_ref = bf16[2560,1024]{1,0:T(8,128)(2,1)} fusion(bf16[2560,2048]{1,0:T(8,128)(2,1)} %all-gather.5.cloned.1.call-done, bf16[1024,2048]{1,0:T(8,128)(2,1)} %constant_dynamic-update-slice_fusion.19), kind=kOutput, calls=%fused_computation.24 | convolution fusion | flops 10740039680 | bytes 19922944 | tf_op jit(solution)/shard_map/dot_general | solution.py:39
  289.8 13.7 %gate_stats.1 = f32[8,2560]{1,0:T(8,128)} custom-call(s32[8]{0:T(128)} %iota.29.order_ref, bf16[2560,1024]{1,0:T(8,128)(2,1)} %get-tuple-element.196.y_ref, bf16[2560,1024]{1,0:T(8,128)(2,1)} %convolution_convert_fusion.3.z_ref, bf16[2560,1024]{1,0:T(8,128)(2,1)} %convolution_convert_fusion.2.dn_ref, f32[8,1024]{1,0:T(8,128)} %concatenate.160.gain_ref), custom_call_target="tpu_custom_call" | custom-call | flops 3000000000 | bytes 16000000 | tf_op jit(solution)/shard_map/gate_stats/pallas_call | solution.py:544
  311.6 18.5 %gate_backward.1 = (bf16[2560,1024]{1,0:T(8,128)(2,1)}, bf16[2560,1024]{1,0:T(8,128)(2,1)}, bf16[2560,1024]{1,0:T(8,128)(2,1)}) custom-call(s32[8]{0:T(128)} %iota.28.order_ref, f32[8,2560]{1,0:T(8,128)} %add.368.st_ref, bf16[2560,1024]{1,0:T(8,128)(2,1)} %get-tuple-element.196.y_ref, bf16[2560,1024]{1,0:T(8,128)(2,1)} %convolution_convert_fusion.3.z_ref, ...), custom_call_target="tpu_custom_call" | custom-call | flops 6000000000 | bytes 32000000 | tf_op jit(solution)/shard_map/gate_backward/pallas_call | solution.py:563
  330.2 16.8 %convolution_convert_fusion.4 = bf16[1024,2048]{1,0:T(8,128)(2,1)} fusion(bf16[2560,1024]{1,0:T(8,128)(2,1)} %get-tuple-element.219, bf16[2560,2048]{1,0:T(8,128)(2,1)} %all-gather.5.cloned.1.call-done), kind=kOutput, calls=%fused_computation.38 | convolution fusion | flops 10739515392 | bytes 19922944 | tf_op jit(solution)/shard_map/dot_general | solution.py:47
  347.1 17.6 %fusion.76 = (bf16[2048,1024]{1,0:T(8,128)(2,1)S(1)}, f32[2048,1024]{1,0:T(8,128)}) fusion(bf16[2560,2048]{1,0:T(8,128)(2,1)} %all-gather.3.cloned.1.call-done, bf16[2560,1024]{1,0:T(8,128)(2,1)} %get-tuple-element.218.dz_ref), kind=kOutput, calls=%fused_computation.217 | convolution fusion | flops 10739515392 | bytes 28311552 | tf_op jit(solution)/shard_map/dot_general | solution.py:47
  366.8 16.6 %convolution_convert_fusion = bf16[2560,2048]{1,0:T(8,128)(2,1)} fusion(bf16[2560,1024]{1,0:T(8,128)(2,1)} %get-tuple-element.219, bf16[1024,2048]{1,0:T(8,128)(2,1)} %constant_dynamic-update-slice_fusion.19), kind=kOutput, calls=%fused_computation.1 | convolution fusion | flops 10742661120 | bytes 19922944 | tf_op jit(solution)/shard_map/dot_general | solution.py:43
  388.7 41.5 %ssd_backward.3 = (bf16[2560,2432]{1,0:T(8,128)(2,1)}, f32[8,1280]{1,0:T(8,128)}, f32[8,128]{1,0:T(8,128)}) custom-call(s32[2]{0:T(128)} %pad_add_fusion.1.steps_ref, f32[2560,1408]{1,0:T(8,128)} %fusion.77.p_ref, bf16[2560,1280]{1,0:T(8,128)(2,1)} %get-tuple-element.197.act_ref, bf16[2560,1280]{1,0:T(8,128)(2,1)} %get-tuple-element.198.slope_ref, ...), custom_call_target="tpu_custom_call" | custom-call | flops 20000000000 | bytes 18000000 | tf_op jit(solution)/shard_map/ssd_backward/pallas_call | solution.py:498
  430.3 19.5 %convolution_convert_fusion.1 = bf16[1280,2048]{1,0:T(8,128)(2,1)} fusion(bf16[2560,2432]{1,0:T(8,128)(2,1)} %get-tuple-element.233.refs_0_, s32[]{:T(128)S(6)} %select_n.256, bf16[2048,1024]{1,0:T(8,128)(2,1)S(1)} %copy-done.23, bf16[2048,1408]{1,0:T(8,128)(2,1)} %constant_dynamic-update-slice_fusion), kind=kOutput, calls=%fused_computation.3 | convolution fusion | flops 12773228544 | bytes 21430276 | tf_op jit(solution)/shard_map/dot_general | solution.py:39
  462.2 11.7 %collective-permute-done.37 = bf16[256,1024]{1,0:T(8,128)(2,1)S(1)} collective-permute-done((bf16[256,1024]{1,0:T(8,128)(2,1)}, bf16[256,1024]{1,0:T(8,128)(2,1)S(1)}, u32[]{:S(2)}, u32[]{:S(2)}) %collective-permute-start.37) | collective-permute-done | bytes 524320 | tf_op jit(solution)/shard_map/ppermute | solution.py:804
  480.3 22.5 %ssd_backward.4 = (bf16[2560,2432]{1,0:T(8,128)(2,1)}, f32[8,1280]{1,0:T(8,128)}, f32[8,128]{1,0:T(8,128)}) custom-call(s32[1]{0:T(128)} %bitcast.21.steps_ref, f32[2560,1408]{1,0:T(8,128)} %fusion.77.p_ref, bf16[2560,1280]{1,0:T(8,128)(2,1)} %get-tuple-element.197.act_ref, ...), custom_call_target="tpu_custom_call", output_to_operand_aliasing={{0}: (12, {})} | custom-call | flops 10000000000 | bytes 9000000 | tf_op jit(solution)/shard_map/ssd_backward/pallas_call | solution.py:498
  502.8 12.8 %add_convert_fusion = bf16[640,2048]{1,0:T(8,128)(2,1)} fusion(bf16[1280,2048]{1,0:T(8,128)(2,1)} %collective-permute-done.40, s32[]{:T(128)S(6)} %select_n.258, bf16[2560,2432]{1,0:T(8,128)(2,1)} %get-tuple-element.242.refs_0_, s32[]{:T(128)S(6)} %select_n.257, bf16[2048,1024]{1,0:T(8,128)(2,1)} %constant_dynamic-update-slice_fusion.9, ...), kind=kOutput, calls=%fused_computation.28 | convolution fusion | flops 6399197184 | bytes 18317320 | tf_op jit(solution)/shard_map/dot_general | solution.py:39
  517.1 22.9 %ssd_backward.5 = (bf16[2560,2432]{1,0:T(8,128)(2,1)}, f32[8,1280]{1,0:T(8,128)}, f32[8,128]{1,0:T(8,128)}) custom-call(s32[1]{0:T(128)} %bitcast.18.steps_ref, f32[2560,1408]{1,0:T(8,128)} %fusion.77.p_ref, bf16[2560,1280]{1,0:T(8,128)(2,1)} %get-tuple-element.197.act_ref, ...), custom_call_target="tpu_custom_call", output_to_operand_aliasing={{0}: (12, {})} | custom-call | flops 10000000000 | bytes 9000000 | tf_op jit(solution)/shard_map/ssd_backward/pallas_call | solution.py:498
  584.0 6.9 %fusion.4 = f32[256,1408]{1,0:T(8,128)} fusion(bf16[2560,2432]{1,0:T(8,128)(2,1)} %get-tuple-element.264, bf16[2560,2048]{1,0:T(8,128)(2,1)} %all-gather.3.cloned.1.call-done), kind=kOutput, calls=%fused_computation.8 | convolution fusion | flops 1845493760 | bytes 9961472 | tf_op jit(solution)/shard_map/dot_general | solution.py:47
  590.9 6.9 %fusion.2 = f32[256,1408]{1,0:T(8,128)} fusion(bf16[2560,2432]{1,0:T(8,128)(2,1)} %get-tuple-element.264, bf16[2560,2048]{1,0:T(8,128)(2,1)} %all-gather.3.cloned.1.call-done), kind=kOutput, calls=%fused_computation.6 | convolution fusion | flops 1845493760 | bytes 9961472 | tf_op jit(solution)/shard_map/dot_general | solution.py:47
  605.0 11.6 %convert_add_fusion.2 = f32[640,2048]{1,0:T(8,128)} fusion(bf16[1280,2048]{1,0:T(8,128)(2,1)} %collective-permute-done.40, s32[]{:T(128)S(6)} %select_n.261, bf16[2560,2432]{1,0:T(8,128)(2,1)S(1)} %bitcast.81, s32[]{:T(128)S(6)} %select_n.260, bf16[2048,1024]{1,0:T(8,128)(2,1)} %constant_dynamic-update-slice_fusion.9, ...), kind=kOutput, calls=%fused_computation.27 | convolution fusion | flops 6397886464 | bytes 20938760 | tf_op jit(solution)/shard_map/dot_general | solution.py:39
  (421 shorter events, 249.3 us)
Async XLA Ops:
  7.2 120.1 %all-gather.3.cloned.1.call-start = ((), (), s32[]{:S(2)}) async-start(), calls=%async_computation.2 | async-start | bytes 13107200 | tf_op jit(solution)/shard_map/all_gather | solution.py:924
  56.9 215.5 %all-gather.5.cloned.1.call-start = ((), (), s32[]{:S(2)}) async-start(), calls=%async_computation.3 | async-start | bytes 13107200 | tf_op jit(solution)/shard_map/all_gather | solution.py:924
  127.3 505.2 %reduce-scatter.5.cloned.1.call-start = ((), (), s32[]{:S(2)}) async-start(), calls=%async_computation.5 | async-start | bytes 4718592 | tf_op jit(solution)/shard_map/reduce_scatter | solution.py:1067
  136.8 26.6 %collective-permute-start.15 = (bf16[256,1024]{1,0:T(8,128)(2,1)S(1)}, bf16[256,1024]{1,0:T(8,128)(2,1)S(1)}, u32[]{:S(2)}, u32[]{:S(2)}) collective-permute-start(bf16[256,1024]{1,0:T(8,128)(2,1)S(1)} %copy-done.20), channel_id=1, source_target_pairs={{0,4},{8,0},{16,8},{24,16},{28,24},{20,28},{12,20},{4,12},{1,5},{9... | collective-permute-start | bytes 1572872 | tf_op jit(solution)/shard_map/ppermute | solution.py:804
  138.3 25.1 %collective-permute-start.14 = (bf16[256,1024]{1,0:T(8,128)(2,1)S(1)}, bf16[256,1024]{1,0:T(8,128)(2,1)S(1)}, u32[]{:S(2)}, u32[]{:S(2)}) collective-permute-start(bf16[256,1024]{1,0:T(8,128)(2,1)S(1)} %copy-done.20), channel_id=1, source_target_pairs={{0,8},{8,16},{16,24},{24,28},{28,20},{20,12},{12,4},{4,0},{1,9},{9... | collective-permute-start | bytes 1572872 | tf_op jit(solution)/shard_map/ppermute | solution.py:801
  163.3 26.3 %collective-permute-start.18 = (bf16[256,1024]{1,0:T(8,128)(2,1)S(1)}, bf16[256,1024]{1,0:T(8,128)(2,1)S(1)}, u32[]{:S(2)}, u32[]{:S(2)}) collective-permute-start(bf16[256,1024]{1,0:T(8,128)(2,1)S(1)} %collective-permute-done.14), channel_id=1, source_target_pairs={{0,8},{8,16},{16,24},{24,28},{28,20},{20,12},{12,4},{4,0},{1,9},{9... | collective-permute-start | bytes 1572872 | tf_op jit(solution)/shard_map/ppermute | solution.py:801
  163.9 25.8 %collective-permute-start.19 = (bf16[256,1024]{1,0:T(8,128)(2,1)S(1)}, bf16[256,1024]{1,0:T(8,128)(2,1)S(1)}, u32[]{:S(2)}, u32[]{:S(2)}) collective-permute-start(bf16[256,1024]{1,0:T(8,128)(2,1)S(1)} %collective-permute-done.15), channel_id=1, source_target_pairs={{0,4},{8,0},{16,8},{24,16},{28,24},{20,28},{12,20},{4,12},{1,5},{9... | collective-permute-start | bytes 1572872 | tf_op jit(solution)/shard_map/ppermute | solution.py:804
  165.4 24.3 %collective-permute-start.20 = (bf16[128,2048]{1,0:T(8,128)(2,1)S(1)}, bf16[128,2048]{1,0:T(8,128)(2,1)S(1)}, u32[]{:S(2)}, u32[]{:S(2)}) collective-permute-start(bf16[128,2048]{1,0:T(8,128)(2,1)S(1)} %collective-permute-done.16), channel_id=1, source_target_pairs={{0,8},{8,16},{16,24},{24,28},{28,20},{20,12},{12,4},{4,0},{1,9},{9... | collective-permute-start | bytes 1572872 | tf_op jit(solution)/shard_map/ppermute | solution.py:801
  189.7 27.3 %collective-permute-start.22 = (bf16[256,1024]{1,0:T(8,128)(2,1)S(1)}, bf16[256,1024]{1,0:T(8,128)(2,1)S(1)}, u32[]{:S(2)}, u32[]{:S(2)}) collective-permute-start(bf16[256,1024]{1,0:T(8,128)(2,1)S(1)} %collective-permute-done.18), channel_id=1, source_target_pairs={{0,8},{8,16},{16,24},{24,28},{28,20},{20,12},{12,4},{4,0},{1,9},{9... | collective-permute-start | bytes 1572872 | tf_op jit(solution)/shard_map/ppermute | solution.py:801
  190.3 26.7 %collective-permute-start.23 = (bf16[256,1024]{1,0:T(8,128)(2,1)S(1)}, bf16[256,1024]{1,0:T(8,128)(2,1)S(1)}, u32[]{:S(2)}, u32[]{:S(2)}) collective-permute-start(bf16[256,1024]{1,0:T(8,128)(2,1)S(1)} %collective-permute-done.19), channel_id=1, source_target_pairs={{0,4},{8,0},{16,8},{24,16},{28,24},{20,28},{12,20},{4,12},{1,5},{9... | collective-permute-start | bytes 1572872 | tf_op jit(solution)/shard_map/ppermute | solution.py:804
  191.8 25.2 %collective-permute-start.24 = (bf16[128,2048]{1,0:T(8,128)(2,1)S(1)}, bf16[128,2048]{1,0:T(8,128)(2,1)S(1)}, u32[]{:S(2)}, u32[]{:S(2)}) collective-permute-start(bf16[128,2048]{1,0:T(8,128)(2,1)S(1)} %collective-permute-done.20), channel_id=1, source_target_pairs={{0,8},{8,16},{16,24},{24,28},{28,20},{20,12},{12,4},{4,0},{1,9},{9... | collective-permute-start | bytes 1572872 | tf_op jit(solution)/shard_map/ppermute | solution.py:801
  192.3 24.7 %collective-permute-start.25 = (bf16[128,2048]{1,0:T(8,128)(2,1)S(1)}, bf16[128,2048]{1,0:T(8,128)(2,1)S(1)}, u32[]{:S(2)}, u32[]{:S(2)}) collective-permute-start(bf16[128,2048]{1,0:T(8,128)(2,1)S(1)} %collective-permute-done.21), channel_id=1, source_target_pairs={{0,4},{8,0},{16,8},{24,16},{28,24},{20,28},{12,20},{4,12},{1,5},{9... | collective-permute-start | bytes 1572872 | tf_op jit(solution)/shard_map/ppermute | solution.py:804
  217.1 25.5 %collective-permute-start.29 = (bf16[64,2048]{1,0:T(8,128)(2,1)S(1)}, bf16[64,2048]{1,0:T(8,128)(2,1)S(1)}, u32[]{:S(2)}, u32[]{:S(2)}) collective-permute-start(bf16[64,2048]{1,0:T(8,128)(2,1)S(1)} %slice.299), channel_id=1, source_target_pairs={{0,4},{8,0},{16,8},{24,16},{28,24},{20,28},{12,20},{4,12},{1,5},{9... | collective-permute-start | bytes 786440 | tf_op jit(solution)/shard_map/ppermute | solution.py:804
  218.6 24.0 %collective-permute-start.28 = (bf16[64,2048]{1,0:T(8,128)(2,1)S(1)}, bf16[64,2048]{1,0:T(8,128)(2,1)S(1)}, u32[]{:S(2)}, u32[]{:S(2)}) collective-permute-start(bf16[64,2048]{1,0:T(8,128)(2,1)S(1)} %slice.298), channel_id=1, source_target_pairs={{0,8},{8,16},{16,24},{24,28},{28,20},{20,12},{12,4},{4,0},{1,9},{9... | collective-permute-start | bytes 786440 | tf_op jit(solution)/shard_map/ppermute | solution.py:801
  347.0 309.6 %reduce-scatter.3.cloned.1.call-start = ((), (), s32[]{:S(2)}) async-start(), calls=%async_computation.4 | async-start | bytes 13107200 | tf_op jit(solution)/shard_map/reduce_scatter | solution.py:1067
  385.8 44.4 %collective-permute-start.34 = (bf16[256,1024]{1,0:T(8,128)(2,1)S(1)}, bf16[256,1024]{1,0:T(8,128)(2,1)S(1)}, u32[]{:S(2)}, u32[]{:S(2)}) collective-permute-start(bf16[256,1024]{1,0:T(8,128)(2,1)S(1)} %pad_maximum_fusion.5), channel_id=1, source_target_pairs={{0,8},{8,16},{16,24},{24,28},{28,20},{20,12},{12,4},{4,0},{1,9},{9... | collective-permute-start | bytes 1572872 | tf_op jit(solution)/shard_map/ppermute | solution.py:801
  385.9 44.3 %collective-permute-start.35 = (bf16[256,1024]{1,0:T(8,128)(2,1)S(1)}, bf16[256,1024]{1,0:T(8,128)(2,1)S(1)}, u32[]{:S(2)}, u32[]{:S(2)}) collective-permute-start(bf16[256,1024]{1,0:T(8,128)(2,1)S(1)} %pad_maximum_fusion.6), channel_id=1, source_target_pairs={{0,4},{8,0},{16,8},{24,16},{28,24},{20,28},{12,20},{4,12},{1,5},{9... | collective-permute-start | bytes 1572872 | tf_op jit(solution)/shard_map/ppermute | solution.py:804
  449.8 53.0 %collective-permute-start.40 = (bf16[1280,2048]{1,0:T(8,128)(2,1)}, bf16[1280,2048]{1,0:T(8,128)(2,1)}, u32[]{:S(2)}, u32[]{:S(2)}) collective-permute-start(bf16[1280,2048]{1,0:T(8,128)(2,1)} %convolution_convert_fusion.1), channel_id=1, source_target_pairs={{0,2},{2,0},{1,3},{3,1},{4,6},{6,4},{5,7},{7,5},{8,10},{10,8},{9,1... | collective-permute-start | bytes 15728648 | tf_op jit(solution)/shard_map/ppermute | solution.py:731
  478.3 37.4 %collective-permute-start.39 = (bf16[256,1024]{1,0:T(8,128)(2,1)S(1)}, bf16[256,1024]{1,0:T(8,128)(2,1)S(1)}, u32[]{:S(2)}, u32[]{:S(2)}) collective-permute-start(bf16[256,1024]{1,0:T(8,128)(2,1)S(1)} %get-tuple-element.280), channel_id=1, source_target_pairs={{0,4},{8,0},{16,8},{24,16},{28,24},{20,28},{12,20},{4,12},{1,5},{9... | collective-permute-start | bytes 1572872 | tf_op jit(solution)/shard_map/ppermute | solution.py:804
  478.7 36.9 %collective-permute-start.38 = (bf16[256,1024]{1,0:T(8,128)(2,1)S(1)}, bf16[256,1024]{1,0:T(8,128)(2,1)S(1)}, u32[]{:S(2)}, u32[]{:S(2)}) collective-permute-start(bf16[256,1024]{1,0:T(8,128)(2,1)S(1)} %get-tuple-element.281), channel_id=1, source_target_pairs={{0,8},{8,16},{16,24},{24,28},{28,20},{20,12},{12,4},{4,0},{1,9},{9... | collective-permute-start | bytes 1572872 | tf_op jit(solution)/shard_map/ppermute | solution.py:801
  550.8 84.4 %collective-permute-start.47 = (bf16[640,2048]{1,0:T(8,128)(2,1)}, bf16[640,2048]{1,0:T(8,128)(2,1)}, u32[]{:S(2)}, u32[]{:S(2)}) collective-permute-start(bf16[640,2048]{1,0:T(8,128)(2,1)} %add_convert_fusion), channel_id=1, source_target_pairs={{0,1},{1,0},{2,3},{3,2},{4,5},{5,4},{6,7},{7,6},{8,9},{9,8},{10,11... | collective-permute-start | bytes 7864328 | tf_op jit(solution)/shard_map/ppermute | solution.py:727
  551.7 24.5 %collective-permute-start.41 = (bf16[128,1024]{1,0:T(8,128)(2,1)S(1)}, bf16[128,1024]{1,0:T(8,128)(2,1)S(1)}, u32[]{:S(2)}, u32[]{:S(2)}) collective-permute-start(bf16[128,1024]{1,0:T(8,128)(2,1)S(1)} %get-tuple-element.299), channel_id=1, source_target_pairs={{0,2},{2,0},{1,3},{3,1},{4,6},{6,4},{5,7},{7,5},{8,10},{10,8},{9,1... | collective-permute-start | bytes 786440 | tf_op jit(solution)/shard_map/ppermute | solution.py:731
  578.4 52.8 %collective-permute-start.48 = (bf16[2,64,1024]{2,1,0:T(8,128)(2,1)}, bf16[2,64,1024]{2,1,0:T(8,128)(2,1)}, u32[]{:S(2)}, u32[]{:S(2)}) collective-permute-start(bf16[2,64,1024]{2,1,0:T(8,128)(2,1)} %dynamic-slice_bitcast_fusion.2), channel_id=1, source_target_pairs={{0,1},{1,0},{2,3},{3,2},{4,5},{5,4},{6,7},{7,6},{8,9},{9,8},{10,11... | collective-permute-start | bytes 786440 | tf_op jit(solution)/shard_map/ppermute | solution.py:727
  604.1 27.1 %collective-permute-start.49 = (f32[21952]{0:T(1024)S(1)}, f32[21952]{0:T(1024)S(1)}, u32[]{:S(2)}, u32[]{:S(2)}) collective-permute-start(f32[21952]{0:T(1024)S(1)} %add.399), channel_id=1, source_target_pairs={{0,4},{1,5},{2,6},{3,7},{4,0},{5,1},{6,2},{7,3},{8,12},{9,13},{10,... | collective-permute-start | bytes 263432 | tf_op jit(solution)/shard_map/ppermute | solution.py:875
  (86 other events, 1098.8 us)
Sparse Core Ops, SparseCore 0:
  57.0 70.1 all-gather.2
  128.8 70.1 all-gather.4
  347.2 98.9 reduce-scatter.4
  462.3 84.1 reduce-scatter.2

commit v3 on v2

--- a/solution.py
+++ b/solution.py
@@ -185,17 +185,17 @@
 
 
 def bwd_kernel(
-    steps_ref, p_ref, act_ref, slope_ref, dy_ref, dz_ref, h_ref, cw_ref, hp_ref, dsk_ref, seg_ref, bc_ref, *refs
+    steps_ref, p_ref, act_ref, slope_ref, dy_ref, dz_ref, h_ref, cw_ref, hp_ref, dsk_ref, seg_ref, bc_ref, sofar_ref, *refs
 ):
-    dp_ref, acc_ref, hacc_ref = refs[-18:-15]
+    dp_ref, acc_ref = refs[-17:-15]
+    heads_at = slice(XBC, XCOLS)
     dt_s, parts_s, grow_s, ct_s, gt_s, dgt_s, kc_s, kr_s, fold_s, dbc_s, ds_s, da_s, dst_s, after_s, sums_s = refs[-15:]
     lane = lane_index()
     head_row = lax.broadcasted_iota(jnp.int32, (LOCAL_HEADS, 1), 0)
 
     @pl.when(pl.program_id(0) == 0)
     def _():
-        acc_ref[...] = jnp.zeros_like(acc_ref)
-        hacc_ref[...] = jnp.zeros_like(hacc_ref)
+        acc_ref[...] = sofar_ref[...]
 
     rate = hp_ref[1:2]
     dt_s[...] = softplus(p_ref[:, XBC:] + hp_ref[0:1])
@@ -319,7 +319,7 @@
         da_s[rows, WIDTH + STATE :] = dc
         d_rate = running_sum(d_cum, False)
         dst_s[rows, :] = d_dt + d_rate * rate
-        hacc_ref[1:2, :] += jnp.sum(d_rate * dt, axis=0, keepdims=True)
+        acc_ref[1:2, heads_at] += jnp.sum(d_rate * dt, axis=0, keepdims=True)
 
     block(0, HEAD, False, False)
     block(HEAD + SPAN, SPAN, True, False)
@@ -327,7 +327,7 @@
 
     d_soft = dst_s[...] * jax.nn.sigmoid(p_ref[:, XBC:] + hp_ref[0:1])
     d_soft = jnp.where(lane < LOCAL_HEADS, d_soft, 0.0)
-    hacc_ref[0:1, :] += jnp.sum(d_soft, axis=0, keepdims=True)
+    acc_ref[0:1, heads_at] += jnp.sum(d_soft, axis=0, keepdims=True)
     dp_ref[:, XBC:XCOLS] = d_soft.astype(BF)
     dp_ref[:, XCOLS:] = dz_ref[...]
     sums_s[...] = jnp.zeros_like(sums_s)
@@ -356,7 +356,7 @@
 
     lax.fori_loop(0, TILE // ROWS, conv_step, 0)
     for k in range(KERNEL + 1):
-        acc_ref[k : k + 1, :] += jnp.sum(sums_s[k], axis=0, keepdims=True)
+        acc_ref[k : k + 1, :XBC] += jnp.sum(sums_s[k], axis=0, keepdims=True)
 
 
 def stats_kernel(order_ref, y_ref, z_ref, dn_ref, gain_ref, st_ref, both_s):
@@ -491,10 +491,10 @@
     )(jnp.stack(steps).astype(jnp.int32), proj, conv_w, conv_b, heads, skip, seg, spread, *more)
 
 
-def ssd_backward(steps, proj, act, slope, dy, dz, states, conv_w, conv_b, heads, skip, seg, spread, earlier=()):
+def ssd_backward(steps, proj, act, slope, dy, dz, states, conv_w, conv_b, heads, skip, seg, spread, sofar, earlier=()):
     tokens = proj.shape[0]
     count = len(steps)
-    more, more_specs, aliases = onto(earlier, 12)
+    more, more_specs, aliases = onto(earlier, 13)
     return pl.pallas_call(
         bwd_kernel,
         grid_spec=pltpu.PrefetchScalarGridSpec(
@@ -503,9 +503,9 @@
             in_specs=[
                 placed(XCOLS), placed(XBC), placed(XBC), placed(WIDTH), placed(WIDTH), STATES, whole((8, XBC)),
                 whole((8, 128)), whole((8, WIDTH)), whole((128, WIDTH)), whole((128, 128 * LOCAL_HEADS)),
-                *more_specs,
+                whole((8, XCOLS)), *more_specs,
             ],
-            out_specs=[placed(XCOLS + WIDTH), whole((8, XBC)), whole((8, 128))],
+            out_specs=[placed(XCOLS + WIDTH), whole((8, XCOLS))],
             scratch_shapes=[
                 pltpu.VMEM((TILE, 128), F32),
                 pltpu.VMEM((SPAN, 128), BF),
@@ -526,8 +526,7 @@
         ),
         out_shape=[
             jax.ShapeDtypeStruct((tokens, XCOLS + WIDTH), BF),
-            jax.ShapeDtypeStruct((8, XBC), F32),
-            jax.ShapeDtypeStruct((8, 128), F32),
+            jax.ShapeDtypeStruct((8, XCOLS), F32),
         ],
         input_output_aliases=aliases,
         compiler_params=params(),
@@ -535,7 +534,7 @@
             flops=count * 10 * 10**9, bytes_accessed=count * 9 * 10**6, transcendentals=count * 4 * 10**6
         ),
         name="ssd_backward",
-    )(jnp.stack(steps).astype(jnp.int32), proj, act, slope, dy, dz, states, conv_w, heads, skip, seg, spread, *more)
+    )(jnp.stack(steps).astype(jnp.int32), proj, act, slope, dy, dz, states, conv_w, heads, skip, seg, spread, sofar, *more)
 
 
 def gate_stats(order, y, z, dn, gain):
@@ -593,38 +592,36 @@
     )(order, *values, gain)[0]
 
 
-def pack_kernel(at_ref, in_ref, dt_ref, small_ref, send_ref, keep_ref):
+def pack_kernel(at_ref, in_ref, dt_ref, small_ref, send_ref, keep_ref, z_send_ref, z_keep_ref):
     rows = in_ref.shape[0]
-    send_ref[:, rows:, :] = jnp.zeros((2, 8, XCOLS + WIDTH), BF)
+    send_ref[:, rows:, :] = jnp.zeros((2, 8, XCOLS), BF)
     send_ref[0, rows:, :] = small_ref[...]
     source = lax.broadcasted_iota(jnp.int32, (HEADS, 128), 0)
     lane = lax.broadcasted_iota(jnp.int32, (HEADS, 128), 1)
-    for out_ref, x in ((send_ref, 1 - at_ref[0]), (keep_ref, at_ref[0])):
+    for x_ref, z_ref, x in ((send_ref, z_send_ref, 1 - at_ref[0]), (keep_ref, z_keep_ref, at_ref[0])):
         for core in range(2):
             slot = 2 * core + x
             for k in range(AHEADS):
+                cols = slice(k * 128, k * 128 + 128)
                 at = (k * SLOTS + slot) * 128
-                out_ref[core, :rows, XCOLS + k * 128 : XCOLS + k * 128 + 128] = in_ref[
-                    :, pl.ds(pl.multiple_of(at, 128), 128)
-                ]
-                out_ref[core, :rows, k * 128 : k * 128 + 128] = in_ref[
-                    :, pl.ds(pl.multiple_of(DI + at, 128), 128)
-                ]
-            out_ref[core, :rows, WIDTH:XBC] = in_ref[:, 2 * DI :]
+                z_ref[core, :, cols] = in_ref[:, pl.ds(pl.multiple_of(at, 128), 128)]
+                x_ref[core, :rows, cols] = in_ref[:, pl.ds(pl.multiple_of(DI + at, 128), 128)]
+            x_ref[core, :rows, WIDTH:XBC] = in_ref[:, 2 * DI :]
             wanted = jnp.where(lane < LOCAL_HEADS, (lane // 2) * 8 + slot * 2 + lane % 2, -1)
-            out_ref[core, :rows, XBC:XCOLS] = nn(
+            x_ref[core, :rows, XBC:XCOLS] = nn(
                 dt_ref[...], jnp.where(source == wanted, 1.0, 0.0).astype(BF)
             ).astype(BF)
 
 
 def pack_weights(xi, in_w, dt_w, small):
     rows = in_w.shape[0]
-    small = pad_rows(pad_cols(small[None], XCOLS + WIDTH))
+    small = pad_rows(pad_cols(small[None], XCOLS))
+    shapes = [(2, rows + 8, XCOLS), (2, rows, XCOLS), (2, rows, WIDTH), (2, rows, WIDTH)]
     return pl.pallas_call(
         pack_kernel,
         in_specs=[pl.BlockSpec(memory_space=pltpu.SMEM)] + [pl.BlockSpec(memory_space=pltpu.VMEM)] * 3,
-        out_specs=[pl.BlockSpec(memory_space=pltpu.VMEM)] * 2,
-        out_shape=[jax.ShapeDtypeStruct((2, r, XCOLS + WIDTH), BF) for r in (rows + 8, rows)],
+        out_specs=[pl.BlockSpec(memory_space=pltpu.VMEM)] * 4,
+        out_shape=[jax.ShapeDtypeStruct(shape, BF) for shape in shapes],
         cost_estimate=pl.CostEstimate(flops=10**8, bytes_accessed=3 * 10**6, transcendentals=0),
         name="pack_weights",
     )(xi[None].astype(jnp.int32), in_w, dt_w, small)
@@ -651,21 +648,18 @@
     )(jnp.stack([xi, ci]).astype(jnp.int32), keep, got)
 
 
-def place_kernel(at_ref, stay_ref, got_ref, x_ref, z_ref):
+def place_kernel(at_ref, stay_ref, got_ref, out_ref):
     rows = stay_ref.shape[0]
     for index, ref in ((at_ref[0], stay_ref), (1 - at_ref[0], got_ref)):
-        at = pl.ds(pl.multiple_of(index * rows, rows), rows)
-        x_ref[at, :] = ref[:, :XCOLS]
-        z_ref[at, :] = ref[:, XCOLS:]
+        out_ref[pl.ds(pl.multiple_of(index * rows, rows), rows), :] = ref[...]
 
 
 def place_rows(index, stay, got):
-    rows = 2 * stay.shape[0]
     return pl.pallas_call(
         place_kernel,
         in_specs=[pl.BlockSpec(memory_space=pltpu.SMEM)] + [pl.BlockSpec(memory_space=pltpu.VMEM)] * 2,
-        out_specs=[pl.BlockSpec(memory_space=pltpu.VMEM)] * 2,
-        out_shape=[jax.ShapeDtypeStruct((rows, XCOLS), BF), jax.ShapeDtypeStruct((rows, WIDTH), BF)],
+        out_specs=pl.BlockSpec(memory_space=pltpu.VMEM),
+        out_shape=jax.ShapeDtypeStruct((2 * stay.shape[0], stay.shape[1]), BF),
         cost_estimate=pl.CostEstimate(flops=0, bytes_accessed=2 * 10**6, transcendentals=0),
         name="place_rows",
     )(index[None].astype(jnp.int32), stay, got)
@@ -723,6 +717,70 @@
     )(xi[None].astype(jnp.int32), z_pair, z_got, x_pair, x_got, in_w, dt_w)
 
 
+def small_kernel(at_ref, own_ref, x_ref, far_ref, taps_ref, heads_ref):
+    xi, ci = at_ref[0], at_ref[1]
+    terms = (
+        (2 * ci + xi, own_ref), (2 * ci + 1 - xi, x_ref),
+        (2 - 2 * ci + xi, far_ref.at[0]), (3 - 2 * ci - xi, far_ref.at[1]),
+    )
+    shared = jnp.zeros((8, 2 * STATE), F32)
+    heads = jnp.zeros((8, HEADS), F32)
+    source = lax.broadcasted_iota(jnp.int32, (128, HEADS), 0)
+    place = lax.broadcasted_iota(jnp.int32, (128, HEADS), 1)
+    row = lax.broadcasted_iota(jnp.int32, (8, 1), 0)
+    exact = functools.partial(
+        lax.dot_general,
+        dimension_numbers=(((1,), (0,)), ((), ())),
+        precision=lax.Precision.HIGHEST,
+        preferred_element_type=F32,
+    )
+    for slot, ref in terms:
+        for k in range(AHEADS):
+            cols = ref[:, k * 128 : k * 128 + 128]
+            taps_ref[:, pl.ds(pl.multiple_of((k * SLOTS + slot) * 128, 128), 128)] = cols
+            wanted = jnp.where(place == k * 8 + slot * 2 + source // HEAD_DIM, 1.0, 0.0)
+            heads = heads + exact(jnp.where(row == 5, cols, 0.0), wanted)
+        shared = shared + ref[:, WIDTH:XBC]
+        wanted = jnp.where(
+            (source < LOCAL_HEADS) & (place == (source // 2) * 8 + slot * 2 + source % 2), 1.0, 0.0
+        )
+        heads = heads + exact(jnp.where(row < 2, ref[:, XBC:], 0.0), wanted)
+    taps_ref[:, DI:] = shared
+    heads_ref[...] = heads
+
+
+def assemble_small(xi, ci, own, x, far):
+    return pl.pallas_call(
+        small_kernel,
+        in_specs=[pl.BlockSpec(memory_space=pltpu.SMEM)] + [pl.BlockSpec(memory_space=pltpu.VMEM)] * 3,
+        out_specs=[pl.BlockSpec(memory_space=pltpu.VMEM)] * 2,
+        out_shape=[jax.ShapeDtypeStruct((8, DI + 2 * STATE), F32), jax.ShapeDtypeStruct((8, HEADS), F32)],
+        cost_estimate=pl.CostEstimate(flops=10**7, bytes_accessed=10**6, transcendentals=0),
+        name="assemble_small",
+    )(jnp.stack([xi, ci]).astype(jnp.int32), own, x, far)
+
+
+def rows_kernel(order_ref, *refs):
+    rows = refs[0].shape[0]
+    out_ref = refs[-1]
+    for k, (ref, shift) in enumerate(zip(refs[:-1], (0, 0, 0, 0, 0, rows // 2, 0, 0, 0))):
+        at = order_ref[k if k < 5 else k - 1] * rows + shift
+        out_ref[pl.ds(pl.multiple_of(at, rows // 2), ref.shape[0]), :] = ref[...]
+
+
+def ordered_rows(order, blocks):
+    rows, cols = blocks[0].shape
+    return pl.pallas_call(
+        rows_kernel,
+        in_specs=[pl.BlockSpec(memory_space=pltpu.SMEM)] + [pl.BlockSpec(memory_space=pltpu.VMEM)] * len(blocks),
+        out_specs=pl.BlockSpec(memory_space=pltpu.VMEM),
+        out_shape=jax.ShapeDtypeStruct((AHEADS * rows, cols), BF),
+        compiler_params=params(),
+        cost_estimate=pl.CostEstimate(flops=0, bytes_accessed=8 * 10**6, transcendentals=0),
+        name="ordered_rows",
+    )(order, *blocks)
+
+
 def swap_x(v):
     return lax.ppermute(v, "x", SWAP)
 
@@ -821,14 +879,14 @@
         self.rights.append(r)
         self.lefts.append(l)
 
-    def blocks(self):
+    def pieces(self):
         r, l = self.rights, self.lefts
-        return [r[0], l[1], l[2], l[3], jnp.concatenate([r[4], l[4]], axis=0), r[3], r[2], r[1]]
+        return [r[0], l[1], l[2], l[3], r[4], l[4], r[3], r[2], r[1]]
 
 
 class Scatter:
-    def __init__(self, ring, block):
-        self.ring, self.block, self.count = ring, block, 0
+    def __init__(self, ring, block, chain):
+        self.ring, self.block, self.chain, self.count = ring, block, chain, 0
 
     def start(self):
         block, ring, k = self.block, self.ring, self.count
@@ -838,7 +896,7 @@
             half = far.shape[0] // 2
             sends = far[:half], far[half:]
         elif k == 1:
-            up, down = self.next
+            up, down = block(3), block(5)
             half = up.shape[0] // 2
             r, l = self.right.astype(F32), self.left.astype(F32)
             sends = (
@@ -846,15 +904,15 @@
                 jnp.concatenate([down[:half], down[half:] + l], axis=0),
             )
         else:
-            sends = self.next[0] + self.right.astype(F32), self.next[1] + self.left.astype(F32)
-        self.flying = ring.right(sends[0].astype(BF)), ring.left(sends[1].astype(BF))
-        self.next = (block(3 - k), block(5 + k)) if k < 3 else (block(0),)
+            sends = block(4 - k) + self.right.astype(F32), block(4 + k) + self.left.astype(F32)
+        sends = self.chain.mark((sends[0].astype(BF), sends[1].astype(BF)))
+        self.flying = ring.right(sends[0]), ring.left(sends[1])
 
     def land(self, chain):
         self.right, self.left = chain.take(self.flying)
 
     def total(self):
-        return self.next[0] + self.right.astype(F32) + self.left.astype(F32)
+        return self.block(0) + self.right.astype(F32) + self.left.astype(F32)
 
 
 def flat_index(sizes):
@@ -865,17 +923,16 @@
 
 
 class SmallSum:
-    def __init__(self, v, sizes):
+    def __init__(self, v):
         self.value = v
-        self.count = int(np.prod(sizes))
-        self.bits = [2, 4, 8, 16, 1]
+        self.bits = [1, 2, 4]
 
     def start(self):
         bit = self.bits.pop(0)
-        self.flying = lax.ppermute(self.value, ALL, [(i, i ^ bit) for i in range(self.count)])
+        self.flying = lax.ppermute(self.value, "ra", [(i, i ^ bit) for i in range(len(CYCLE))])
 
     def land(self, chain):
-        self.value = self.value + chain.take(self.flying)
+        self.value = chain.mark(self.value + chain.take(self.flying))
 
 
 def permute_blocks(v, order, width):
@@ -932,7 +989,7 @@
 
     if ringed:
         rows, n = in_w.shape[0], small.shape[0]
-        x_send, x_keep = chain.mark(pack_weights(xi, in_w, dt_w, small))
+        x_send, x_keep, z_send, z_keep = chain.mark(pack_weights(xi, in_w, dt_w, small))
         x_got = chain.take(swap_x(x_send))
         small = widen(small[None], x_got[0, rows : rows + 1, :n], 1)
         passing = stage(small, 2)
@@ -943,11 +1000,12 @@
         got = chain.take(got)
         small = widen(small, chain.take(passing), 4)
         passing = stage(small, 8)
-        x_block, z_block = chain.mark(place_rows(ci, stay, got))
+        x_block = chain.mark(place_rows(ci, stay, got))
         small = widen(small, chain.take(passing), 8)
         small = widen(small, chain.take(stage(small, 16)), 16)
         gather_x = Gather(ring, chain.tie(x_block))
         gather_x.start()
+        z_got = swap_x(chain.tie(z_send))
     else:
         small = lax.all_gather(small[None], ALL, axis=0, tiled=True)
     norm_full = pad_rows(small[:, ends[2] : ends[3]].reshape(1, -1).astype(F32))
@@ -980,7 +1038,10 @@
         & (head_rows % LOCAL_HEADS == np.arange(128 * LOCAL_HEADS)[None, :] // 128),
         BF,
     )
-    seq_params = (conv_taps, conv_bias, heads, skip, seg, spread)
+    gate_mine, *seq_params = chain.mark((gate_mine, conv_taps, conv_bias, heads, skip, seg, spread))
+    if ringed:
+        send, stay = chain.mark(pair_rows(xi, ci, z_keep, chain.take(z_got)))
+        z_block = chain.mark(place_rows(ci, stay, chain.take(swap_core(send))))
     slots = [jnp.int32(k) for k in range(SLOTS)]
 
     if ringed:
@@ -988,18 +1049,17 @@
         gather_x.start()
         gather_x.land(chain)
         gather_x.start()
+        gather_z = Gather(ring, z_block)
+        gather_z.start()
+        gather_z.land(chain)
         gather_x.land(chain)
-        o_block, z_block = chain.tie((out_w, z_block))
-        gather_o, gather_z = Gather(ring, o_block), Gather(ring, z_block)
-        both = gather_o, gather_z
-        gather_o.start()
-        gather_z.start()
-        w_x = chain.mark(jnp.concatenate(gather_x.blocks(), axis=0))
+        w_x = chain.mark(jnp.concatenate(gather_x.pieces(), axis=0))
         xh = chain.take(xh)
         dv = everyone(chain.tie(dv_own))
-        for gather in both:
-            gather.land(chain)
-            gather.start()
+        gather_z.start()
+        gather_o = Gather(ring, chain.tie(out_w))
+        gather_o.start()
+        both = gather_o, gather_z
         proj = chain.mark(nn(chain.tie(xh), w_x))
         for gather in both:
             gather.land(chain)
@@ -1011,12 +1071,11 @@
         y, act, slope, states = chain.mark(ssd_forward(slots[2:], chain.tie(proj), *seq_params, earlier=kept))
         for gather in both:
             gather.land(chain)
-        w_all = chain.mark(jnp.concatenate([w_x, jnp.concatenate(gather_z.blocks(), axis=0)], axis=1))
+        gather_o.start()
+        w_all = chain.mark(jnp.concatenate([w_x, jnp.concatenate(gather_z.pieces(), axis=0)], axis=1))
         z = chain.mark(nn(chain.tie(xh), w_all[:, XCOLS:]).astype(BF))
-        w_o = jnp.zeros((WIDTH, D), BF)
-        for k, block in enumerate(gather_o.blocks()):
-            w_o = lax.dynamic_update_slice(w_o, chain.tie(block), (order[k] * (WIDTH // AHEADS), 0))
-        w_o = chain.mark(w_o)
+        gather_o.land(chain)
+        w_o = chain.mark(ordered_rows(order, chain.tie(gather_o.pieces())))
         dv = chain.take(dv)
         dn = chain.mark(nt(dv, w_o).astype(BF))
     else:
@@ -1048,19 +1107,12 @@
         dx = chain.tie(dx)
         return nt(rows_of(dx, start, count), w_all)
 
-    here = (jnp.arange(SLOTS) == slot).astype(F32)
-    spread_cols = lambda v: (v.reshape(v.shape[0], AHEADS, 1, -1) * here[:, None]).reshape(v.shape[0], -1)
-
-    def small_terms(acc, hacc):
-        conv_part = jnp.concatenate([spread_cols(acc[:5, :WIDTH]), acc[:5, WIDTH:]], axis=1)
-        skip_part = jnp.sum(acc[5, :WIDTH].reshape(LOCAL_HEADS, HEAD_DIM), axis=1)
-        head_part = spread_cols(jnp.stack([hacc[0, :LOCAL_HEADS], hacc[1, :LOCAL_HEADS], skip_part]))
-        return jnp.concatenate([conv_part.reshape(-1), head_part.reshape(-1)])
-
-    def backward_call(steps, earlier):
+    def backward_call(steps, sofar, earlier):
         return chain.mark(
-            ssd_backward(steps, chain.tie(proj), act, slope, dy, dz, states, *seq_params, earlier=earlier)
+            ssd_backward(steps, chain.tie(proj), act, slope, dy, dz, states, *seq_params, sofar, earlier=earlier)
         )
+
+    none_yet = jnp.zeros((8, XCOLS), F32)
 
     far, mid = 2 * (1 - ci), 2 * ci + 1 - xi
     g_out = chain.mark(tn(n, dv).astype(BF))
@@ -1069,7 +1121,7 @@
         own_out = reduced(g_out, "ra").astype(F32)
         g_z = chain.mark(tn(chain.tie(xh), dz))
         blocks_z = g_z.reshape(AHEADS, -1, WIDTH)
-        scatter_z = Scatter(ring, lambda k: blocks_z[k])
+        scatter_z = Scatter(ring, lambda k: blocks_z[k], chain)
         scatter_z.start()
     else:
         g_z = tn(xh, dz)
@@ -1078,56 +1130,63 @@
     if ringed:
         scatter_z.land(chain)
         scatter_z.start()
-        dx, acc, hacc = backward_call([far, far + 1], ())
+        dx, acc = backward_call([far, far + 1], none_yet, ())
         scatter_z.land(chain)
         scatter_z.start()
         far_u = swap_core(chain.mark(unit_product(dx, far, 2).astype(BF)))
+        dx, acc = backward_call([mid], acc, (chain.tie(dx),))
         scatter_z.land(chain)
         scatter_z.start()
-        dx, acc2, hacc2 = backward_call([mid], (chain.tie(dx),))
-        acc, hacc = acc + acc2, hacc + hacc2
         far_u = chain.take(far_u)
         mid_u = chain.mark(
             (unit_product(dx, mid, 1) + rows_of(far_u, 1 - xi, 1).astype(F32)).astype(BF)
         )
         mid_u = swap_x(mid_u)
+        dx, acc = backward_call([slot], acc, (chain.tie(dx),))
         scatter_z.land(chain)
         back_z = Return(chain.mark(scatter_z.total()))
-        dx, acc2, hacc2 = backward_call([slot], (chain.tie(dx),))
-        acc, hacc = acc + acc2, hacc + hacc2
-        scatter_x = Scatter(
-            ring, lambda k: chain.mark(tn(xh[:, k * feature : (k + 1) * feature], chain.tie(dx)[:, :XCOLS]))
-        )
+
+        def blocks_x(first, last):
+            part = tn(xh[:, first * feature : last * feature], chain.tie(dx)[:, :XCOLS])
+            return dict(enumerate(chain.mark(part).reshape(last - first, feature, XCOLS), first))
+
+        made = blocks_x(3, 6)
+        scatter_x = Scatter(ring, lambda k: made[k], chain)
         scatter_x.start()
+        made.update(blocks_x(0, 3))
+        scatter_x.land(chain)
+        scatter_x.start()
+        made.update(blocks_x(6, 8))
+        du_own = chain.mark(unit_product(dx, slot, 1) + rows_of(far_u, xi, 1).astype(F32))
         scatter_x.land(chain)
         scatter_x.start()
         back_z.turn(chain)
-        tally = SmallSum(small_terms(*chain.tie((acc, hacc))), sizes)
+        tally = SmallSum(chain.tie(acc))
         tally.start()
         scatter_x.land(chain)
         scatter_x.start()
         tally.land(chain)
         tally.start()
-        du_own = chain.mark(unit_product(dx, slot, 1) + rows_of(far_u, xi, 1).astype(F32))
-        scatter_x.land(chain)
-        scatter_x.start()
-        tally.land(chain)
-        tally.start()
-        back_z.land(chain)
         mid_u = chain.take(mid_u)
-        du = du_own + mid_u.astype(F32)
+        du = chain.mark(du_own + mid_u.astype(F32))
         scatter_x.land(chain)
         back_x = Return(chain.mark(scatter_x.total()))
         tally.land(chain)
         tally.start()
+        back_z.land(chain)
         back_x.turn(chain)
         tally.land(chain)
-        tally.start()
+        acc = tally.value
+        acc_x = chain.take(swap_x(acc))
+        acc_far = swap_core(jnp.stack([acc, acc_x]))
     else:
-        dx, acc, hacc = backward_call(slots, ())
+        dx, acc = backward_call(slots, none_yet, ())
         du = reduced(nt(dx, w_all), group)
         g_x = tn(xh, dx[:, :XCOLS])
-        total = lax.psum(small_terms(acc, hacc), ALL)
+        acc = lax.psum(acc, ("ra", "rb"))
+        acc_x = swap_x(acc)
+        acc_far = swap_core(jnp.stack([acc, acc_x]))
+        taps_total, head_total = assemble_small(xi, ci, acc, acc_x, acc_far)
     v_s, v_l = branch[:short].astype(F32), branch[short:].astype(F32)
     du_s, du_l = du[:short], du[short:]
 
@@ -1151,8 +1210,7 @@
             assemble_rows(xi, back_z.pair, back_z.got, back_x.pair, back_x.got, in_w, dt_w)
         )
         norm_sum = norm_sum[:, 0]
-        tally.land(chain)
-        total = tally.value
+        taps_total, head_total = assemble_small(xi, ci, acc, acc_x, chain.take(acc_far))
     else:
         here = (jnp.arange(SLOTS) == slot).astype(F32)
         wider = lambda v: (v.reshape(D, AHEADS, 1, -1) * here[:, None]).reshape(D, -1)
@@ -1170,9 +1228,7 @@
     grad_norm_gain = norm_sum / norm_gain.astype(F32)
     grad_gate_gain = jnp.sum(out_w.astype(F32) * own_out, axis=1) / gate_gain.astype(F32)
 
-    conv_total = total[: 5 * (DI + 2 * STATE)].reshape(5, -1)
-    head_total = total[5 * (DI + 2 * STATE) :].reshape(3, HEADS)
-    own_conv = lax.dynamic_slice(conv_total, (0, flat_index(sizes) * width), (5, width))
+    own_conv = lax.dynamic_slice(taps_total, (0, flat_index(sizes) * width), (KERNEL + 1, width))
     return (
         out_short,
         out_long,
@@ -1185,7 +1241,7 @@
         own_conv[KERNEL],
         head_total[0],
         head_total[1] * neg_rate,
-        head_total[2],
+        head_total[5],
         grad_gate_gain,
         own_out,
     )

time: 686 us -> 630 us (0.918)
  waiting for transfers between devices: 125 us -> 63.2 us
  matrix products: 191 us -> 177 us
  Pallas kernels: 176 us -> 187 us
  other arithmetic: 50.2 us -> 57.2 us
    ppermute x20, waiting for transfers between devices: 79 us -> 30.4 us  [left(): return lax.ppermute(v, 'ra', self.pairs(-1))]
    dot_general x10 -> x5, matrix products: 75.3 us -> 62.1 us  [tn(): lax.dot_general(a, b, (((0,), (0,)), ((), ())), preferred_element_type=F32)]
    pallas_call x0 -> x2, Pallas kernels: none -> 7.78 us  [the longest x1 4.41 us: ordered_rows(): pl.pallas_call(rows_kernel, in_specs=[pl.BlockSpec(memory_space=pltpu.SME...]
    ppermute x5 -> x7, waiting for transfers between devices: 18.7 us -> 12.6 us  [swap_x(): return lax.ppermute(v, 'x', SWAP)]
    unnamed x128 -> x143, local copies, waits for them, and re-layouts: 19.5 us -> 25 us
    convert_element_type x7 -> x6, other arithmetic: 14.5 us -> 15.1 us  [start(): sends = self.chain.mark((sends[0].astype(BF), sends[1].astype(BF)))]
  transfers between devices with their start and end apart: 63 -> 65, of which waited for: 29 -> 20; matrix products, arithmetic and copies ran while one was open for 36% -> 38% of each run, Pallas kernels for 20% -> 23%
where the time goes in v3:
time: 630 us; the launch traced here: 621 us
  Pallas kernels  187 us (30%)
  matrix products  177 us (28%)
  starting transfers between devices  63.8 us (10%)
  waiting for transfers between devices  63.2 us (10%)
  other arithmetic  57.2 us (9%)
  local copies, waits for them, and re-layouts  51.7 us (8%)
  between operations  20.4 us (3%)
    pallas_call x3, Pallas kernels, ssd_backward(): pl.pallas_call(bwd_kernel, grid_spec=pltpu.PrefetchScalarGridSpec(num_sca...  87 us
    dot_general x5, matrix products, tn(): lax.dot_general(a, b, (((0,), (0,)), ((), ())), preferred_element_type=F32)  62.1 us
    dot_general x4, matrix products, nt(): lax.dot_general(a, b, (((1,), (1,)), ((), ())), preferred_element_type=F32)  59.8 us
    dot_general x3, matrix products, nn(): lax.dot_general(a, b, (((1,), (0,)), ((), ())), preferred_element_type=F32)  55.6 us
    pallas_call x2, Pallas kernels, ssd_forward(): pl.pallas_call(fwd_kernel, grid_spec=pltpu.PrefetchScalarGridSpec(num_sca...  40.9 us
    ppermute x20, starting transfers between devices, left(): return lax.ppermute(v, 'ra', self.pairs(-1))  30.7 us
    ppermute x20, waiting for transfers between devices, left(): return lax.ppermute(v, 'ra', self.pairs(-1))  30.4 us
    unnamed x143, local copies, waits for them, and re-layouts  25 us
  transfers between devices with their start and end apart: 65, of which 20 were waited for; matrix products, arithmetic and copies ran while one was open for 38% of the time, Pallas kernels for 23%

profile of v3, /device:TPU:0, one launch (start us, length us, event | category | flops | bytes accessed | tf_op | source)
XLA Modules:
  0.0 621.2 jit_solution(7588405704087077157)
XLA Ops:
  15.4 8.9 %collective-permute-done.got_ref = bf16[2,72,1408]{2,1,0:T(8,128)(2,1)S(1)} collective-permute-done((bf16[2,72,1408]{2,1,0:T(8,128)(2,1)}, bf16[2,72,1408]{2,1,0:T(8,128)(2,1)S(1)}, u32[]{:S(2)}, u32[]{:S(2)}) %collective-permute-start) | collective-permute-done | bytes 405536 | tf_op jit(solution)/shard_map/ppermute | solution.py:785
  56.7 10.0 %collective-permute-done.7 = bf16[256,1408]{1,0:T(8,128)(2,1)} collective-permute-done((bf16[256,1408]{1,0:T(8,128)(2,1)S(1)}, bf16[256,1408]{1,0:T(8,128)(2,1)}, u32[]{:S(2)}, u32[]{:S(2)}) %collective-permute-start.7) | collective-permute-done | bytes 720928 | tf_op jit(solution)/shard_map/ppermute | solution.py:862
  92.7 13.3 %collective-permute-done.13 = bf16[256,1408]{1,0:T(8,128)(2,1)} collective-permute-done((bf16[256,1408]{1,0:T(8,128)(2,1)}, bf16[256,1408]{1,0:T(8,128)(2,1)}, u32[]{:S(2)}, u32[]{:S(2)}) %collective-permute-start.13) | collective-permute-done | bytes 720928 | tf_op jit(solution)/shard_map/ppermute | solution.py:862
  136.0 23.3 %fusion.66.p_ref = f32[2560,1408]{1,0:T(8,128)} fusion(bf16[2560,2048]{1,0:T(8,128)(2,1)} %all-gather.3.cloned.1.call-done, bf16[2048,1408]{1,0:T(8,128)(2,1)} %constant_dynamic-update-slice_fusion), kind=kOutput, calls=%fused_computation.187 | convolution fusion | flops 14763950080 | bytes 30670848 | tf_op jit(solution)/shard_map/dot_general | solution.py:43
  166.2 20.4 %ssd_forward.2 = (bf16[2560,1024]{1,0:T(8,128)(2,1)}, bf16[2560,1280]{1,0:T(8,128)(2,1)}, bf16[2560,1280]{1,0:T(8,128)(2,1)}, f32[4,128,1024]{2,1,0:T(8,128)}) custom-call(s32[2]{0:T(128)} %iota.26.steps_ref, f32[2560,1408]{1,0:T(8,128)} %fusion.66.p_ref, f32[8,1280]{1,0:T(8,128)} %concatenate.141.cw_ref, f32[8,1280]{1,0:T(8,128)} %select_maximum_fusion.cb_ref, ...), custom_call_target="tpu_custom_call" | custom-call | flops 8000000000 | bytes 12000000 | tf_op jit(solution)/shard_map/ssd_forward/pallas_call | solution.py:461
  190.8 20.5 %ssd_forward.3 = (bf16[2560,1024]{1,0:T(8,128)(2,1)}, bf16[2560,1280]{1,0:T(8,128)(2,1)}, bf16[2560,1280]{1,0:T(8,128)(2,1)}, f32[4,128,1024]{2,1,0:T(8,128)}) custom-call(s32[2]{0:T(128)} %constant.185.clone.1.steps_ref, f32[2560,1408]{1,0:T(8,128)} %fusion.66.p_ref, ...), custom_call_target="tpu_custom_call", output_to_operand_aliasing={{0}: (8, {}), {1}: (9, {}), {2}: (10, {}), {3}: (11, {})} | custom-call | flops 8000000000 | bytes 12000000 | tf_op jit(solution)/shard_map/ssd_forward/pallas_call | solution.py:461
  218.6 16.5 %convolution_convert_fusion.3.z_ref = bf16[2560,1024]{1,0:T(8,128)(2,1)} fusion(bf16[2560,2048]{1,0:T(8,128)(2,1)} %all-gather.3.cloned.1.call-done, bf16[2048,1024]{1,0:T(8,128)(2,1)} %constant_dynamic-update-slice_fusion.9), kind=kOutput, calls=%fused_computation.15 | convolution fusion | flops 10740039680 | bytes 19922944 | tf_op jit(solution)/shard_map/dot_general | solution.py:43
  241.0 16.5 %convolution_convert_fusion.2.dn_ref = bf16[2560,1024]{1,0:T(8,128)(2,1)} fusion(bf16[2560,2048]{1,0:T(8,128)(2,1)} %all-gather.5.cloned.1.call-done, bf16[1024,2048]{1,0:T(8,128)(2,1)} %ordered_rows.1), kind=kOutput, calls=%fused_computation.14 | convolution fusion | flops 10740039680 | bytes 19922944 | tf_op jit(solution)/shard_map/dot_general | solution.py:39
  258.1 13.8 %gate_stats.1 = f32[8,2560]{1,0:T(8,128)} custom-call(s32[8]{0:T(128)} %iota.24.order_ref, bf16[2560,1024]{1,0:T(8,128)(2,1)} %get-tuple-element.194.y_ref, bf16[2560,1024]{1,0:T(8,128)(2,1)} %convolution_convert_fusion.3.z_ref, bf16[2560,1024]{1,0:T(8,128)(2,1)} %convolution_convert_fusion.2.dn_ref, f32[8,1024]{1,0:T(8,128)} %concatenate.139.gain_ref), custom_call_target="tpu_custom_call" | custom-call | flops 3000000000 | bytes 16000000 | tf_op jit(solution)/shard_map/gate_stats/pallas_call | solution.py:543
  280.0 18.6 %gate_backward.1 = (bf16[2560,1024]{1,0:T(8,128)(2,1)}, bf16[2560,1024]{1,0:T(8,128)(2,1)}, bf16[2560,1024]{1,0:T(8,128)(2,1)}) custom-call(s32[8]{0:T(128)} %iota.23.order_ref, f32[8,2560]{1,0:T(8,128)} %add.318.st_ref, bf16[2560,1024]{1,0:T(8,128)(2,1)} %get-tuple-element.194.y_ref, bf16[2560,1024]{1,0:T(8,128)(2,1)} %convolution_convert_fusion.3.z_ref, ...), custom_call_target="tpu_custom_call" | custom-call | flops 6000000000 | bytes 32000000 | tf_op jit(solution)/shard_map/gate_backward/pallas_call | solution.py:562
  298.6 17.0 %convolution_convert_fusion.4 = bf16[1024,2048]{1,0:T(8,128)(2,1)} fusion(bf16[2560,1024]{1,0:T(8,128)(2,1)} %get-tuple-element.222, bf16[2560,2048]{1,0:T(8,128)(2,1)} %all-gather.5.cloned.1.call-done), kind=kOutput, calls=%fused_computation.30 | convolution fusion | flops 10739515392 | bytes 19922944 | tf_op jit(solution)/shard_map/dot_general | solution.py:47
  315.7 17.5 %fusion.64 = (bf16[2048,1024]{1,0:T(8,128)(2,1)S(1)}, f32[2048,1024]{1,0:T(8,128)}) fusion(bf16[2560,2048]{1,0:T(8,128)(2,1)} %all-gather.3.cloned.1.call-done, bf16[2560,1024]{1,0:T(8,128)(2,1)} %get-tuple-element.221.dz_ref), kind=kOutput, calls=%fused_computation.185 | convolution fusion | flops 10739515392 | bytes 28311552 | tf_op jit(solution)/shard_map/dot_general | solution.py:47
  335.3 15.7 %convolution_convert_fusion = bf16[2560,2048]{1,0:T(8,128)(2,1)} fusion(bf16[2560,1024]{1,0:T(8,128)(2,1)} %get-tuple-element.222, bf16[1024,2048]{1,0:T(8,128)(2,1)S(1)} %copy-done.8), kind=kOutput, calls=%fused_computation.1 | convolution fusion | flops 10742661120 | bytes 19922944 | tf_op jit(solution)/shard_map/dot_general | solution.py:43
  357.0 41.2 %ssd_backward.3 = (bf16[2560,2432]{1,0:T(8,128)(2,1)}, f32[8,1408]{1,0:T(8,128)}) custom-call(s32[2]{0:T(128)} %pad_add_fusion.1.steps_ref, f32[2560,1408]{1,0:T(8,128)} %fusion.66.p_ref, bf16[2560,1280]{1,0:T(8,128)(2,1)} %get-tuple-element.195.act_ref, bf16[2560,1280]{1,0:T(8,128)(2,1)} %get-tuple-element.196.slope_ref, ...), custom_call_target="tpu_custom_call" | custom-call | flops 20000000000 | bytes 18000000 | tf_op jit(solution)/shard_map/ssd_backward/pallas_call | solution.py:498
  400.9 20.2 %convolution_convert_fusion.1 = bf16[1280,2048]{1,0:T(8,128)(2,1)} fusion(bf16[2560,2432]{1,0:T(8,128)(2,1)} %get-tuple-element.233.refs_0_, s32[]{:T(128)S(6)} %select_n.224, bf16[2048,1024]{1,0:T(8,128)(2,1)} %constant_dynamic-update-slice_fusion.9, bf16[2048,1408]{1,0:T(8,128)(2,1)} %constant_dynamic-update-slice_fusion), kind=kOutput, calls=%fused_computation.3 | convolution fusion | flops 12773228544 | bytes 21430276 | tf_op jit(solution)/shard_map/dot_general | solution.py:39
  424.5 23.3 %ssd_backward.4 = (bf16[2560,2432]{1,0:T(8,128)(2,1)}, f32[8,1408]{1,0:T(8,128)}) custom-call(s32[1]{0:T(128)} %bitcast.11.steps_ref, f32[2560,1408]{1,0:T(8,128)} %fusion.66.p_ref, bf16[2560,1280]{1,0:T(8,128)(2,1)} %get-tuple-element.195.act_ref, bf16[2560,1280]{1,0:T(8,128)(2,1)} %get-tuple-element.196.slope_ref, ...), custom_call_target="tpu_custom_call", output_to_operand_aliasing={{0}: (13, {})} | custom-call | flops 10000000000 | bytes 9000000 | tf_op jit(solution)/shard_map/ssd_backward/pallas_call | solution.py:498
  452.7 11.5 %add_convert_fusion = bf16[640,2048]{1,0:T(8,128)(2,1)} fusion(bf16[1280,2048]{1,0:T(8,128)(2,1)} %collective-permute-done.38, s32[]{:T(128)S(6)} %select_n.226, bf16[2560,2432]{1,0:T(8,128)(2,1)} %get-tuple-element.241.refs_0_, s32[]{:T(128)S(6)} %select_n.225, bf16[2048,1024]{1,0:T(8,128)(2,1)S(1)} %copy-done.35, ...), kind=kOutput, calls=%fused_computation.18 | convolution fusion | flops 6399197184 | bytes 18317320 | tf_op jit(solution)/shard_map/dot_general | solution.py:39
  465.4 22.5 %ssd_backward.5 = (bf16[2560,2432]{1,0:T(8,128)(2,1)}, f32[8,1408]{1,0:T(8,128)}) custom-call(s32[1]{0:T(128)} %bitcast.10.steps_ref, f32[2560,1408]{1,0:T(8,128)} %fusion.66.p_ref, bf16[2560,1280]{1,0:T(8,128)(2,1)} %get-tuple-element.195.act_ref, bf16[2560,1280]{1,0:T(8,128)(2,1)} %get-tuple-element.196.slope_ref, ...), custom_call_target="tpu_custom_call", output_to_operand_aliasing={{0}: (13, {})} | custom-call | flops 10000000000 | bytes 9000000 | tf_op jit(solution)/shard_map/ssd_backward/pallas_call | solution.py:498
  490.3 10.4 %fusion.65 = (bf16[768,1408]{1,0:T(8,128)(2,1)S(1)}, f32[768,1408]{1,0:T(8,128)S(1)}) fusion(bf16[2560,2432]{1,0:T(8,128)(2,1)} %get-tuple-element.251, bf16[2560,2048]{1,0:T(8,128)(2,1)} %all-gather.3.cloned.1.call-done), kind=kOutput, calls=%fused_computation.186 | convolution fusion | flops 5537562624 | bytes 17629184 | tf_op jit(solution)/shard_map/dot_general | solution.py:47
  502.9 9.5 %fusion.2 = f32[768,1408]{1,0:T(8,128)} fusion(bf16[2560,2432]{1,0:T(8,128)(2,1)S(1)} %bitcast.72, bf16[2560,2048]{1,0:T(8,128)(2,1)} %all-gather.3.cloned.1.call-done), kind=kOutput, calls=%fused_computation.6 | convolution fusion | flops 5536481280 | bytes 15466496 | tf_op jit(solution)/shard_map/dot_general | solution.py:47
  515.6 7.7 %fusion = f32[512,1408]{1,0:T(8,128)} fusion(bf16[2560,2432]{1,0:T(8,128)(2,1)S(1)} %bitcast.72, bf16[2560,2048]{1,0:T(8,128)(2,1)} %all-gather.3.cloned.1.call-done), kind=kOutput, calls=%fused_computation.4 | convolution fusion | flops 3690987520 | bytes 12713984 | tf_op jit(solution)/shard_map/dot_general | solution.py:47
  523.4 11.6 %convert_add_fusion.2 = f32[640,2048]{1,0:T(8,128)} fusion(bf16[1280,2048]{1,0:T(8,128)(2,1)} %collective-permute-done.38, s32[]{:T(128)S(6)} %select_n.228, bf16[2560,2432]{1,0:T(8,128)(2,1)S(1)} %bitcast.72, s32[]{:T(128)S(6)} %select_n.227, bf16[2048,1024]{1,0:T(8,128)(2,1)} %constant_dynamic-update-slice_fusion.9, ...), kind=kOutput, calls=%fused_computation.17 | convolution fusion | flops 6397886464 | bytes 20938760 | tf_op jit(solution)/shard_map/dot_general | solution.py:39
  572.8 6.4 %collective-permute-done.54 = bf16[256,1408]{1,0:T(8,128)(2,1)} collective-permute-done((bf16[256,1408]{1,0:T(8,128)(2,1)}, bf16[256,1408]{1,0:T(8,128)(2,1)}, u32[]{:S(2)}, u32[]{:S(2)}) %collective-permute-start.54) | collective-permute-done | bytes 720928 | tf_op jit(solution)/shard_map/ppermute | solution.py:859
  592.1 6.1 fusion.12
  (401 shorter events, 218.3 us)
Async XLA Ops:
  7.2 123.4 %all-gather.3.cloned.1.call-start = ((), (), s32[]{:S(2)}) async-start(), calls=%async_computation.2 | async-start | bytes 13107200 | tf_op jit(solution)/shard_map/all_gather | solution.py:981
  50.2 190.9 %all-gather.5.cloned.1.call-start = ((), (), s32[]{:S(2)}) async-start(), calls=%async_computation.3 | async-start | bytes 13107200 | tf_op jit(solution)/shard_map/all_gather | solution.py:981
  54.2 24.2 %collective-permute-start.10 = (bf16[2,64,1024]{2,1,0:T(8,128)(2,1)}, bf16[2,64,1024]{2,1,0:T(8,128)(2,1)}, u32[]{:S(2)}, u32[]{:S(2)}) collective-permute-start(bf16[2,64,1024]{2,1,0:T(8,128)(2,1)} %get-tuple-element.160), channel_id=1, source_target_pairs={{0,1},{1,0},{2,3},{3,2},{4,5},{5,4},{6,7},{7,6},{8,9},{9,8},{10,11... | collective-permute-start | bytes 786440 | tf_op jit(solution)/shard_map/ppermute | solution.py:785
  89.0 28.3 %collective-permute-start.17 = (bf16[256,1024]{1,0:T(8,128)(2,1)}, bf16[256,1024]{1,0:T(8,128)(2,1)}, u32[]{:S(2)}, u32[]{:S(2)}) collective-permute-start(bf16[256,1024]{1,0:T(8,128)(2,1)} %place_rows.3), channel_id=1, source_target_pairs={{0,4},{8,0},{16,8},{24,16},{28,24},{20,28},{12,20},{4,12},{1,5},{9... | collective-permute-start | bytes 1572872 | tf_op jit(solution)/shard_map/ppermute | solution.py:862
  89.9 28.2 %collective-permute-start.16 = (bf16[256,1024]{1,0:T(8,128)(2,1)}, bf16[256,1024]{1,0:T(8,128)(2,1)S(1)}, u32[]{:S(2)}, u32[]{:S(2)}) collective-permute-start(bf16[256,1024]{1,0:T(8,128)(2,1)} %place_rows.3), channel_id=1, source_target_pairs={{0,8},{8,16},{16,24},{24,28},{28,20},{20,12},{12,4},{4,0},{1,9},{9... | collective-permute-start | bytes 1572872 | tf_op jit(solution)/shard_map/ppermute | solution.py:859
  130.6 435.3 %reduce-scatter.5.cloned.1.call-start = ((), (), s32[]{:S(2)}) async-start(), calls=%async_computation.5 | async-start | bytes 4718592 | tf_op jit(solution)/shard_map/reduce_scatter | solution.py:1119
  130.7 28.6 %collective-permute-start.18 = (bf16[256,1024]{1,0:T(8,128)(2,1)S(1)}, bf16[256,1024]{1,0:T(8,128)(2,1)S(1)}, u32[]{:S(2)}, u32[]{:S(2)}) collective-permute-start(bf16[256,1024]{1,0:T(8,128)(2,1)S(1)} %collective-permute-done.16), channel_id=1, source_target_pairs={{0,8},{8,16},{16,24},{24,28},{28,20},{20,12},{12,4},{4,0},{1,9},{9... | collective-permute-start | bytes 1572872 | tf_op jit(solution)/shard_map/ppermute | solution.py:859
  131.8 27.5 %collective-permute-start.19 = (bf16[256,1024]{1,0:T(8,128)(2,1)}, bf16[256,1024]{1,0:T(8,128)(2,1)S(1)}, u32[]{:S(2)}, u32[]{:S(2)}) collective-permute-start(bf16[256,1024]{1,0:T(8,128)(2,1)} %collective-permute-done.17), channel_id=1, source_target_pairs={{0,4},{8,0},{16,8},{24,16},{28,24},{20,28},{12,20},{4,12},{1,5},{9... | collective-permute-start | bytes 1572872 | tf_op jit(solution)/shard_map/ppermute | solution.py:862
  133.9 25.4 %collective-permute-start.21 = (bf16[128,2048]{1,0:T(8,128)(2,1)S(1)}, bf16[128,2048]{1,0:T(8,128)(2,1)S(1)}, u32[]{:S(2)}, u32[]{:S(2)}) collective-permute-start(bf16[128,2048]{1,0:T(8,128)(2,1)S(1)} %copy-done.11), channel_id=1, source_target_pairs={{0,4},{8,0},{16,8},{24,16},{28,24},{20,28},{12,20},{4,12},{1,5},{9... | collective-permute-start | bytes 1572872 | tf_op jit(solution)/shard_map/ppermute | solution.py:862
  159.3 27.3 %collective-permute-start.22 = (bf16[256,1024]{1,0:T(8,128)(2,1)S(1)}, bf16[256,1024]{1,0:T(8,128)(2,1)S(1)}, u32[]{:S(2)}, u32[]{:S(2)}) collective-permute-start(bf16[256,1024]{1,0:T(8,128)(2,1)S(1)} %collective-permute-done.18), channel_id=1, source_target_pairs={{0,8},{8,16},{16,24},{24,28},{28,20},{20,12},{12,4},{4,0},{1,9},{9... | collective-permute-start | bytes 1572872 | tf_op jit(solution)/shard_map/ppermute | solution.py:859
  160.4 26.2 %collective-permute-start.23 = (bf16[256,1024]{1,0:T(8,128)(2,1)S(1)}, bf16[256,1024]{1,0:T(8,128)(2,1)S(1)}, u32[]{:S(2)}, u32[]{:S(2)}) collective-permute-start(bf16[256,1024]{1,0:T(8,128)(2,1)S(1)} %collective-permute-done.19), channel_id=1, source_target_pairs={{0,4},{8,0},{16,8},{24,16},{28,24},{20,28},{12,20},{4,12},{1,5},{9... | collective-permute-start | bytes 1572872 | tf_op jit(solution)/shard_map/ppermute | solution.py:862
  161.4 25.2 %collective-permute-start.24 = (bf16[128,2048]{1,0:T(8,128)(2,1)S(1)}, bf16[128,2048]{1,0:T(8,128)(2,1)S(1)}, u32[]{:S(2)}, u32[]{:S(2)}) collective-permute-start(bf16[128,2048]{1,0:T(8,128)(2,1)S(1)} %collective-permute-done.20.refs_8_), channel_id=1, source_target_pairs={{0,8},{8,16},{16,24},{24,28},{28,20},{20,12},{12,4},{4,0},{1,9},{9... | collective-permute-start | bytes 1572872 | tf_op jit(solution)/shard_map/ppermute | solution.py:859
  162.5 24.1 %collective-permute-start.25 = (bf16[128,2048]{1,0:T(8,128)(2,1)S(1)}, bf16[128,2048]{1,0:T(8,128)(2,1)S(1)}, u32[]{:S(2)}, u32[]{:S(2)}) collective-permute-start(bf16[128,2048]{1,0:T(8,128)(2,1)S(1)} %collective-permute-done.21.refs_1_), channel_id=1, source_target_pairs={{0,4},{8,0},{16,8},{24,16},{28,24},{20,28},{12,20},{4,12},{1,5},{9... | collective-permute-start | bytes 1572872 | tf_op jit(solution)/shard_map/ppermute | solution.py:862
  186.7 25.5 %collective-permute-start.28 = (bf16[128,2048]{1,0:T(8,128)(2,1)S(1)}, bf16[128,2048]{1,0:T(8,128)(2,1)S(1)}, u32[]{:S(2)}, u32[]{:S(2)}) collective-permute-start(bf16[128,2048]{1,0:T(8,128)(2,1)S(1)} %collective-permute-done.24.refs_7_), channel_id=1, source_target_pairs={{0,8},{8,16},{16,24},{24,28},{28,20},{20,12},{12,4},{4,0},{1,9},{9... | collective-permute-start | bytes 1572872 | tf_op jit(solution)/shard_map/ppermute | solution.py:859
  187.8 24.4 %collective-permute-start.29 = (bf16[128,2048]{1,0:T(8,128)(2,1)S(1)}, bf16[128,2048]{1,0:T(8,128)(2,1)S(1)}, u32[]{:S(2)}, u32[]{:S(2)}) collective-permute-start(bf16[128,2048]{1,0:T(8,128)(2,1)S(1)} %collective-permute-done.25.refs_2_), channel_id=1, source_target_pairs={{0,4},{8,0},{16,8},{24,16},{28,24},{20,28},{12,20},{4,12},{1,5},{9... | collective-permute-start | bytes 1572872 | tf_op jit(solution)/shard_map/ppermute | solution.py:862
  315.6 276.5 %reduce-scatter.3.cloned.1.call-start = ((), (), s32[]{:S(2)}) async-start(), calls=%async_computation.4 | async-start | bytes 13107200 | tf_op jit(solution)/shard_map/reduce_scatter | solution.py:1119
  352.9 45.2 %collective-permute-start.36 = (bf16[256,1024]{1,0:T(8,128)(2,1)S(1)}, bf16[256,1024]{1,0:T(8,128)(2,1)S(1)}, u32[]{:S(2)}, u32[]{:S(2)}) collective-permute-start(bf16[256,1024]{1,0:T(8,128)(2,1)S(1)} %pad_maximum_fusion.4), channel_id=1, source_target_pairs={{0,8},{8,16},{16,24},{24,28},{28,20},{20,12},{12,4},{4,0},{1,9},{9... | collective-permute-start | bytes 1572872 | tf_op jit(solution)/shard_map/ppermute | solution.py:859
  353.6 44.6 %collective-permute-start.37 = (bf16[256,1024]{1,0:T(8,128)(2,1)S(1)}, bf16[256,1024]{1,0:T(8,128)(2,1)S(1)}, u32[]{:S(2)}, u32[]{:S(2)}) collective-permute-start(bf16[256,1024]{1,0:T(8,128)(2,1)S(1)} %pad_maximum_fusion.5), channel_id=1, source_target_pairs={{0,4},{8,0},{16,8},{24,16},{28,24},{20,28},{12,20},{4,12},{1,5},{9... | collective-permute-start | bytes 1572872 | tf_op jit(solution)/shard_map/ppermute | solution.py:862
  421.1 31.6 %collective-permute-start.38 = (bf16[1280,2048]{1,0:T(8,128)(2,1)}, bf16[1280,2048]{1,0:T(8,128)(2,1)}, u32[]{:S(2)}, u32[]{:S(2)}) collective-permute-start(bf16[1280,2048]{1,0:T(8,128)(2,1)} %convolution_convert_fusion.1), channel_id=1, source_target_pairs={{0,2},{2,0},{1,3},{3,1},{4,6},{6,4},{5,7},{7,5},{8,10},{10,8},{9,1... | collective-permute-start | bytes 15728648 | tf_op jit(solution)/shard_map/ppermute | solution.py:789
  422.5 25.4 %collective-permute-start.40 = (bf16[256,1024]{1,0:T(8,128)(2,1)}, bf16[256,1024]{1,0:T(8,128)(2,1)S(1)}, u32[]{:S(2)}, u32[]{:S(2)}) collective-permute-start(bf16[256,1024]{1,0:T(8,128)(2,1)} %get-tuple-element.278), channel_id=1, source_target_pairs={{0,4},{8,0},{16,8},{24,16},{28,24},{20,28},{12,20},{4,12},{1,5},{9... | collective-permute-start | bytes 1572872 | tf_op jit(solution)/shard_map/ppermute | solution.py:862
  450.2 37.7 %collective-permute-start.42 = (bf16[256,1024]{1,0:T(8,128)(2,1)S(1)}, bf16[256,1024]{1,0:T(8,128)(2,1)S(1)}, u32[]{:S(2)}, u32[]{:S(2)}) collective-permute-start(bf16[256,1024]{1,0:T(8,128)(2,1)S(1)} %get-tuple-element.276), channel_id=1, source_target_pairs={{0,4},{8,0},{16,8},{24,16},{28,24},{20,28},{12,20},{4,12},{1,5},{9... | collective-permute-start | bytes 1572872 | tf_op jit(solution)/shard_map/ppermute | solution.py:862
  452.2 35.7 %collective-permute-start.41 = (bf16[256,1024]{1,0:T(8,128)(2,1)S(1)}, bf16[256,1024]{1,0:T(8,128)(2,1)S(1)}, u32[]{:S(2)}, u32[]{:S(2)}) collective-permute-start(bf16[256,1024]{1,0:T(8,128)(2,1)S(1)} %get-tuple-element.277), channel_id=1, source_target_pairs={{0,8},{8,16},{16,24},{24,28},{28,20},{20,12},{12,4},{4,0},{1,9},{9... | collective-permute-start | bytes 1572872 | tf_op jit(solution)/shard_map/ppermute | solution.py:859
  464.2 104.4 %collective-permute-start.45 = (bf16[640,2048]{1,0:T(8,128)(2,1)}, bf16[640,2048]{1,0:T(8,128)(2,1)}, u32[]{:S(2)}, u32[]{:S(2)}) collective-permute-start(bf16[640,2048]{1,0:T(8,128)(2,1)} %add_convert_fusion), channel_id=1, source_target_pairs={{0,1},{1,0},{2,3},{3,2},{4,5},{5,4},{6,7},{7,6},{8,9},{9,8},{10,11... | collective-permute-start | bytes 7864328 | tf_op jit(solution)/shard_map/ppermute | solution.py:785
  554.6 31.4 %collective-permute-start.52 = (bf16[2,64,1024]{2,1,0:T(8,128)(2,1)}, bf16[2,64,1024]{2,1,0:T(8,128)(2,1)S(1)}, u32[]{:S(2)}, u32[]{:S(2)}) collective-permute-start(bf16[2,64,1024]{2,1,0:T(8,128)(2,1)} %dynamic-slice_bitcast_fusion.2), channel_id=1, source_target_pairs={{0,1},{1,0},{2,3},{3,2},{4,5},{5,4},{6,7},{7,6},{8,9},{9,8},{10,11... | collective-permute-start | bytes 786440 | tf_op jit(solution)/shard_map/ppermute | solution.py:785
  (97 other events, 1354.0 us)
Sparse Core Ops, SparseCore 0:
  50.3 70.8 all-gather.2
  130.7 69.4 all-gather.4
  315.7 98.9 reduce-scatter.4
  422.6 124.0 reduce-scatter.2

commit v4 on v3

--- a/solution.py
+++ b/solution.py
@@ -1150,35 +1150,41 @@
             part = tn(xh[:, first * feature : last * feature], chain.tie(dx)[:, :XCOLS])
             return dict(enumerate(chain.mark(part).reshape(last - first, feature, XCOLS), first))
 
-        made = blocks_x(3, 6)
+        made = blocks_x(4, 5)
         scatter_x = Scatter(ring, lambda k: made[k], chain)
         scatter_x.start()
-        made.update(blocks_x(0, 3))
-        scatter_x.land(chain)
-        scatter_x.start()
-        made.update(blocks_x(6, 8))
-        du_own = chain.mark(unit_product(dx, slot, 1) + rows_of(far_u, xi, 1).astype(F32))
-        scatter_x.land(chain)
-        scatter_x.start()
-        back_z.turn(chain)
         tally = SmallSum(chain.tie(acc))
         tally.start()
+        made.update(blocks_x(3, 4))
+        made.update(blocks_x(5, 6))
         scatter_x.land(chain)
+        tally.land(chain)
         scatter_x.start()
+        tally.start()
+        made.update(blocks_x(0, 3))
+        made.update(blocks_x(6, 8))
+        scatter_x.land(chain)
         tally.land(chain)
+        scatter_x.start()
         tally.start()
+        back_z.turn(chain)
+        du_own = unit_product(dx, slot, 1) + rows_of(far_u, xi, 1).astype(F32)
+        du_own = chain.mark(lax.optimization_barrier(du_own))
+        scatter_x.land(chain)
+        tally.land(chain)
+        scatter_x.start()
         mid_u = chain.take(mid_u)
         du = chain.mark(du_own + mid_u.astype(F32))
         scatter_x.land(chain)
         back_x = Return(chain.mark(scatter_x.total()))
-        tally.land(chain)
-        tally.start()
+        acc = tally.value
+        acc_x = swap_x(acc)
         back_z.land(chain)
         back_x.turn(chain)
-        tally.land(chain)
-        acc = tally.value
-        acc_x = chain.take(swap_x(acc))
-        acc_far = swap_core(jnp.stack([acc, acc_x]))
+        acc_x = chain.take(acc_x)
+        acc_far = chain.take(swap_core(jnp.stack([acc, acc_x])))
+        taps_total, head_total = chain.mark(assemble_small(xi, ci, acc, acc_x, acc_far))
+        own_conv = lax.dynamic_slice(taps_total, (0, flat_index(sizes) * width), (KERNEL + 1, width))
     else:
         dx, acc = backward_call(slots, none_yet, ())
         du = reduced(nt(dx, w_all), group)
@@ -1187,6 +1193,7 @@
         acc_x = swap_x(acc)
         acc_far = swap_core(jnp.stack([acc, acc_x]))
         taps_total, head_total = assemble_small(xi, ci, acc, acc_x, acc_far)
+        own_conv = lax.dynamic_slice(taps_total, (0, flat_index(sizes) * width), (KERNEL + 1, width))
     v_s, v_l = branch[:short].astype(F32), branch[short:].astype(F32)
     du_s, du_l = du[:short], du[short:]
 
@@ -1210,7 +1217,6 @@
             assemble_rows(xi, back_z.pair, back_z.got, back_x.pair, back_x.got, in_w, dt_w)
         )
         norm_sum = norm_sum[:, 0]
-        taps_total, head_total = assemble_small(xi, ci, acc, acc_x, chain.take(acc_far))
     else:
         here = (jnp.arange(SLOTS) == slot).astype(F32)
         wider = lambda v: (v.reshape(D, AHEADS, 1, -1) * here[:, None]).reshape(D, -1)
@@ -1228,7 +1234,6 @@
     grad_norm_gain = norm_sum / norm_gain.astype(F32)
     grad_gate_gain = jnp.sum(out_w.astype(F32) * own_out, axis=1) / gate_gain.astype(F32)
 
-    own_conv = lax.dynamic_slice(taps_total, (0, flat_index(sizes) * width), (KERNEL + 1, width))
     return (
         out_short,
         out_long,

time: 630 us -> 624 us (level)
  other arithmetic: 57.2 us -> 50.4 us
    ppermute x20, waiting for transfers between devices: 16.3 us -> 9.64 us  [right(): return lax.ppermute(v, 'ra', self.pairs(1))]
    dot_general x5 -> x7, matrix products: 62.1 us -> 64.2 us  [tn(): lax.dot_general(a, b, (((0,), (0,)), ((), ())), preferred_element_type=F32)]
    unnamed x143 -> x139, local copies, waits for them, and re-layouts: 25 us -> 25.1 us
  transfers between devices with their start and end apart: 65 -> 65, of which waited for: 20 -> 19; matrix products, arithmetic and copies ran while one was open for 38% -> 38% of each run, Pallas kernels for 23% -> 23%
where the time goes in v4:
time: 624 us; the launch traced here: 616 us
  Pallas kernels  188 us (30%)
  matrix products  180 us (29%)
  waiting for transfers between devices  63.9 us (10%)
  starting transfers between devices  63 us (10%)
  other arithmetic  50.4 us (8%)
  local copies, waits for them, and re-layouts  50.1 us (8%)
  between operations  20.4 us (3%)
    pallas_call x3, Pallas kernels, ssd_backward(): pl.pallas_call(bwd_kernel, grid_spec=pltpu.PrefetchScalarGridSpec(num_sca...  87.6 us
    dot_general x7, matrix products, tn(): lax.dot_general(a, b, (((0,), (0,)), ((), ())), preferred_element_type=F32)  64.2 us
    dot_general x4, matrix products, nt(): lax.dot_general(a, b, (((1,), (1,)), ((), ())), preferred_element_type=F32)  60.2 us
    dot_general x3, matrix products, nn(): lax.dot_general(a, b, (((1,), (0,)), ((), ())), preferred_element_type=F32)  55.6 us
    pallas_call x2, Pallas kernels, ssd_forward(): pl.pallas_call(fwd_kernel, grid_spec=pltpu.PrefetchScalarGridSpec(num_sca...  40.8 us
    ppermute x20, waiting for transfers between devices, left(): return lax.ppermute(v, 'ra', self.pairs(-1))  35.3 us
    ppermute x20, starting transfers between devices, left(): return lax.ppermute(v, 'ra', self.pairs(-1))  27.8 us
    unnamed x139, local copies, waits for them, and re-layouts  25.1 us
  transfers between devices with their start and end apart: 65, of which 19 were waited for; matrix products, arithmetic and copies ran while one was open for 38% of the time, Pallas kernels for 23%

profile of v4, /device:TPU:0, one launch (start us, length us, event | category | flops | bytes accessed | tf_op | source)
XLA Modules:
  0.0 615.6 jit_solution(11106495092500239224)
XLA Ops:
  15.4 9.0 %collective-permute-done.got_ref = bf16[2,72,1408]{2,1,0:T(8,128)(2,1)S(1)} collective-permute-done((bf16[2,72,1408]{2,1,0:T(8,128)(2,1)}, bf16[2,72,1408]{2,1,0:T(8,128)(2,1)S(1)}, u32[]{:S(2)}, u32[]{:S(2)}) %collective-permute-start) | collective-permute-done | bytes 405536 | tf_op jit(solution)/shard_map/ppermute | solution.py:785
  44.5 5.6 norm_tokens.1
  56.7 10.0 %collective-permute-done.7 = bf16[256,1408]{1,0:T(8,128)(2,1)} collective-permute-done((bf16[256,1408]{1,0:T(8,128)(2,1)S(1)}, bf16[256,1408]{1,0:T(8,128)(2,1)}, u32[]{:S(2)}, u32[]{:S(2)}) %collective-permute-start.7) | collective-permute-done | bytes 720928 | tf_op jit(solution)/shard_map/ppermute | solution.py:862
  92.7 13.3 %collective-permute-done.13 = bf16[256,1408]{1,0:T(8,128)(2,1)} collective-permute-done((bf16[256,1408]{1,0:T(8,128)(2,1)}, bf16[256,1408]{1,0:T(8,128)(2,1)}, u32[]{:S(2)}, u32[]{:S(2)}) %collective-permute-start.13) | collective-permute-done | bytes 720928 | tf_op jit(solution)/shard_map/ppermute | solution.py:862
  136.0 23.3 %fusion.74.p_ref = f32[2560,1408]{1,0:T(8,128)} fusion(bf16[2560,2048]{1,0:T(8,128)(2,1)} %all-gather.3.cloned.1.call-done, bf16[2048,1408]{1,0:T(8,128)(2,1)} %constant_dynamic-update-slice_fusion), kind=kOutput, calls=%fused_computation.195 | convolution fusion | flops 14763950080 | bytes 30670848 | tf_op jit(solution)/shard_map/dot_general | solution.py:43
  166.5 20.4 %ssd_forward.2 = (bf16[2560,1024]{1,0:T(8,128)(2,1)}, bf16[2560,1280]{1,0:T(8,128)(2,1)}, bf16[2560,1280]{1,0:T(8,128)(2,1)}, f32[4,128,1024]{2,1,0:T(8,128)}) custom-call(s32[2]{0:T(128)} %iota.26.steps_ref, f32[2560,1408]{1,0:T(8,128)} %fusion.74.p_ref, f32[8,1280]{1,0:T(8,128)} %concatenate.141.cw_ref, f32[8,1280]{1,0:T(8,128)} %select_maximum_fusion.cb_ref, ...), custom_call_target="tpu_custom_call" | custom-call | flops 8000000000 | bytes 12000000 | tf_op jit(solution)/shard_map/ssd_forward/pallas_call | solution.py:461
  191.2 20.4 %ssd_forward.3 = (bf16[2560,1024]{1,0:T(8,128)(2,1)}, bf16[2560,1280]{1,0:T(8,128)(2,1)}, bf16[2560,1280]{1,0:T(8,128)(2,1)}, f32[4,128,1024]{2,1,0:T(8,128)}) custom-call(s32[2]{0:T(128)} %constant.185.clone.1.steps_ref, f32[2560,1408]{1,0:T(8,128)} %fusion.74.p_ref, ...), custom_call_target="tpu_custom_call", output_to_operand_aliasing={{0}: (8, {}), {1}: (9, {}), {2}: (10, {}), {3}: (11, {})} | custom-call | flops 8000000000 | bytes 12000000 | tf_op jit(solution)/shard_map/ssd_forward/pallas_call | solution.py:461
  218.7 16.5 %convolution_convert_fusion.3.z_ref = bf16[2560,1024]{1,0:T(8,128)(2,1)} fusion(bf16[2560,2048]{1,0:T(8,128)(2,1)} %all-gather.3.cloned.1.call-done, bf16[2048,1024]{1,0:T(8,128)(2,1)} %constant_dynamic-update-slice_fusion.9), kind=kOutput, calls=%fused_computation.19 | convolution fusion | flops 10740039680 | bytes 19922944 | tf_op jit(solution)/shard_map/dot_general | solution.py:43
  241.1 16.6 %convolution_convert_fusion.2.dn_ref = bf16[2560,1024]{1,0:T(8,128)(2,1)} fusion(bf16[2560,2048]{1,0:T(8,128)(2,1)} %all-gather.5.cloned.1.call-done, bf16[1024,2048]{1,0:T(8,128)(2,1)} %ordered_rows.1), kind=kOutput, calls=%fused_computation.18 | convolution fusion | flops 10740039680 | bytes 19922944 | tf_op jit(solution)/shard_map/dot_general | solution.py:39
  258.2 13.7 %gate_stats.1 = f32[8,2560]{1,0:T(8,128)} custom-call(s32[8]{0:T(128)} %iota.24.order_ref, bf16[2560,1024]{1,0:T(8,128)(2,1)} %get-tuple-element.196.y_ref, bf16[2560,1024]{1,0:T(8,128)(2,1)} %convolution_convert_fusion.3.z_ref, bf16[2560,1024]{1,0:T(8,128)(2,1)} %convolution_convert_fusion.2.dn_ref, f32[8,1024]{1,0:T(8,128)} %concatenate.139.gain_ref), custom_call_target="tpu_custom_call" | custom-call | flops 3000000000 | bytes 16000000 | tf_op jit(solution)/shard_map/gate_stats/pallas_call | solution.py:543
  280.0 18.6 %gate_backward.1 = (bf16[2560,1024]{1,0:T(8,128)(2,1)}, bf16[2560,1024]{1,0:T(8,128)(2,1)}, bf16[2560,1024]{1,0:T(8,128)(2,1)}) custom-call(s32[8]{0:T(128)} %iota.23.order_ref, f32[8,2560]{1,0:T(8,128)} %add.318.st_ref, bf16[2560,1024]{1,0:T(8,128)(2,1)} %get-tuple-element.196.y_ref, bf16[2560,1024]{1,0:T(8,128)(2,1)} %convolution_convert_fusion.3.z_ref, ...), custom_call_target="tpu_custom_call" | custom-call | flops 6000000000 | bytes 32000000 | tf_op jit(solution)/shard_map/gate_backward/pallas_call | solution.py:562
  298.5 17.2 %convolution_convert_fusion.4 = bf16[1024,2048]{1,0:T(8,128)(2,1)} fusion(bf16[2560,1024]{1,0:T(8,128)(2,1)} %get-tuple-element.224, bf16[2560,2048]{1,0:T(8,128)(2,1)} %all-gather.5.cloned.1.call-done), kind=kOutput, calls=%fused_computation.33 | convolution fusion | flops 10739515392 | bytes 19922944 | tf_op jit(solution)/shard_map/dot_general | solution.py:47
  315.8 17.5 %fusion.73 = (bf16[2048,1024]{1,0:T(8,128)(2,1)S(1)}, f32[2048,1024]{1,0:T(8,128)}) fusion(bf16[2560,2048]{1,0:T(8,128)(2,1)} %all-gather.3.cloned.1.call-done, bf16[2560,1024]{1,0:T(8,128)(2,1)} %get-tuple-element.223.dz_ref), kind=kOutput, calls=%fused_computation.194 | convolution fusion | flops 10739515392 | bytes 28311552 | tf_op jit(solution)/shard_map/dot_general | solution.py:47
  335.5 15.7 %convolution_convert_fusion = bf16[2560,2048]{1,0:T(8,128)(2,1)} fusion(bf16[2560,1024]{1,0:T(8,128)(2,1)} %get-tuple-element.224, bf16[1024,2048]{1,0:T(8,128)(2,1)S(1)} %copy-done.10), kind=kOutput, calls=%fused_computation.1 | convolution fusion | flops 10742661120 | bytes 19922944 | tf_op jit(solution)/shard_map/dot_general | solution.py:43
  357.2 41.1 %ssd_backward.3 = (bf16[2560,2432]{1,0:T(8,128)(2,1)}, f32[8,1408]{1,0:T(8,128)}) custom-call(s32[2]{0:T(128)} %pad_add_fusion.1.steps_ref, f32[2560,1408]{1,0:T(8,128)} %fusion.74.p_ref, bf16[2560,1280]{1,0:T(8,128)(2,1)} %get-tuple-element.197.act_ref, bf16[2560,1280]{1,0:T(8,128)(2,1)} %get-tuple-element.198.slope_ref, ...), custom_call_target="tpu_custom_call" | custom-call | flops 20000000000 | bytes 18000000 | tf_op jit(solution)/shard_map/ssd_backward/pallas_call | solution.py:498
  401.1 20.5 %convolution_convert_fusion.1 = bf16[1280,2048]{1,0:T(8,128)(2,1)} fusion(bf16[2560,2432]{1,0:T(8,128)(2,1)} %get-tuple-element.235.refs_0_, s32[]{:T(128)S(6)} %select_n.224, bf16[2048,1024]{1,0:T(8,128)(2,1)} %constant_dynamic-update-slice_fusion.9, bf16[2048,1408]{1,0:T(8,128)(2,1)} %constant_dynamic-update-slice_fusion), kind=kOutput, calls=%fused_computation.3 | convolution fusion | flops 12773228544 | bytes 21430276 | tf_op jit(solution)/shard_map/dot_general | solution.py:39
  431.1 23.3 %ssd_backward.4 = (bf16[2560,2432]{1,0:T(8,128)(2,1)}, f32[8,1408]{1,0:T(8,128)}) custom-call(s32[1]{0:T(128)} %bitcast.11.steps_ref, f32[2560,1408]{1,0:T(8,128)} %fusion.74.p_ref, bf16[2560,1280]{1,0:T(8,128)(2,1)} %get-tuple-element.197.act_ref, bf16[2560,1280]{1,0:T(8,128)(2,1)} %get-tuple-element.198.slope_ref, ...), custom_call_target="tpu_custom_call", output_to_operand_aliasing={{0}: (13, {})} | custom-call | flops 10000000000 | bytes 9000000 | tf_op jit(solution)/shard_map/ssd_backward/pallas_call | solution.py:498
  459.0 11.5 %add_convert_fusion = bf16[640,2048]{1,0:T(8,128)(2,1)} fusion(bf16[1280,2048]{1,0:T(8,128)(2,1)} %collective-permute-done.38, s32[]{:T(128)S(6)} %select_n.226, bf16[2560,2432]{1,0:T(8,128)(2,1)} %get-tuple-element.243.refs_0_, s32[]{:T(128)S(6)} %select_n.225, bf16[2048,1024]{1,0:T(8,128)(2,1)S(1)} %copy-done.38, ...), kind=kOutput, calls=%fused_computation.22 | convolution fusion | flops 6399197184 | bytes 18317320 | tf_op jit(solution)/shard_map/dot_general | solution.py:39
  470.5 23.1 %ssd_backward.5 = (bf16[2560,2432]{1,0:T(8,128)(2,1)}, f32[8,1408]{1,0:T(8,128)}) custom-call(s32[1]{0:T(128)} %bitcast.10.steps_ref, f32[2560,1408]{1,0:T(8,128)} %fusion.74.p_ref, bf16[2560,1280]{1,0:T(8,128)(2,1)} %get-tuple-element.197.act_ref, bf16[2560,1280]{1,0:T(8,128)(2,1)} %get-tuple-element.198.slope_ref, ...), custom_call_target="tpu_custom_call", output_to_operand_aliasing={{0}: (13, {})} | custom-call | flops 10000000000 | bytes 9000000 | tf_op jit(solution)/shard_map/ssd_backward/pallas_call | solution.py:498
  495.1 5.8 fusion.25
  516.4 8.8 %fusion.2 = f32[768,1408]{1,0:T(8,128)S(1)} fusion(bf16[2560,2432]{1,0:T(8,128)(2,1)S(1)} %copy-done, bf16[2560,2048]{1,0:T(8,128)(2,1)} %all-gather.3.cloned.1.call-done), kind=kOutput, calls=%fused_computation.6 | convolution fusion | flops 5536481280 | bytes 15466496 | tf_op jit(solution)/shard_map/dot_general | solution.py:47
  525.2 7.7 %fusion = f32[512,1408]{1,0:T(8,128)S(1)} fusion(bf16[2560,2432]{1,0:T(8,128)(2,1)S(1)} %copy-done, bf16[2560,2048]{1,0:T(8,128)(2,1)} %all-gather.3.cloned.1.call-done), kind=kOutput, calls=%fused_computation.4 | convolution fusion | flops 3690987520 | bytes 12713984 | tf_op jit(solution)/shard_map/dot_general | solution.py:47
  538.6 11.5 %convert_add_fusion.2 = f32[640,2048]{1,0:T(8,128)} fusion(bf16[1280,2048]{1,0:T(8,128)(2,1)} %collective-permute-done.38, s32[]{:T(128)S(6)} %select_n.229, bf16[2560,2432]{1,0:T(8,128)(2,1)S(1)} %copy-done, s32[]{:T(128)S(6)} %select_n.228, bf16[2048,1024]{1,0:T(8,128)(2,1)} %constant_dynamic-update-slice_fusion.9, ...), kind=kOutput, calls=%fused_computation.21 | convolution fusion | flops 6397886464 | bytes 20938760 | tf_op jit(solution)/shard_map/dot_general | solution.py:39
  595.3 6.1 fusion.16
  (402 shorter events, 217.7 us)
Async XLA Ops:
  7.2 123.5 %all-gather.3.cloned.1.call-start = ((), (), s32[]{:S(2)}) async-start(), calls=%async_computation.2 | async-start | bytes 13107200 | tf_op jit(solution)/shard_map/all_gather | solution.py:981
  50.2 190.9 %all-gather.5.cloned.1.call-start = ((), (), s32[]{:S(2)}) async-start(), calls=%async_computation.3 | async-start | bytes 13107200 | tf_op jit(solution)/shard_map/all_gather | solution.py:981
  89.0 28.3 %collective-permute-start.17 = (bf16[256,1024]{1,0:T(8,128)(2,1)}, bf16[256,1024]{1,0:T(8,128)(2,1)}, u32[]{:S(2)}, u32[]{:S(2)}) collective-permute-start(bf16[256,1024]{1,0:T(8,128)(2,1)} %place_rows.3), channel_id=1, source_target_pairs={{0,4},{8,0},{16,8},{24,16},{28,24},{20,28},{12,20},{4,12},{1,5},{9... | collective-permute-start | bytes 1572872 | tf_op jit(solution)/shard_map/ppermute | solution.py:862
  90.0 28.2 %collective-permute-start.16 = (bf16[256,1024]{1,0:T(8,128)(2,1)}, bf16[256,1024]{1,0:T(8,128)(2,1)S(1)}, u32[]{:S(2)}, u32[]{:S(2)}) collective-permute-start(bf16[256,1024]{1,0:T(8,128)(2,1)} %place_rows.3), channel_id=1, source_target_pairs={{0,8},{8,16},{16,24},{24,28},{28,20},{20,12},{12,4},{4,0},{1,9},{9... | collective-permute-start | bytes 1572872 | tf_op jit(solution)/shard_map/ppermute | solution.py:859
  130.7 432.0 %reduce-scatter.5.cloned.1.call-start = ((), (), s32[]{:S(2)}) async-start(), calls=%async_computation.5 | async-start | bytes 4718592 | tf_op jit(solution)/shard_map/reduce_scatter | solution.py:1119
  130.8 28.6 %collective-permute-start.18 = (bf16[256,1024]{1,0:T(8,128)(2,1)S(1)}, bf16[256,1024]{1,0:T(8,128)(2,1)S(1)}, u32[]{:S(2)}, u32[]{:S(2)}) collective-permute-start(bf16[256,1024]{1,0:T(8,128)(2,1)S(1)} %collective-permute-done.16), channel_id=1, source_target_pairs={{0,8},{8,16},{16,24},{24,28},{28,20},{20,12},{12,4},{4,0},{1,9},{9... | collective-permute-start | bytes 1572872 | tf_op jit(solution)/shard_map/ppermute | solution.py:859
  131.9 27.5 %collective-permute-start.19 = (bf16[256,1024]{1,0:T(8,128)(2,1)}, bf16[256,1024]{1,0:T(8,128)(2,1)S(1)}, u32[]{:S(2)}, u32[]{:S(2)}) collective-permute-start(bf16[256,1024]{1,0:T(8,128)(2,1)} %collective-permute-done.17), channel_id=1, source_target_pairs={{0,4},{8,0},{16,8},{24,16},{28,24},{20,28},{12,20},{4,12},{1,5},{9... | collective-permute-start | bytes 1572872 | tf_op jit(solution)/shard_map/ppermute | solution.py:862
  134.0 25.4 %collective-permute-start.21 = (bf16[128,2048]{1,0:T(8,128)(2,1)S(1)}, bf16[128,2048]{1,0:T(8,128)(2,1)S(1)}, u32[]{:S(2)}, u32[]{:S(2)}) collective-permute-start(bf16[128,2048]{1,0:T(8,128)(2,1)S(1)} %copy-done.15), channel_id=1, source_target_pairs={{0,4},{8,0},{16,8},{24,16},{28,24},{20,28},{12,20},{4,12},{1,5},{9... | collective-permute-start | bytes 1572872 | tf_op jit(solution)/shard_map/ppermute | solution.py:862
  159.4 27.6 %collective-permute-start.22 = (bf16[256,1024]{1,0:T(8,128)(2,1)S(1)}, bf16[256,1024]{1,0:T(8,128)(2,1)S(1)}, u32[]{:S(2)}, u32[]{:S(2)}) collective-permute-start(bf16[256,1024]{1,0:T(8,128)(2,1)S(1)} %collective-permute-done.18), channel_id=1, source_target_pairs={{0,8},{8,16},{16,24},{24,28},{28,20},{20,12},{12,4},{4,0},{1,9},{9... | collective-permute-start | bytes 1572872 | tf_op jit(solution)/shard_map/ppermute | solution.py:859
  160.5 26.5 %collective-permute-start.23 = (bf16[256,1024]{1,0:T(8,128)(2,1)S(1)}, bf16[256,1024]{1,0:T(8,128)(2,1)S(1)}, u32[]{:S(2)}, u32[]{:S(2)}) collective-permute-start(bf16[256,1024]{1,0:T(8,128)(2,1)S(1)} %collective-permute-done.19), channel_id=1, source_target_pairs={{0,4},{8,0},{16,8},{24,16},{28,24},{20,28},{12,20},{4,12},{1,5},{9... | collective-permute-start | bytes 1572872 | tf_op jit(solution)/shard_map/ppermute | solution.py:862
  161.5 25.4 %collective-permute-start.24 = (bf16[128,2048]{1,0:T(8,128)(2,1)S(1)}, bf16[128,2048]{1,0:T(8,128)(2,1)S(1)}, u32[]{:S(2)}, u32[]{:S(2)}) collective-permute-start(bf16[128,2048]{1,0:T(8,128)(2,1)S(1)} %collective-permute-done.20.refs_8_), channel_id=1, source_target_pairs={{0,8},{8,16},{16,24},{24,28},{28,20},{20,12},{12,4},{4,0},{1,9},{9... | collective-permute-start | bytes 1572872 | tf_op jit(solution)/shard_map/ppermute | solution.py:859
  162.6 24.4 %collective-permute-start.25 = (bf16[128,2048]{1,0:T(8,128)(2,1)S(1)}, bf16[128,2048]{1,0:T(8,128)(2,1)S(1)}, u32[]{:S(2)}, u32[]{:S(2)}) collective-permute-start(bf16[128,2048]{1,0:T(8,128)(2,1)S(1)} %collective-permute-done.21.refs_1_), channel_id=1, source_target_pairs={{0,4},{8,0},{16,8},{24,16},{28,24},{20,28},{12,20},{4,12},{1,5},{9... | collective-permute-start | bytes 1572872 | tf_op jit(solution)/shard_map/ppermute | solution.py:862
  187.1 25.4 %collective-permute-start.28 = (bf16[128,2048]{1,0:T(8,128)(2,1)S(1)}, bf16[128,2048]{1,0:T(8,128)(2,1)S(1)}, u32[]{:S(2)}, u32[]{:S(2)}) collective-permute-start(bf16[128,2048]{1,0:T(8,128)(2,1)S(1)} %collective-permute-done.24.refs_7_), channel_id=1, source_target_pairs={{0,8},{8,16},{16,24},{24,28},{28,20},{20,12},{12,4},{4,0},{1,9},{9... | collective-permute-start | bytes 1572872 | tf_op jit(solution)/shard_map/ppermute | solution.py:859
  315.8 279.5 %reduce-scatter.3.cloned.1.call-start = ((), (), s32[]{:S(2)}) async-start(), calls=%async_computation.4 | async-start | bytes 13107200 | tf_op jit(solution)/shard_map/reduce_scatter | solution.py:1119
  353.1 45.3 %collective-permute-start.36 = (bf16[256,1024]{1,0:T(8,128)(2,1)S(1)}, bf16[256,1024]{1,0:T(8,128)(2,1)S(1)}, u32[]{:S(2)}, u32[]{:S(2)}) collective-permute-start(bf16[256,1024]{1,0:T(8,128)(2,1)S(1)} %pad_maximum_fusion.4), channel_id=1, source_target_pairs={{0,8},{8,16},{16,24},{24,28},{28,20},{20,12},{12,4},{4,0},{1,9},{9... | collective-permute-start | bytes 1572872 | tf_op jit(solution)/shard_map/ppermute | solution.py:859
  353.8 44.6 %collective-permute-start.37 = (bf16[256,1024]{1,0:T(8,128)(2,1)S(1)}, bf16[256,1024]{1,0:T(8,128)(2,1)S(1)}, u32[]{:S(2)}, u32[]{:S(2)}) collective-permute-start(bf16[256,1024]{1,0:T(8,128)(2,1)S(1)} %pad_maximum_fusion.5), channel_id=1, source_target_pairs={{0,4},{8,0},{16,8},{24,16},{28,24},{20,28},{12,20},{4,12},{1,5},{9... | collective-permute-start | bytes 1572872 | tf_op jit(solution)/shard_map/ppermute | solution.py:862
  421.6 37.3 %collective-permute-start.38 = (bf16[1280,2048]{1,0:T(8,128)(2,1)}, bf16[1280,2048]{1,0:T(8,128)(2,1)}, u32[]{:S(2)}, u32[]{:S(2)}) collective-permute-start(bf16[1280,2048]{1,0:T(8,128)(2,1)} %convolution_convert_fusion.1), channel_id=1, source_target_pairs={{0,2},{2,0},{1,3},{3,1},{4,6},{6,4},{5,7},{7,5},{8,10},{10,8},{9,1... | collective-permute-start | bytes 15728648 | tf_op jit(solution)/shard_map/ppermute | solution.py:789
  429.0 25.4 %collective-permute-start.40 = (bf16[256,1024]{1,0:T(8,128)(2,1)}, bf16[256,1024]{1,0:T(8,128)(2,1)S(1)}, u32[]{:S(2)}, u32[]{:S(2)}) collective-permute-start(bf16[256,1024]{1,0:T(8,128)(2,1)} %get-tuple-element.282), channel_id=1, source_target_pairs={{0,4},{8,0},{16,8},{24,16},{28,24},{20,28},{12,20},{4,12},{1,5},{9... | collective-permute-start | bytes 1572872 | tf_op jit(solution)/shard_map/ppermute | solution.py:862
  456.7 36.9 %collective-permute-start.42 = (bf16[256,1024]{1,0:T(8,128)(2,1)S(1)}, bf16[256,1024]{1,0:T(8,128)(2,1)S(1)}, u32[]{:S(2)}, u32[]{:S(2)}) collective-permute-start(bf16[256,1024]{1,0:T(8,128)(2,1)S(1)} %get-tuple-element.280), channel_id=1, source_target_pairs={{0,4},{8,0},{16,8},{24,16},{28,24},{20,28},{12,20},{4,12},{1,5},{9... | collective-permute-start | bytes 1572872 | tf_op jit(solution)/shard_map/ppermute | solution.py:862
  458.7 34.9 %collective-permute-start.41 = (bf16[256,1024]{1,0:T(8,128)(2,1)S(1)}, bf16[256,1024]{1,0:T(8,128)(2,1)S(1)}, u32[]{:S(2)}, u32[]{:S(2)}) collective-permute-start(bf16[256,1024]{1,0:T(8,128)(2,1)S(1)} %get-tuple-element.281), channel_id=1, source_target_pairs={{0,8},{8,16},{16,24},{24,28},{28,20},{20,12},{12,4},{4,0},{1,9},{9... | collective-permute-start | bytes 1572872 | tf_op jit(solution)/shard_map/ppermute | solution.py:859
  506.8 62.6 %collective-permute-start.48 = (bf16[640,2048]{1,0:T(8,128)(2,1)}, bf16[640,2048]{1,0:T(8,128)(2,1)}, u32[]{:S(2)}, u32[]{:S(2)}) collective-permute-start(bf16[640,2048]{1,0:T(8,128)(2,1)} %add_convert_fusion), channel_id=1, source_target_pairs={{0,1},{1,0},{2,3},{3,2},{4,5},{5,4},{6,7},{7,6},{8,9},{9,8},{10,11... | collective-permute-start | bytes 7864328 | tf_op jit(solution)/shard_map/ppermute | solution.py:785
  507.9 30.6 %collective-permute-start.43 = (bf16[128,1024]{1,0:T(8,128)(2,1)S(1)}, bf16[128,1024]{1,0:T(8,128)(2,1)}, u32[]{:S(2)}, u32[]{:S(2)}) collective-permute-start(bf16[128,1024]{1,0:T(8,128)(2,1)S(1)} %get-tuple-element.297), channel_id=1, source_target_pairs={{0,2},{2,0},{1,3},{3,1},{4,6},{6,4},{5,7},{7,5},{8,10},{10,8},{9,1... | collective-permute-start | bytes 786440 | tf_op jit(solution)/shard_map/ppermute | solution.py:789
  552.9 30.4 %collective-permute-start.51 = (bf16[2,64,1024]{2,1,0:T(8,128)(2,1)}, bf16[2,64,1024]{2,1,0:T(8,128)(2,1)}, u32[]{:S(2)}, u32[]{:S(2)}) collective-permute-start(bf16[2,64,1024]{2,1,0:T(8,128)(2,1)} %dynamic-slice_bitcast_fusion.2), channel_id=1, source_target_pairs={{0,1},{1,0},{2,3},{3,2},{4,5},{5,4},{6,7},{7,6},{8,9},{9,8},{10,11... | collective-permute-start | bytes 786440 | tf_op jit(solution)/shard_map/ppermute | solution.py:785
  555.7 27.7 %collective-permute-start.59 = (f32[8,1408]{1,0:T(8,128)S(1)}, f32[8,1408]{1,0:T(8,128)S(1)}, u32[]{:S(2)}, u32[]{:S(2)}) collective-permute-start(f32[8,1408]{1,0:T(8,128)S(1)} %add.368.own_ref), channel_id=1, source_target_pairs={{0,1},{1,0},{2,3},{3,2},{4,5},{5,4},{6,7},{7,6},{8,9},{9,8},{10,11... | collective-permute-start | bytes 135176 | tf_op jit(solution)/shard_map/ppermute | solution.py:785
  (95 other events, 1471.0 us)
Sparse Core Ops, SparseCore 0:
  50.3 70.8 all-gather.2
  130.8 69.4 all-gather.4
  315.9 99.0 reduce-scatter.4
  429.2 88.0 reduce-scatter.2

commit v5 on v4

--- a/solution.py
+++ b/solution.py
@@ -124,7 +124,7 @@
         dt_s[rows, :] = softplus(p_ref[rows, XBC:] + hp_ref[0:1])
         return carry
 
-    lax.fori_loop(0, TILE // ROWS, conv_step, 0)
+    lax.fori_loop(0, TILE // ROWS, conv_step, 0, unroll=2)
     rate = hp_ref[1:2]
 
     def block(off, q, read_state, make_state):
@@ -214,9 +214,6 @@
         dgt_s[:q, :q] = jnp.zeros((q, q), F32)
         kc_s[:q, :] = jnp.zeros((q, 128), F32)
         kr_s[:, :q] = jnp.zeros((LOCAL_HEADS, q), F32)
-        if state_in or state_out:
-            fold_s[:q, :] = jnp.zeros((q, 128), F32)
-            dbc_s[:q, :] = jnp.zeros((q, 128), F32)
         if state_in:
             grow_s[:q, :] = two_parts(jnp.exp2(cum2))
             c_turned = c.astype(F32).T.astype(BF)
@@ -239,16 +236,16 @@
                 hb = h_ref[0, :, lanes].astype(BF)
                 dyc = dy2.astype(F32) * nn(grow_s[:q, :], seg_ref[:, lanes])
                 dyb = dyc.astype(BF)
-                fold_s[:q, :] += nt((dyc * nn(c, hb)).astype(BF), seg_ref[:, lanes])
-                dbc_s[:q, :] += nt(dyb, hb)
+                fold_s[:q, lanes] = (dyc * nn(c, hb)).astype(BF)
+                dbc_s[:q, lanes] = dyb
                 ds_s[:, lanes] = nn(c_turned, dyb).astype(BF)
             if state_out:
                 sb = ds_s[:, lanes]
                 wide = nn(grow_s[:q, :], seg_ref[:, lanes])
                 bd = nn(b, sb)
                 xf = x2.astype(F32)
-                fold_s[:q, :] += nt((xf * bd).astype(BF), seg_ref[:, lanes])
-                dbc_s[:q, :] += nt((wide * xf).astype(BF), sb)
+                fold_s[:q, lanes] = (xf * bd).astype(BF)
+                dbc_s[:q, lanes] = (wide * xf).astype(BF)
                 late = wide * bd
             picks = [jnp.where(lane == p * 2 + j, 1.0, 0.0).astype(BF) for j in range(2)]
             marks = [jnp.where(head_row == p * 2 + j, 1.0, 0.0).astype(BF) for j in range(2)]
@@ -306,11 +303,11 @@
         inverse = jnp.where(dt > 1e-30, 1.0 / jnp.maximum(dt, 1e-30), 0.0)
         d_dt = kcol * inverse
         if state_in:
-            d_cum = d_cum + fold_s[:q, :]
-            dc = dc + dbc_s[:q, :]
+            d_cum = d_cum + nt(fold_s[:q, :], seg_ref[...])
+            dc = dc + nt(dbc_s[:q, :], h_ref[0].astype(BF))
         if state_out:
-            db = db + dbc_s[:q, :]
-            d_weights = fold_s[:q, :]
+            db = db + nt(dbc_s[:q, :], ds_s[...])
+            d_weights = nt(fold_s[:q, :], seg_ref[...])
             d_dt = d_dt + d_weights * decay
             w_term = d_weights * decay * dt
             last = lax.broadcasted_iota(jnp.int32, (q, 1), 0) == q - 1
@@ -354,7 +351,7 @@
             dp_ref[rows, cols] = total.astype(BF)
         return carry
 
-    lax.fori_loop(0, TILE // ROWS, conv_step, 0)
+    lax.fori_loop(0, TILE // ROWS, conv_step, 0, unroll=2)
     for k in range(KERNEL + 1):
         acc_ref[k : k + 1, :XBC] += jnp.sum(sums_s[k], axis=0, keepdims=True)
 
@@ -379,7 +376,7 @@
         )
         return carry
 
-    lax.fori_loop(0, y_ref.shape[0] // ROWS, step, 0)
+    lax.fori_loop(0, y_ref.shape[0] // ROWS, step, 0, unroll=2)
     st_ref[...] = both_s[...].T[0:8]
 
 
@@ -406,7 +403,7 @@
             dz_ref[rows, lanes] = (dg * y * (sg + silu * (1.0 - sg))).astype(BF)
         return carry
 
-    lax.fori_loop(0, y_ref.shape[0] // ROWS, step, 0)
+    lax.fori_loop(0, y_ref.shape[0] // ROWS, step, 0, unroll=2)
 
 
 def norm_kernel(pieces, order_ref, *refs):
@@ -515,8 +512,8 @@
                 pltpu.VMEM((SPAN, SPAN), F32),
                 pltpu.VMEM((SPAN, 128), F32),
                 pltpu.VMEM((LOCAL_HEADS, SPAN), F32),
-                pltpu.VMEM((SPAN, 128), F32),
-                pltpu.VMEM((SPAN, 128), F32),
+                pltpu.VMEM((SPAN, WIDTH), BF),
+                pltpu.VMEM((SPAN, WIDTH), BF),
                 pltpu.VMEM((STATE, WIDTH), BF),
                 pltpu.VMEM((TILE, XBC), F32),
                 pltpu.VMEM((TILE, 128), F32),

time: 624 us -> 620 us (level)
  no operation moved by 1% of the time
where the time goes in v5:
time: 620 us; the launch traced here: 612 us
  Pallas kernels  184 us (30%)
  matrix products  179 us (29%)
  waiting for transfers between devices  63.5 us (10%)
  starting transfers between devices  63.4 us (10%)
  other arithmetic  50.6 us (8%)
  local copies, waits for them, and re-layouts  50.1 us (8%)
  between operations  20.5 us (3%)
    pallas_call x3, Pallas kernels, ssd_backward(): pl.pallas_call(bwd_kernel, grid_spec=pltpu.PrefetchScalarGridSpec(num_sca...  85.9 us
    dot_general x7, matrix products, tn(): lax.dot_general(a, b, (((0,), (0,)), ((), ())), preferred_element_type=F32)  63.9 us
    dot_general x4, matrix products, nt(): lax.dot_general(a, b, (((1,), (1,)), ((), ())), preferred_element_type=F32)  60 us
    dot_general x3, matrix products, nn(): lax.dot_general(a, b, (((1,), (0,)), ((), ())), preferred_element_type=F32)  55.6 us
    pallas_call x2, Pallas kernels, ssd_forward(): pl.pallas_call(fwd_kernel, grid_spec=pltpu.PrefetchScalarGridSpec(num_sca...  41.2 us
    ppermute x20, waiting for transfers between devices, left(): return lax.ppermute(v, 'ra', self.pairs(-1))  34.9 us
    ppermute x20, starting transfers between devices, left(): return lax.ppermute(v, 'ra', self.pairs(-1))  27.3 us
    unnamed x139, local copies, waits for them, and re-layouts  25.1 us
  transfers between devices with their start and end apart: 65, of which 19 were waited for; matrix products, arithmetic and copies ran while one was open for 38% of the time, Pallas kernels for 23%

profile of v5, /device:TPU:0, one launch (start us, length us, event | category | flops | bytes accessed | tf_op | source)
XLA Modules:
  0.0 611.9 jit_solution(412583024913776666)
XLA Ops:
  15.4 9.0 %collective-permute-done.got_ref = bf16[2,72,1408]{2,1,0:T(8,128)(2,1)S(1)} collective-permute-done((bf16[2,72,1408]{2,1,0:T(8,128)(2,1)}, bf16[2,72,1408]{2,1,0:T(8,128)(2,1)S(1)}, u32[]{:S(2)}, u32[]{:S(2)}) %collective-permute-start) | collective-permute-done | bytes 405536 | tf_op jit(solution)/shard_map/ppermute | solution.py:782
  44.5 5.6 norm_tokens.1
  56.7 10.0 %collective-permute-done.7 = bf16[256,1408]{1,0:T(8,128)(2,1)} collective-permute-done((bf16[256,1408]{1,0:T(8,128)(2,1)S(1)}, bf16[256,1408]{1,0:T(8,128)(2,1)}, u32[]{:S(2)}, u32[]{:S(2)}) %collective-permute-start.7) | collective-permute-done | bytes 720928 | tf_op jit(solution)/shard_map/ppermute | solution.py:859
  92.7 13.3 %collective-permute-done.13 = bf16[256,1408]{1,0:T(8,128)(2,1)} collective-permute-done((bf16[256,1408]{1,0:T(8,128)(2,1)}, bf16[256,1408]{1,0:T(8,128)(2,1)}, u32[]{:S(2)}, u32[]{:S(2)}) %collective-permute-start.13) | collective-permute-done | bytes 720928 | tf_op jit(solution)/shard_map/ppermute | solution.py:859
  136.1 23.3 %fusion.74.p_ref = f32[2560,1408]{1,0:T(8,128)} fusion(bf16[2560,2048]{1,0:T(8,128)(2,1)} %all-gather.3.cloned.1.call-done, bf16[2048,1408]{1,0:T(8,128)(2,1)} %constant_dynamic-update-slice_fusion), kind=kOutput, calls=%fused_computation.195 | convolution fusion | flops 14763950080 | bytes 30670848 | tf_op jit(solution)/shard_map/dot_general | solution.py:43
  166.3 20.5 %ssd_forward.2 = (bf16[2560,1024]{1,0:T(8,128)(2,1)}, bf16[2560,1280]{1,0:T(8,128)(2,1)}, bf16[2560,1280]{1,0:T(8,128)(2,1)}, f32[4,128,1024]{2,1,0:T(8,128)}) custom-call(s32[2]{0:T(128)} %iota.26.steps_ref, f32[2560,1408]{1,0:T(8,128)} %fusion.74.p_ref, f32[8,1280]{1,0:T(8,128)} %concatenate.141.cw_ref, f32[8,1280]{1,0:T(8,128)} %select_maximum_fusion.cb_ref, ...), custom_call_target="tpu_custom_call" | custom-call | flops 8000000000 | bytes 12000000 | tf_op jit(solution)/shard_map/ssd_forward/pallas_call | solution.py:458
  191.1 20.6 %ssd_forward.3 = (bf16[2560,1024]{1,0:T(8,128)(2,1)}, bf16[2560,1280]{1,0:T(8,128)(2,1)}, bf16[2560,1280]{1,0:T(8,128)(2,1)}, f32[4,128,1024]{2,1,0:T(8,128)}) custom-call(s32[2]{0:T(128)} %constant.185.clone.1.steps_ref, f32[2560,1408]{1,0:T(8,128)} %fusion.74.p_ref, ...), custom_call_target="tpu_custom_call", output_to_operand_aliasing={{0}: (8, {}), {1}: (9, {}), {2}: (10, {}), {3}: (11, {})} | custom-call | flops 8000000000 | bytes 12000000 | tf_op jit(solution)/shard_map/ssd_forward/pallas_call | solution.py:458
  219.0 16.5 %convolution_convert_fusion.3.z_ref = bf16[2560,1024]{1,0:T(8,128)(2,1)} fusion(bf16[2560,2048]{1,0:T(8,128)(2,1)} %all-gather.3.cloned.1.call-done, bf16[2048,1024]{1,0:T(8,128)(2,1)} %constant_dynamic-update-slice_fusion.9), kind=kOutput, calls=%fused_computation.19 | convolution fusion | flops 10740039680 | bytes 19922944 | tf_op jit(solution)/shard_map/dot_general | solution.py:43
  241.3 16.6 %convolution_convert_fusion.2.dn_ref = bf16[2560,1024]{1,0:T(8,128)(2,1)} fusion(bf16[2560,2048]{1,0:T(8,128)(2,1)} %all-gather.5.cloned.1.call-done, bf16[1024,2048]{1,0:T(8,128)(2,1)} %ordered_rows.1), kind=kOutput, calls=%fused_computation.18 | convolution fusion | flops 10740039680 | bytes 19922944 | tf_op jit(solution)/shard_map/dot_general | solution.py:39
  258.4 12.2 %gate_stats.1 = f32[8,2560]{1,0:T(8,128)} custom-call(s32[8]{0:T(128)} %iota.24.order_ref, bf16[2560,1024]{1,0:T(8,128)(2,1)} %get-tuple-element.196.y_ref, bf16[2560,1024]{1,0:T(8,128)(2,1)} %convolution_convert_fusion.3.z_ref, bf16[2560,1024]{1,0:T(8,128)(2,1)} %convolution_convert_fusion.2.dn_ref, f32[8,1024]{1,0:T(8,128)} %concatenate.139.gain_ref), custom_call_target="tpu_custom_call" | custom-call | flops 3000000000 | bytes 16000000 | tf_op jit(solution)/shard_map/gate_stats/pallas_call | solution.py:540
  278.7 18.0 %gate_backward.1 = (bf16[2560,1024]{1,0:T(8,128)(2,1)}, bf16[2560,1024]{1,0:T(8,128)(2,1)}, bf16[2560,1024]{1,0:T(8,128)(2,1)}) custom-call(s32[8]{0:T(128)} %iota.23.order_ref, f32[8,2560]{1,0:T(8,128)} %add.318.st_ref, bf16[2560,1024]{1,0:T(8,128)(2,1)} %get-tuple-element.196.y_ref, bf16[2560,1024]{1,0:T(8,128)(2,1)} %convolution_convert_fusion.3.z_ref, ...), custom_call_target="tpu_custom_call" | custom-call | flops 6000000000 | bytes 32000000 | tf_op jit(solution)/shard_map/gate_backward/pallas_call | solution.py:559
  296.7 17.0 %convolution_convert_fusion.4 = bf16[1024,2048]{1,0:T(8,128)(2,1)} fusion(bf16[2560,1024]{1,0:T(8,128)(2,1)} %get-tuple-element.224, bf16[2560,2048]{1,0:T(8,128)(2,1)} %all-gather.5.cloned.1.call-done), kind=kOutput, calls=%fused_computation.33 | convolution fusion | flops 10739515392 | bytes 19922944 | tf_op jit(solution)/shard_map/dot_general | solution.py:47
  313.8 17.5 %fusion.73 = (bf16[2048,1024]{1,0:T(8,128)(2,1)S(1)}, f32[2048,1024]{1,0:T(8,128)}) fusion(bf16[2560,2048]{1,0:T(8,128)(2,1)} %all-gather.3.cloned.1.call-done, bf16[2560,1024]{1,0:T(8,128)(2,1)} %get-tuple-element.223.dz_ref), kind=kOutput, calls=%fused_computation.194 | convolution fusion | flops 10739515392 | bytes 28311552 | tf_op jit(solution)/shard_map/dot_general | solution.py:47
  333.4 15.7 %convolution_convert_fusion = bf16[2560,2048]{1,0:T(8,128)(2,1)} fusion(bf16[2560,1024]{1,0:T(8,128)(2,1)} %get-tuple-element.224, bf16[1024,2048]{1,0:T(8,128)(2,1)S(1)} %copy-done.10), kind=kOutput, calls=%fused_computation.1 | convolution fusion | flops 10742661120 | bytes 19922944 | tf_op jit(solution)/shard_map/dot_general | solution.py:43
  355.2 40.8 %ssd_backward.3 = (bf16[2560,2432]{1,0:T(8,128)(2,1)}, f32[8,1408]{1,0:T(8,128)}) custom-call(s32[2]{0:T(128)} %pad_add_fusion.1.steps_ref, f32[2560,1408]{1,0:T(8,128)} %fusion.74.p_ref, bf16[2560,1280]{1,0:T(8,128)(2,1)} %get-tuple-element.197.act_ref, bf16[2560,1280]{1,0:T(8,128)(2,1)} %get-tuple-element.198.slope_ref, ...), custom_call_target="tpu_custom_call" | custom-call | flops 20000000000 | bytes 18000000 | tf_op jit(solution)/shard_map/ssd_backward/pallas_call | solution.py:495
  398.7 20.0 %convolution_convert_fusion.1 = bf16[1280,2048]{1,0:T(8,128)(2,1)} fusion(bf16[2560,2432]{1,0:T(8,128)(2,1)} %get-tuple-element.235.refs_0_, s32[]{:T(128)S(6)} %select_n.224, bf16[2048,1024]{1,0:T(8,128)(2,1)} %constant_dynamic-update-slice_fusion.9, bf16[2048,1408]{1,0:T(8,128)(2,1)} %constant_dynamic-update-slice_fusion), kind=kOutput, calls=%fused_computation.3 | convolution fusion | flops 12773228544 | bytes 21430276 | tf_op jit(solution)/shard_map/dot_general | solution.py:39
  428.2 22.9 %ssd_backward.4 = (bf16[2560,2432]{1,0:T(8,128)(2,1)}, f32[8,1408]{1,0:T(8,128)}) custom-call(s32[1]{0:T(128)} %bitcast.11.steps_ref, f32[2560,1408]{1,0:T(8,128)} %fusion.74.p_ref, bf16[2560,1280]{1,0:T(8,128)(2,1)} %get-tuple-element.197.act_ref, bf16[2560,1280]{1,0:T(8,128)(2,1)} %get-tuple-element.198.slope_ref, ...), custom_call_target="tpu_custom_call", output_to_operand_aliasing={{0}: (13, {})} | custom-call | flops 10000000000 | bytes 9000000 | tf_op jit(solution)/shard_map/ssd_backward/pallas_call | solution.py:495
  455.6 11.9 %add_convert_fusion = bf16[640,2048]{1,0:T(8,128)(2,1)} fusion(bf16[1280,2048]{1,0:T(8,128)(2,1)} %collective-permute-done.38, s32[]{:T(128)S(6)} %select_n.226, bf16[2560,2432]{1,0:T(8,128)(2,1)} %get-tuple-element.243.refs_0_, s32[]{:T(128)S(6)} %select_n.225, bf16[2048,1024]{1,0:T(8,128)(2,1)S(1)} %copy-done.38, ...), kind=kOutput, calls=%fused_computation.22 | convolution fusion | flops 6399197184 | bytes 18317320 | tf_op jit(solution)/shard_map/dot_general | solution.py:39
  467.4 22.3 %ssd_backward.5 = (bf16[2560,2432]{1,0:T(8,128)(2,1)}, f32[8,1408]{1,0:T(8,128)}) custom-call(s32[1]{0:T(128)} %bitcast.10.steps_ref, f32[2560,1408]{1,0:T(8,128)} %fusion.74.p_ref, bf16[2560,1280]{1,0:T(8,128)(2,1)} %get-tuple-element.197.act_ref, bf16[2560,1280]{1,0:T(8,128)(2,1)} %get-tuple-element.198.slope_ref, ...), custom_call_target="tpu_custom_call", output_to_operand_aliasing={{0}: (13, {})} | custom-call | flops 10000000000 | bytes 9000000 | tf_op jit(solution)/shard_map/ssd_backward/pallas_call | solution.py:495
  491.3 5.8 fusion.25
  512.8 8.7 %fusion.2 = f32[768,1408]{1,0:T(8,128)S(1)} fusion(bf16[2560,2432]{1,0:T(8,128)(2,1)S(1)} %copy-done, bf16[2560,2048]{1,0:T(8,128)(2,1)} %all-gather.3.cloned.1.call-done), kind=kOutput, calls=%fused_computation.6 | convolution fusion | flops 5536481280 | bytes 15466496 | tf_op jit(solution)/shard_map/dot_general | solution.py:47
  521.5 7.7 %fusion = f32[512,1408]{1,0:T(8,128)S(1)} fusion(bf16[2560,2432]{1,0:T(8,128)(2,1)S(1)} %copy-done, bf16[2560,2048]{1,0:T(8,128)(2,1)} %all-gather.3.cloned.1.call-done), kind=kOutput, calls=%fused_computation.4 | convolution fusion | flops 3690987520 | bytes 12713984 | tf_op jit(solution)/shard_map/dot_general | solution.py:47
  534.6 11.5 %convert_add_fusion.2 = f32[640,2048]{1,0:T(8,128)} fusion(bf16[1280,2048]{1,0:T(8,128)(2,1)} %collective-permute-done.38, s32[]{:T(128)S(6)} %select_n.229, bf16[2560,2432]{1,0:T(8,128)(2,1)S(1)} %copy-done, s32[]{:T(128)S(6)} %select_n.228, bf16[2048,1024]{1,0:T(8,128)(2,1)} %constant_dynamic-update-slice_fusion.9, ...), kind=kOutput, calls=%fused_computation.21 | convolution fusion | flops 6397886464 | bytes 20938760 | tf_op jit(solution)/shard_map/dot_general | solution.py:39
  591.6 6.1 fusion.16
  (402 shorter events, 217.9 us)
Async XLA Ops:
  7.2 123.5 %all-gather.3.cloned.1.call-start = ((), (), s32[]{:S(2)}) async-start(), calls=%async_computation.2 | async-start | bytes 13107200 | tf_op jit(solution)/shard_map/all_gather | solution.py:978
  50.2 191.2 %all-gather.5.cloned.1.call-start = ((), (), s32[]{:S(2)}) async-start(), calls=%async_computation.3 | async-start | bytes 13107200 | tf_op jit(solution)/shard_map/all_gather | solution.py:978
  89.0 28.3 %collective-permute-start.17 = (bf16[256,1024]{1,0:T(8,128)(2,1)}, bf16[256,1024]{1,0:T(8,128)(2,1)}, u32[]{:S(2)}, u32[]{:S(2)}) collective-permute-start(bf16[256,1024]{1,0:T(8,128)(2,1)} %place_rows.3), channel_id=1, source_target_pairs={{0,4},{8,0},{16,8},{24,16},{28,24},{20,28},{12,20},{4,12},{1,5},{9... | collective-permute-start | bytes 1572872 | tf_op jit(solution)/shard_map/ppermute | solution.py:859
  90.0 28.2 %collective-permute-start.16 = (bf16[256,1024]{1,0:T(8,128)(2,1)}, bf16[256,1024]{1,0:T(8,128)(2,1)S(1)}, u32[]{:S(2)}, u32[]{:S(2)}) collective-permute-start(bf16[256,1024]{1,0:T(8,128)(2,1)} %place_rows.3), channel_id=1, source_target_pairs={{0,8},{8,16},{16,24},{24,28},{28,20},{20,12},{12,4},{4,0},{1,9},{9... | collective-permute-start | bytes 1572872 | tf_op jit(solution)/shard_map/ppermute | solution.py:856
  130.7 428.1 %reduce-scatter.5.cloned.1.call-start = ((), (), s32[]{:S(2)}) async-start(), calls=%async_computation.5 | async-start | bytes 4718592 | tf_op jit(solution)/shard_map/reduce_scatter | solution.py:1116
  130.8 28.6 %collective-permute-start.18 = (bf16[256,1024]{1,0:T(8,128)(2,1)S(1)}, bf16[256,1024]{1,0:T(8,128)(2,1)S(1)}, u32[]{:S(2)}, u32[]{:S(2)}) collective-permute-start(bf16[256,1024]{1,0:T(8,128)(2,1)S(1)} %collective-permute-done.16), channel_id=1, source_target_pairs={{0,8},{8,16},{16,24},{24,28},{28,20},{20,12},{12,4},{4,0},{1,9},{9... | collective-permute-start | bytes 1572872 | tf_op jit(solution)/shard_map/ppermute | solution.py:856
  131.9 27.5 %collective-permute-start.19 = (bf16[256,1024]{1,0:T(8,128)(2,1)}, bf16[256,1024]{1,0:T(8,128)(2,1)S(1)}, u32[]{:S(2)}, u32[]{:S(2)}) collective-permute-start(bf16[256,1024]{1,0:T(8,128)(2,1)} %collective-permute-done.17), channel_id=1, source_target_pairs={{0,4},{8,0},{16,8},{24,16},{28,24},{20,28},{12,20},{4,12},{1,5},{9... | collective-permute-start | bytes 1572872 | tf_op jit(solution)/shard_map/ppermute | solution.py:859
  134.0 25.4 %collective-permute-start.21 = (bf16[128,2048]{1,0:T(8,128)(2,1)S(1)}, bf16[128,2048]{1,0:T(8,128)(2,1)S(1)}, u32[]{:S(2)}, u32[]{:S(2)}) collective-permute-start(bf16[128,2048]{1,0:T(8,128)(2,1)S(1)} %copy-done.15), channel_id=1, source_target_pairs={{0,4},{8,0},{16,8},{24,16},{28,24},{20,28},{12,20},{4,12},{1,5},{9... | collective-permute-start | bytes 1572872 | tf_op jit(solution)/shard_map/ppermute | solution.py:859
  159.4 27.4 %collective-permute-start.22 = (bf16[256,1024]{1,0:T(8,128)(2,1)S(1)}, bf16[256,1024]{1,0:T(8,128)(2,1)S(1)}, u32[]{:S(2)}, u32[]{:S(2)}) collective-permute-start(bf16[256,1024]{1,0:T(8,128)(2,1)S(1)} %collective-permute-done.18), channel_id=1, source_target_pairs={{0,8},{8,16},{16,24},{24,28},{28,20},{20,12},{12,4},{4,0},{1,9},{9... | collective-permute-start | bytes 1572872 | tf_op jit(solution)/shard_map/ppermute | solution.py:856
  160.5 26.4 %collective-permute-start.23 = (bf16[256,1024]{1,0:T(8,128)(2,1)S(1)}, bf16[256,1024]{1,0:T(8,128)(2,1)S(1)}, u32[]{:S(2)}, u32[]{:S(2)}) collective-permute-start(bf16[256,1024]{1,0:T(8,128)(2,1)S(1)} %collective-permute-done.19), channel_id=1, source_target_pairs={{0,4},{8,0},{16,8},{24,16},{28,24},{20,28},{12,20},{4,12},{1,5},{9... | collective-permute-start | bytes 1572872 | tf_op jit(solution)/shard_map/ppermute | solution.py:859
  161.5 25.3 %collective-permute-start.24 = (bf16[128,2048]{1,0:T(8,128)(2,1)S(1)}, bf16[128,2048]{1,0:T(8,128)(2,1)S(1)}, u32[]{:S(2)}, u32[]{:S(2)}) collective-permute-start(bf16[128,2048]{1,0:T(8,128)(2,1)S(1)} %collective-permute-done.20.refs_8_), channel_id=1, source_target_pairs={{0,8},{8,16},{16,24},{24,28},{28,20},{20,12},{12,4},{4,0},{1,9},{9... | collective-permute-start | bytes 1572872 | tf_op jit(solution)/shard_map/ppermute | solution.py:856
  186.9 25.6 %collective-permute-start.28 = (bf16[128,2048]{1,0:T(8,128)(2,1)S(1)}, bf16[128,2048]{1,0:T(8,128)(2,1)S(1)}, u32[]{:S(2)}, u32[]{:S(2)}) collective-permute-start(bf16[128,2048]{1,0:T(8,128)(2,1)S(1)} %collective-permute-done.24.refs_7_), channel_id=1, source_target_pairs={{0,8},{8,16},{16,24},{24,28},{28,20},{20,12},{12,4},{4,0},{1,9},{9... | collective-permute-start | bytes 1572872 | tf_op jit(solution)/shard_map/ppermute | solution.py:856
  188.0 24.5 %collective-permute-start.29 = (bf16[128,2048]{1,0:T(8,128)(2,1)S(1)}, bf16[128,2048]{1,0:T(8,128)(2,1)S(1)}, u32[]{:S(2)}, u32[]{:S(2)}) collective-permute-start(bf16[128,2048]{1,0:T(8,128)(2,1)S(1)} %collective-permute-done.25.refs_2_), channel_id=1, source_target_pairs={{0,4},{8,0},{16,8},{24,16},{28,24},{20,28},{12,20},{4,12},{1,5},{9... | collective-permute-start | bytes 1572872 | tf_op jit(solution)/shard_map/ppermute | solution.py:859
  313.7 277.8 %reduce-scatter.3.cloned.1.call-start = ((), (), s32[]{:S(2)}) async-start(), calls=%async_computation.4 | async-start | bytes 13107200 | tf_op jit(solution)/shard_map/reduce_scatter | solution.py:1116
  351.1 44.9 %collective-permute-start.36 = (bf16[256,1024]{1,0:T(8,128)(2,1)S(1)}, bf16[256,1024]{1,0:T(8,128)(2,1)S(1)}, u32[]{:S(2)}, u32[]{:S(2)}) collective-permute-start(bf16[256,1024]{1,0:T(8,128)(2,1)S(1)} %pad_maximum_fusion.4), channel_id=1, source_target_pairs={{0,8},{8,16},{16,24},{24,28},{28,20},{20,12},{12,4},{4,0},{1,9},{9... | collective-permute-start | bytes 1572872 | tf_op jit(solution)/shard_map/ppermute | solution.py:856
  351.7 44.2 %collective-permute-start.37 = (bf16[256,1024]{1,0:T(8,128)(2,1)S(1)}, bf16[256,1024]{1,0:T(8,128)(2,1)S(1)}, u32[]{:S(2)}, u32[]{:S(2)}) collective-permute-start(bf16[256,1024]{1,0:T(8,128)(2,1)S(1)} %pad_maximum_fusion.5), channel_id=1, source_target_pairs={{0,4},{8,0},{16,8},{24,16},{28,24},{20,28},{12,20},{4,12},{1,5},{9... | collective-permute-start | bytes 1572872 | tf_op jit(solution)/shard_map/ppermute | solution.py:859
  418.7 36.8 %collective-permute-start.38 = (bf16[1280,2048]{1,0:T(8,128)(2,1)}, bf16[1280,2048]{1,0:T(8,128)(2,1)}, u32[]{:S(2)}, u32[]{:S(2)}) collective-permute-start(bf16[1280,2048]{1,0:T(8,128)(2,1)} %convolution_convert_fusion.1), channel_id=1, source_target_pairs={{0,2},{2,0},{1,3},{3,1},{4,6},{6,4},{5,7},{7,5},{8,10},{10,8},{9,1... | collective-permute-start | bytes 15728648 | tf_op jit(solution)/shard_map/ppermute | solution.py:786
  426.1 24.9 %collective-permute-start.40 = (bf16[256,1024]{1,0:T(8,128)(2,1)}, bf16[256,1024]{1,0:T(8,128)(2,1)S(1)}, u32[]{:S(2)}, u32[]{:S(2)}) collective-permute-start(bf16[256,1024]{1,0:T(8,128)(2,1)} %get-tuple-element.282), channel_id=1, source_target_pairs={{0,4},{8,0},{16,8},{24,16},{28,24},{20,28},{12,20},{4,12},{1,5},{9... | collective-permute-start | bytes 1572872 | tf_op jit(solution)/shard_map/ppermute | solution.py:859
  453.5 36.3 %collective-permute-start.42 = (bf16[256,1024]{1,0:T(8,128)(2,1)S(1)}, bf16[256,1024]{1,0:T(8,128)(2,1)S(1)}, u32[]{:S(2)}, u32[]{:S(2)}) collective-permute-start(bf16[256,1024]{1,0:T(8,128)(2,1)S(1)} %get-tuple-element.280), channel_id=1, source_target_pairs={{0,4},{8,0},{16,8},{24,16},{28,24},{20,28},{12,20},{4,12},{1,5},{9... | collective-permute-start | bytes 1572872 | tf_op jit(solution)/shard_map/ppermute | solution.py:859
  455.5 34.3 %collective-permute-start.41 = (bf16[256,1024]{1,0:T(8,128)(2,1)S(1)}, bf16[256,1024]{1,0:T(8,128)(2,1)S(1)}, u32[]{:S(2)}, u32[]{:S(2)}) collective-permute-start(bf16[256,1024]{1,0:T(8,128)(2,1)S(1)} %get-tuple-element.281), channel_id=1, source_target_pairs={{0,8},{8,16},{16,24},{24,28},{28,20},{20,12},{12,4},{4,0},{1,9},{9... | collective-permute-start | bytes 1572872 | tf_op jit(solution)/shard_map/ppermute | solution.py:856
  502.9 63.5 %collective-permute-start.48 = (bf16[640,2048]{1,0:T(8,128)(2,1)}, bf16[640,2048]{1,0:T(8,128)(2,1)}, u32[]{:S(2)}, u32[]{:S(2)}) collective-permute-start(bf16[640,2048]{1,0:T(8,128)(2,1)} %add_convert_fusion), channel_id=1, source_target_pairs={{0,1},{1,0},{2,3},{3,2},{4,5},{5,4},{6,7},{7,6},{8,9},{9,8},{10,11... | collective-permute-start | bytes 7864328 | tf_op jit(solution)/shard_map/ppermute | solution.py:782
  504.4 30.2 %collective-permute-start.43 = (bf16[128,1024]{1,0:T(8,128)(2,1)S(1)}, bf16[128,1024]{1,0:T(8,128)(2,1)}, u32[]{:S(2)}, u32[]{:S(2)}) collective-permute-start(bf16[128,1024]{1,0:T(8,128)(2,1)S(1)} %get-tuple-element.297), channel_id=1, source_target_pairs={{0,2},{2,0},{1,3},{3,1},{4,6},{6,4},{5,7},{7,5},{8,10},{10,8},{9,1... | collective-permute-start | bytes 786440 | tf_op jit(solution)/shard_map/ppermute | solution.py:786
  548.9 30.5 %collective-permute-start.51 = (bf16[2,64,1024]{2,1,0:T(8,128)(2,1)}, bf16[2,64,1024]{2,1,0:T(8,128)(2,1)}, u32[]{:S(2)}, u32[]{:S(2)}) collective-permute-start(bf16[2,64,1024]{2,1,0:T(8,128)(2,1)} %dynamic-slice_bitcast_fusion.2), channel_id=1, source_target_pairs={{0,1},{1,0},{2,3},{3,2},{4,5},{5,4},{6,7},{7,6},{8,9},{9,8},{10,11... | collective-permute-start | bytes 786440 | tf_op jit(solution)/shard_map/ppermute | solution.py:782
  551.4 28.0 %collective-permute-start.59 = (f32[8,1408]{1,0:T(8,128)S(1)}, f32[8,1408]{1,0:T(8,128)S(1)}, u32[]{:S(2)}, u32[]{:S(2)}) collective-permute-start(f32[8,1408]{1,0:T(8,128)S(1)} %add.368.own_ref), channel_id=1, source_target_pairs={{0,1},{1,0},{2,3},{3,2},{4,5},{5,4},{6,7},{7,6},{8,9},{9,8},{10,11... | collective-permute-start | bytes 135176 | tf_op jit(solution)/shard_map/ppermute | solution.py:782
  (95 other events, 1470.6 us)
Sparse Core Ops, SparseCore 0:
  50.3 70.8 all-gather.2
  130.8 69.4 all-gather.4
  313.8 99.0 reduce-scatter.4
  426.2 88.9 reduce-scatter.2

commit v6 on v5

--- a/solution.py
+++ b/solution.py
@@ -1116,7 +1116,7 @@
     reduced = lambda v, axes: lax.psum_scatter(v, axes, scatter_dimension=0, tiled=True)
     if ringed:
         own_out = reduced(g_out, "ra").astype(F32)
-        g_z = chain.mark(tn(chain.tie(xh), dz))
+        g_z = chain.mark(tn(chain.tie(xh), dz).astype(BF))
         blocks_z = g_z.reshape(AHEADS, -1, WIDTH)
         scatter_z = Scatter(ring, lambda k: blocks_z[k], chain)
         scatter_z.start()
@@ -1144,7 +1144,7 @@
         back_z = Return(chain.mark(scatter_z.total()))
 
         def blocks_x(first, last):
-            part = tn(xh[:, first * feature : last * feature], chain.tie(dx)[:, :XCOLS])
+            part = tn(xh[:, first * feature : last * feature], chain.tie(dx)[:, :XCOLS]).astype(BF)
             return dict(enumerate(chain.mark(part).reshape(last - first, feature, XCOLS), first))
 
         made = blocks_x(4, 5)

time: 620 us -> 617 us (level)
  transfers between devices with their start and end apart: 65 -> 65, of which waited for: 19 -> 19; matrix products, arithmetic and copies ran while one was open for 38% -> 37% of each run, Pallas kernels for 23% -> 23%
where the time goes in v6:
time: 617 us; the launch traced here: 609 us
  Pallas kernels  184 us (30%)
  matrix products  177 us (29%)
  starting transfers between devices  64.1 us (10%)
  waiting for transfers between devices  62.6 us (10%)
  local copies, waits for them, and re-layouts  51.3 us (8%)
  other arithmetic  49.1 us (8%)
  between operations  20.4 us (3%)
    pallas_call x3, Pallas kernels, ssd_backward(): pl.pallas_call(bwd_kernel, grid_spec=pltpu.PrefetchScalarGridSpec(num_sca...  85.8 us
    dot_general x7, matrix products, tn(): lax.dot_general(a, b, (((0,), (0,)), ((), ())), preferred_element_type=F32)  60.8 us
    dot_general x4, matrix products, nt(): lax.dot_general(a, b, (((1,), (1,)), ((), ())), preferred_element_type=F32)  60.6 us
    dot_general x3, matrix products, nn(): lax.dot_general(a, b, (((1,), (0,)), ((), ())), preferred_element_type=F32)  55.7 us
    pallas_call x2, Pallas kernels, ssd_forward(): pl.pallas_call(fwd_kernel, grid_spec=pltpu.PrefetchScalarGridSpec(num_sca...  41.2 us
    ppermute x20, waiting for transfers between devices, left(): return lax.ppermute(v, 'ra', self.pairs(-1))  33.5 us
    ppermute x20, starting transfers between devices, left(): return lax.ppermute(v, 'ra', self.pairs(-1))  27 us
    unnamed x139, local copies, waits for them, and re-layouts  26.5 us
  transfers between devices with their start and end apart: 65, of which 19 were waited for; matrix products, arithmetic and copies ran while one was open for 37% of the time, Pallas kernels for 23%

profile of v6, /device:TPU:0, one launch (start us, length us, event | category | flops | bytes accessed | tf_op | source)
XLA Modules:
  0.0 609.0 jit_solution(17397261321097921578)
XLA Ops:
  15.4 9.0 %collective-permute-done.got_ref = bf16[2,72,1408]{2,1,0:T(8,128)(2,1)S(1)} collective-permute-done((bf16[2,72,1408]{2,1,0:T(8,128)(2,1)}, bf16[2,72,1408]{2,1,0:T(8,128)(2,1)S(1)}, u32[]{:S(2)}, u32[]{:S(2)}) %collective-permute-start) | collective-permute-done | bytes 405536 | tf_op jit(solution)/shard_map/ppermute | solution.py:782
  56.7 10.0 %collective-permute-done.7 = bf16[256,1408]{1,0:T(8,128)(2,1)} collective-permute-done((bf16[256,1408]{1,0:T(8,128)(2,1)S(1)}, bf16[256,1408]{1,0:T(8,128)(2,1)}, u32[]{:S(2)}, u32[]{:S(2)}) %collective-permute-start.7) | collective-permute-done | bytes 720928 | tf_op jit(solution)/shard_map/ppermute | solution.py:859
  92.7 13.3 %collective-permute-done.13 = bf16[256,1408]{1,0:T(8,128)(2,1)} collective-permute-done((bf16[256,1408]{1,0:T(8,128)(2,1)}, bf16[256,1408]{1,0:T(8,128)(2,1)}, u32[]{:S(2)}, u32[]{:S(2)}) %collective-permute-start.13) | collective-permute-done | bytes 720928 | tf_op jit(solution)/shard_map/ppermute | solution.py:859
  136.0 23.4 %fusion.73.p_ref = f32[2560,1408]{1,0:T(8,128)} fusion(bf16[2560,2048]{1,0:T(8,128)(2,1)} %all-gather.3.cloned.1.call-done, bf16[2048,1408]{1,0:T(8,128)(2,1)} %constant_dynamic-update-slice_fusion), kind=kOutput, calls=%fused_computation.183 | convolution fusion | flops 14763950080 | bytes 30670848 | tf_op jit(solution)/shard_map/dot_general | solution.py:43
  166.2 20.6 %ssd_forward.2 = (bf16[2560,1024]{1,0:T(8,128)(2,1)}, bf16[2560,1280]{1,0:T(8,128)(2,1)}, bf16[2560,1280]{1,0:T(8,128)(2,1)}, f32[4,128,1024]{2,1,0:T(8,128)}) custom-call(s32[2]{0:T(128)} %iota.26.steps_ref, f32[2560,1408]{1,0:T(8,128)} %fusion.73.p_ref, f32[8,1280]{1,0:T(8,128)} %concatenate.141.cw_ref, f32[8,1280]{1,0:T(8,128)} %select_maximum_fusion.cb_ref, ...), custom_call_target="tpu_custom_call" | custom-call | flops 8000000000 | bytes 12000000 | tf_op jit(solution)/shard_map/ssd_forward/pallas_call | solution.py:458
  191.1 20.6 %ssd_forward.3 = (bf16[2560,1024]{1,0:T(8,128)(2,1)}, bf16[2560,1280]{1,0:T(8,128)(2,1)}, bf16[2560,1280]{1,0:T(8,128)(2,1)}, f32[4,128,1024]{2,1,0:T(8,128)}) custom-call(s32[2]{0:T(128)} %constant.185.clone.1.steps_ref, f32[2560,1408]{1,0:T(8,128)} %fusion.73.p_ref, ...), custom_call_target="tpu_custom_call", output_to_operand_aliasing={{0}: (8, {}), {1}: (9, {}), {2}: (10, {}), {3}: (11, {})} | custom-call | flops 8000000000 | bytes 12000000 | tf_op jit(solution)/shard_map/ssd_forward/pallas_call | solution.py:458
  219.0 16.5 %convolution_convert_fusion.3.z_ref = bf16[2560,1024]{1,0:T(8,128)(2,1)} fusion(bf16[2560,2048]{1,0:T(8,128)(2,1)} %all-gather.3.cloned.1.call-done, bf16[2048,1024]{1,0:T(8,128)(2,1)} %constant_dynamic-update-slice_fusion.9), kind=kOutput, calls=%fused_computation.19 | convolution fusion | flops 10740039680 | bytes 19922944 | tf_op jit(solution)/shard_map/dot_general | solution.py:43
  241.4 16.5 %convolution_convert_fusion.2.dn_ref = bf16[2560,1024]{1,0:T(8,128)(2,1)} fusion(bf16[2560,2048]{1,0:T(8,128)(2,1)} %all-gather.5.cloned.1.call-done, bf16[1024,2048]{1,0:T(8,128)(2,1)} %ordered_rows.1), kind=kOutput, calls=%fused_computation.18 | convolution fusion | flops 10740039680 | bytes 19922944 | tf_op jit(solution)/shard_map/dot_general | solution.py:39
  258.4 12.2 %gate_stats.1 = f32[8,2560]{1,0:T(8,128)} custom-call(s32[8]{0:T(128)} %iota.24.order_ref, bf16[2560,1024]{1,0:T(8,128)(2,1)} %get-tuple-element.196.y_ref, bf16[2560,1024]{1,0:T(8,128)(2,1)} %convolution_convert_fusion.3.z_ref, bf16[2560,1024]{1,0:T(8,128)(2,1)} %convolution_convert_fusion.2.dn_ref, f32[8,1024]{1,0:T(8,128)} %concatenate.139.gain_ref), custom_call_target="tpu_custom_call" | custom-call | flops 3000000000 | bytes 16000000 | tf_op jit(solution)/shard_map/gate_stats/pallas_call | solution.py:540
  278.7 17.9 %gate_backward.1 = (bf16[2560,1024]{1,0:T(8,128)(2,1)}, bf16[2560,1024]{1,0:T(8,128)(2,1)}, bf16[2560,1024]{1,0:T(8,128)(2,1)}) custom-call(s32[8]{0:T(128)} %iota.23.order_ref, f32[8,2560]{1,0:T(8,128)} %add.318.st_ref, bf16[2560,1024]{1,0:T(8,128)(2,1)} %get-tuple-element.196.y_ref, bf16[2560,1024]{1,0:T(8,128)(2,1)} %convolution_convert_fusion.3.z_ref, ...), custom_call_target="tpu_custom_call" | custom-call | flops 6000000000 | bytes 32000000 | tf_op jit(solution)/shard_map/gate_backward/pallas_call | solution.py:559
  296.6 17.0 %convolution_convert_fusion.4 = bf16[1024,2048]{1,0:T(8,128)(2,1)} fusion(bf16[2560,1024]{1,0:T(8,128)(2,1)} %get-tuple-element.224, bf16[2560,2048]{1,0:T(8,128)(2,1)} %all-gather.5.cloned.1.call-done), kind=kOutput, calls=%fused_computation.33 | convolution fusion | flops 10739515392 | bytes 19922944 | tf_op jit(solution)/shard_map/dot_general | solution.py:47
  313.7 15.6 %convolution_convert_fusion.5 = bf16[2048,1024]{1,0:T(8,128)(2,1)S(1)} fusion(bf16[2560,2048]{1,0:T(8,128)(2,1)} %all-gather.3.cloned.1.call-done, bf16[2560,1024]{1,0:T(8,128)(2,1)} %get-tuple-element.223.dz_ref), kind=kOutput, calls=%fused_computation.34 | convolution fusion | flops 10739515392 | bytes 19922944 | tf_op jit(solution)/shard_map/dot_general | solution.py:47
  333.5 15.8 %convolution_convert_fusion = bf16[2560,2048]{1,0:T(8,128)(2,1)} fusion(bf16[2560,1024]{1,0:T(8,128)(2,1)} %get-tuple-element.224, bf16[1024,2048]{1,0:T(8,128)(2,1)S(1)} %copy-done.10), kind=kOutput, calls=%fused_computation.1 | convolution fusion | flops 10742661120 | bytes 19922944 | tf_op jit(solution)/shard_map/dot_general | solution.py:43
  354.8 40.6 %ssd_backward.3 = (bf16[2560,2432]{1,0:T(8,128)(2,1)}, f32[8,1408]{1,0:T(8,128)}) custom-call(s32[2]{0:T(128)} %pad_add_fusion.1.steps_ref, f32[2560,1408]{1,0:T(8,128)} %fusion.73.p_ref, bf16[2560,1280]{1,0:T(8,128)(2,1)} %get-tuple-element.197.act_ref, bf16[2560,1280]{1,0:T(8,128)(2,1)} %get-tuple-element.198.slope_ref, ...), custom_call_target="tpu_custom_call" | custom-call | flops 20000000000 | bytes 18000000 | tf_op jit(solution)/shard_map/ssd_backward/pallas_call | solution.py:495
  397.8 20.0 %convolution_convert_fusion.1 = bf16[1280,2048]{1,0:T(8,128)(2,1)} fusion(bf16[2560,2432]{1,0:T(8,128)(2,1)} %get-tuple-element.235.refs_0_, s32[]{:T(128)S(6)} %select_n.224, bf16[2048,1024]{1,0:T(8,128)(2,1)} %constant_dynamic-update-slice_fusion.9, bf16[2048,1408]{1,0:T(8,128)(2,1)} %constant_dynamic-update-slice_fusion), kind=kOutput, calls=%fused_computation.3 | convolution fusion | flops 12773228544 | bytes 21430276 | tf_op jit(solution)/shard_map/dot_general | solution.py:39
  427.1 22.9 %ssd_backward.4 = (bf16[2560,2432]{1,0:T(8,128)(2,1)}, f32[8,1408]{1,0:T(8,128)}) custom-call(s32[1]{0:T(128)} %bitcast.11.steps_ref, f32[2560,1408]{1,0:T(8,128)} %fusion.73.p_ref, bf16[2560,1280]{1,0:T(8,128)(2,1)} %get-tuple-element.197.act_ref, bf16[2560,1280]{1,0:T(8,128)(2,1)} %get-tuple-element.198.slope_ref, ...), custom_call_target="tpu_custom_call", output_to_operand_aliasing={{0}: (13, {})} | custom-call | flops 10000000000 | bytes 9000000 | tf_op jit(solution)/shard_map/ssd_backward/pallas_call | solution.py:495
  454.0 12.4 %add_convert_fusion = bf16[640,2048]{1,0:T(8,128)(2,1)} fusion(bf16[1280,2048]{1,0:T(8,128)(2,1)} %collective-permute-done.38, s32[]{:T(128)S(6)} %select_n.226, bf16[2560,2432]{1,0:T(8,128)(2,1)} %get-tuple-element.243.refs_0_, s32[]{:T(128)S(6)} %select_n.225, bf16[2048,1024]{1,0:T(8,128)(2,1)} %constant_dynamic-update-slice_fusion.9, ...), kind=kOutput, calls=%fused_computation.22 | convolution fusion | flops 6399197184 | bytes 18317320 | tf_op jit(solution)/shard_map/dot_general | solution.py:39
  466.4 22.3 %ssd_backward.5 = (bf16[2560,2432]{1,0:T(8,128)(2,1)}, f32[8,1408]{1,0:T(8,128)}) custom-call(s32[1]{0:T(128)} %bitcast.10.steps_ref, f32[2560,1408]{1,0:T(8,128)} %fusion.73.p_ref, bf16[2560,1280]{1,0:T(8,128)(2,1)} %get-tuple-element.197.act_ref, bf16[2560,1280]{1,0:T(8,128)(2,1)} %get-tuple-element.198.slope_ref, ...), custom_call_target="tpu_custom_call", output_to_operand_aliasing={{0}: (13, {})} | custom-call | flops 10000000000 | bytes 9000000 | tf_op jit(solution)/shard_map/ssd_backward/pallas_call | solution.py:495
  490.1 5.8 fusion.33
  511.5 8.3 %fusion.20 = bf16[768,1408]{1,0:T(8,128)(2,1)S(1)} fusion(bf16[2560,2432]{1,0:T(8,128)(2,1)S(1)} %copy-done, bf16[2560,2048]{1,0:T(8,128)(2,1)} %all-gather.3.cloned.1.call-done), kind=kOutput, calls=%fused_computation.35 | convolution fusion | flops 5537562624 | bytes 13303808 | tf_op jit(solution)/shard_map/dot_general | solution.py:47
  519.8 6.9 %fusion.29 = bf16[512,1408]{1,0:T(8,128)(2,1)S(1)} fusion(bf16[2560,2432]{1,0:T(8,128)(2,1)S(1)} %copy-done, bf16[2560,2048]{1,0:T(8,128)(2,1)} %all-gather.3.cloned.1.call-done), kind=kOutput, calls=%fused_computation.40 | convolution fusion | flops 3691708416 | bytes 11272192 | tf_op jit(solution)/shard_map/dot_general | solution.py:47
  533.0 11.6 %convert_add_fusion.2 = f32[640,2048]{1,0:T(8,128)} fusion(bf16[1280,2048]{1,0:T(8,128)(2,1)} %collective-permute-done.38, s32[]{:T(128)S(6)} %select_n.229, bf16[2560,2432]{1,0:T(8,128)(2,1)S(1)} %copy-done, s32[]{:T(128)S(6)} %select_n.228, bf16[2048,1024]{1,0:T(8,128)(2,1)} %constant_dynamic-update-slice_fusion.9, ...), kind=kOutput, calls=%fused_computation.21 | convolution fusion | flops 6397886464 | bytes 20938760 | tf_op jit(solution)/shard_map/dot_general | solution.py:39
  559.3 6.3 %collective-permute-done.48 = bf16[640,2048]{1,0:T(8,128)(2,1)} collective-permute-done((bf16[640,2048]{1,0:T(8,128)(2,1)}, bf16[640,2048]{1,0:T(8,128)(2,1)}, u32[]{:S(2)}, u32[]{:S(2)}) %collective-permute-start.48) | collective-permute-done | bytes 2621472 | tf_op jit(solution)/shard_map/ppermute | solution.py:782
  588.6 6.1 fusion.16
  (402 shorter events, 216.8 us)
Async XLA Ops:
  7.2 123.4 %all-gather.3.cloned.1.call-start = ((), (), s32[]{:S(2)}) async-start(), calls=%async_computation.2 | async-start | bytes 13107200 | tf_op jit(solution)/shard_map/all_gather | solution.py:978
  50.2 191.2 %all-gather.5.cloned.1.call-start = ((), (), s32[]{:S(2)}) async-start(), calls=%async_computation.3 | async-start | bytes 13107200 | tf_op jit(solution)/shard_map/all_gather | solution.py:978
  89.0 28.3 %collective-permute-start.17 = (bf16[256,1024]{1,0:T(8,128)(2,1)}, bf16[256,1024]{1,0:T(8,128)(2,1)}, u32[]{:S(2)}, u32[]{:S(2)}) collective-permute-start(bf16[256,1024]{1,0:T(8,128)(2,1)} %place_rows.3), channel_id=1, source_target_pairs={{0,4},{8,0},{16,8},{24,16},{28,24},{20,28},{12,20},{4,12},{1,5},{9... | collective-permute-start | bytes 1572872 | tf_op jit(solution)/shard_map/ppermute | solution.py:859
  90.0 28.2 %collective-permute-start.16 = (bf16[256,1024]{1,0:T(8,128)(2,1)}, bf16[256,1024]{1,0:T(8,128)(2,1)S(1)}, u32[]{:S(2)}, u32[]{:S(2)}) collective-permute-start(bf16[256,1024]{1,0:T(8,128)(2,1)} %place_rows.3), channel_id=1, source_target_pairs={{0,8},{8,16},{16,24},{24,28},{28,20},{20,12},{12,4},{4,0},{1,9},{9... | collective-permute-start | bytes 1572872 | tf_op jit(solution)/shard_map/ppermute | solution.py:856
  130.6 426.0 %reduce-scatter.5.cloned.1.call-start = ((), (), s32[]{:S(2)}) async-start(), calls=%async_computation.5 | async-start | bytes 4718592 | tf_op jit(solution)/shard_map/reduce_scatter | solution.py:1116
  130.7 28.7 %collective-permute-start.18 = (bf16[256,1024]{1,0:T(8,128)(2,1)S(1)}, bf16[256,1024]{1,0:T(8,128)(2,1)S(1)}, u32[]{:S(2)}, u32[]{:S(2)}) collective-permute-start(bf16[256,1024]{1,0:T(8,128)(2,1)S(1)} %collective-permute-done.16), channel_id=1, source_target_pairs={{0,8},{8,16},{16,24},{24,28},{28,20},{20,12},{12,4},{4,0},{1,9},{9... | collective-permute-start | bytes 1572872 | tf_op jit(solution)/shard_map/ppermute | solution.py:856
  131.8 27.6 %collective-permute-start.19 = (bf16[256,1024]{1,0:T(8,128)(2,1)}, bf16[256,1024]{1,0:T(8,128)(2,1)S(1)}, u32[]{:S(2)}, u32[]{:S(2)}) collective-permute-start(bf16[256,1024]{1,0:T(8,128)(2,1)} %collective-permute-done.17), channel_id=1, source_target_pairs={{0,4},{8,0},{16,8},{24,16},{28,24},{20,28},{12,20},{4,12},{1,5},{9... | collective-permute-start | bytes 1572872 | tf_op jit(solution)/shard_map/ppermute | solution.py:859
  133.9 25.5 %collective-permute-start.21 = (bf16[128,2048]{1,0:T(8,128)(2,1)S(1)}, bf16[128,2048]{1,0:T(8,128)(2,1)S(1)}, u32[]{:S(2)}, u32[]{:S(2)}) collective-permute-start(bf16[128,2048]{1,0:T(8,128)(2,1)S(1)} %copy-done.14), channel_id=1, source_target_pairs={{0,4},{8,0},{16,8},{24,16},{28,24},{20,28},{12,20},{4,12},{1,5},{9... | collective-permute-start | bytes 1572872 | tf_op jit(solution)/shard_map/ppermute | solution.py:859
  159.4 27.5 %collective-permute-start.22 = (bf16[256,1024]{1,0:T(8,128)(2,1)S(1)}, bf16[256,1024]{1,0:T(8,128)(2,1)S(1)}, u32[]{:S(2)}, u32[]{:S(2)}) collective-permute-start(bf16[256,1024]{1,0:T(8,128)(2,1)S(1)} %collective-permute-done.18), channel_id=1, source_target_pairs={{0,8},{8,16},{16,24},{24,28},{28,20},{20,12},{12,4},{4,0},{1,9},{9... | collective-permute-start | bytes 1572872 | tf_op jit(solution)/shard_map/ppermute | solution.py:856
  160.5 26.4 %collective-permute-start.23 = (bf16[256,1024]{1,0:T(8,128)(2,1)S(1)}, bf16[256,1024]{1,0:T(8,128)(2,1)S(1)}, u32[]{:S(2)}, u32[]{:S(2)}) collective-permute-start(bf16[256,1024]{1,0:T(8,128)(2,1)S(1)} %collective-permute-done.19), channel_id=1, source_target_pairs={{0,4},{8,0},{16,8},{24,16},{28,24},{20,28},{12,20},{4,12},{1,5},{9... | collective-permute-start | bytes 1572872 | tf_op jit(solution)/shard_map/ppermute | solution.py:859
  161.5 25.3 %collective-permute-start.24 = (bf16[128,2048]{1,0:T(8,128)(2,1)S(1)}, bf16[128,2048]{1,0:T(8,128)(2,1)S(1)}, u32[]{:S(2)}, u32[]{:S(2)}) collective-permute-start(bf16[128,2048]{1,0:T(8,128)(2,1)S(1)} %collective-permute-done.20.refs_8_), channel_id=1, source_target_pairs={{0,8},{8,16},{16,24},{24,28},{28,20},{20,12},{12,4},{4,0},{1,9},{9... | collective-permute-start | bytes 1572872 | tf_op jit(solution)/shard_map/ppermute | solution.py:856
  186.9 25.6 %collective-permute-start.28 = (bf16[128,2048]{1,0:T(8,128)(2,1)S(1)}, bf16[128,2048]{1,0:T(8,128)(2,1)S(1)}, u32[]{:S(2)}, u32[]{:S(2)}) collective-permute-start(bf16[128,2048]{1,0:T(8,128)(2,1)S(1)} %collective-permute-done.24.refs_7_), channel_id=1, source_target_pairs={{0,8},{8,16},{16,24},{24,28},{28,20},{20,12},{12,4},{4,0},{1,9},{9... | collective-permute-start | bytes 1572872 | tf_op jit(solution)/shard_map/ppermute | solution.py:856
  188.1 24.5 %collective-permute-start.29 = (bf16[128,2048]{1,0:T(8,128)(2,1)S(1)}, bf16[128,2048]{1,0:T(8,128)(2,1)S(1)}, u32[]{:S(2)}, u32[]{:S(2)}) collective-permute-start(bf16[128,2048]{1,0:T(8,128)(2,1)S(1)} %collective-permute-done.25.refs_2_), channel_id=1, source_target_pairs={{0,4},{8,0},{16,8},{24,16},{28,24},{20,28},{12,20},{4,12},{1,5},{9... | collective-permute-start | bytes 1572872 | tf_op jit(solution)/shard_map/ppermute | solution.py:859
  313.7 274.8 %reduce-scatter.3.cloned.1.call-start = ((), (), s32[]{:S(2)}) async-start(), calls=%async_computation.4 | async-start | bytes 13107200 | tf_op jit(solution)/shard_map/reduce_scatter | solution.py:1116
  351.4 44.0 %collective-permute-start.36 = (bf16[256,1024]{1,0:T(8,128)(2,1)S(1)}, bf16[256,1024]{1,0:T(8,128)(2,1)S(1)}, u32[]{:S(2)}, u32[]{:S(2)}) collective-permute-start(bf16[256,1024]{1,0:T(8,128)(2,1)S(1)} %pad_maximum_fusion.4), channel_id=1, source_target_pairs={{0,8},{8,16},{16,24},{24,28},{28,20},{20,12},{12,4},{4,0},{1,9},{9... | collective-permute-start | bytes 1572872 | tf_op jit(solution)/shard_map/ppermute | solution.py:856
  351.9 43.5 %collective-permute-start.37 = (bf16[256,1024]{1,0:T(8,128)(2,1)S(1)}, bf16[256,1024]{1,0:T(8,128)(2,1)S(1)}, u32[]{:S(2)}, u32[]{:S(2)}) collective-permute-start(bf16[256,1024]{1,0:T(8,128)(2,1)S(1)} %pad_maximum_fusion.5), channel_id=1, source_target_pairs={{0,4},{8,0},{16,8},{24,16},{28,24},{20,28},{12,20},{4,12},{1,5},{9... | collective-permute-start | bytes 1572872 | tf_op jit(solution)/shard_map/ppermute | solution.py:859
  417.9 36.1 %collective-permute-start.38 = (bf16[1280,2048]{1,0:T(8,128)(2,1)}, bf16[1280,2048]{1,0:T(8,128)(2,1)}, u32[]{:S(2)}, u32[]{:S(2)}) collective-permute-start(bf16[1280,2048]{1,0:T(8,128)(2,1)} %convolution_convert_fusion.1), channel_id=1, source_target_pairs={{0,2},{2,0},{1,3},{3,1},{4,6},{6,4},{5,7},{7,5},{8,10},{10,8},{9,1... | collective-permute-start | bytes 15728648 | tf_op jit(solution)/shard_map/ppermute | solution.py:786
  425.0 25.0 %collective-permute-start.40 = (bf16[256,1024]{1,0:T(8,128)(2,1)}, bf16[256,1024]{1,0:T(8,128)(2,1)S(1)}, u32[]{:S(2)}, u32[]{:S(2)}) collective-permute-start(bf16[256,1024]{1,0:T(8,128)(2,1)} %get-tuple-element.282), channel_id=1, source_target_pairs={{0,4},{8,0},{16,8},{24,16},{28,24},{20,28},{12,20},{4,12},{1,5},{9... | collective-permute-start | bytes 1572872 | tf_op jit(solution)/shard_map/ppermute | solution.py:859
  451.9 36.8 %collective-permute-start.42 = (bf16[256,1024]{1,0:T(8,128)(2,1)S(1)}, bf16[256,1024]{1,0:T(8,128)(2,1)S(1)}, u32[]{:S(2)}, u32[]{:S(2)}) collective-permute-start(bf16[256,1024]{1,0:T(8,128)(2,1)S(1)} %get-tuple-element.280), channel_id=1, source_target_pairs={{0,4},{8,0},{16,8},{24,16},{28,24},{20,28},{12,20},{4,12},{1,5},{9... | collective-permute-start | bytes 1572872 | tf_op jit(solution)/shard_map/ppermute | solution.py:859
  454.0 34.8 %collective-permute-start.41 = (bf16[256,1024]{1,0:T(8,128)(2,1)S(1)}, bf16[256,1024]{1,0:T(8,128)(2,1)S(1)}, u32[]{:S(2)}, u32[]{:S(2)}) collective-permute-start(bf16[256,1024]{1,0:T(8,128)(2,1)S(1)} %get-tuple-element.281), channel_id=1, source_target_pairs={{0,8},{8,16},{16,24},{24,28},{28,20},{20,12},{12,4},{4,0},{1,9},{9... | collective-permute-start | bytes 1572872 | tf_op jit(solution)/shard_map/ppermute | solution.py:856
  501.7 63.9 %collective-permute-start.48 = (bf16[640,2048]{1,0:T(8,128)(2,1)}, bf16[640,2048]{1,0:T(8,128)(2,1)}, u32[]{:S(2)}, u32[]{:S(2)}) collective-permute-start(bf16[640,2048]{1,0:T(8,128)(2,1)} %add_convert_fusion), channel_id=1, source_target_pairs={{0,1},{1,0},{2,3},{3,2},{4,5},{5,4},{6,7},{7,6},{8,9},{9,8},{10,11... | collective-permute-start | bytes 7864328 | tf_op jit(solution)/shard_map/ppermute | solution.py:782
  503.0 30.0 %collective-permute-start.43 = (bf16[128,1024]{1,0:T(8,128)(2,1)S(1)}, bf16[128,1024]{1,0:T(8,128)(2,1)}, u32[]{:S(2)}, u32[]{:S(2)}) collective-permute-start(bf16[128,1024]{1,0:T(8,128)(2,1)S(1)} %get-tuple-element.297), channel_id=1, source_target_pairs={{0,2},{2,0},{1,3},{3,1},{4,6},{6,4},{5,7},{7,5},{8,10},{10,8},{9,1... | collective-permute-start | bytes 786440 | tf_op jit(solution)/shard_map/ppermute | solution.py:786
  547.5 28.9 %collective-permute-start.51 = (bf16[2,64,1024]{2,1,0:T(8,128)(2,1)}, bf16[2,64,1024]{2,1,0:T(8,128)(2,1)}, u32[]{:S(2)}, u32[]{:S(2)}) collective-permute-start(bf16[2,64,1024]{2,1,0:T(8,128)(2,1)} %dynamic-slice_bitcast_fusion.2), channel_id=1, source_target_pairs={{0,1},{1,0},{2,3},{3,2},{4,5},{5,4},{6,7},{7,6},{8,9},{9,8},{10,11... | collective-permute-start | bytes 786440 | tf_op jit(solution)/shard_map/ppermute | solution.py:782
  549.0 27.4 %collective-permute-start.59 = (f32[8,1408]{1,0:T(8,128)S(1)}, f32[8,1408]{1,0:T(8,128)S(1)}, u32[]{:S(2)}, u32[]{:S(2)}) collective-permute-start(f32[8,1408]{1,0:T(8,128)S(1)} %add.368.own_ref), channel_id=1, source_target_pairs={{0,1},{1,0},{2,3},{3,2},{4,5},{5,4},{6,7},{7,6},{8,9},{9,8},{10,11... | collective-permute-start | bytes 135176 | tf_op jit(solution)/shard_map/ppermute | solution.py:782
  (95 other events, 1463.0 us)
Sparse Core Ops, SparseCore 0:
  50.3 70.8 all-gather.2
  130.7 69.4 all-gather.4
  313.8 98.9 reduce-scatter.4
  425.1 89.6 reduce-scatter.2
